TPU v7x, 512 devices: a whole 4x4x16 slice. The times are simulated.
512 devices in a mesh: row: 32 (over z_hi, x, core), col: 16 (over y, z_lo).
Axes of the slice: x: 4, y: 4, z: 16 (z_hi: 4, z_lo: 4; z = z_hi * 4 + z_lo), core: 2. Of those that a mesh axis runs over, the one named last changes fastest.
Arguments:
- queries: bfloat16 [4096, 2048], P('row', 'col'), may hold values from -48 to 48
- suffix_cache: bfloat16 [4096, 2048], P('row', 'col'), may hold values from -1.875 to 1.875
- suffix_leaf: int32 [32, 128], P('row'), may hold values from 0 to 31, never falling along the last dimension, each value on 1 to 8 neighbouring positions
- leaf_parent: int32 [32, 32], P('row'), may hold values from 0 to 31, as said below
- root_cache: bfloat16 [4096, 2048], P(('row', 'col')), may hold values from -2 to 2
- branch_cache: bfloat16 [32, 8192, 2048], P('row', 'col'), may hold values from -1.875 to 1.875
- branch_length: int32 [32], P('row'), may hold values from 1 to 8192, 196608 in all
- leaf_cache: bfloat16 [1024, 256, 2048], P('row', 'col'), may hold values from -1.875 to 1.875
- leaf_length: int32 [1024], P('row'), may hold values from 1 to 256, 131072 in all
Outputs:
- attention_out: bfloat16 [4096, 2048], P('row', 'col')
Inputs may be any that keep to these rules, and one draw needn't show every extreme that they name: `suffix_leaf`: never falls along a row's tokens; each of the 32 leaves has 1 to 8 tokens. `leaf_parent`: in each row index every branch node is the parent of exactly 1 of its leaves, so at most 8 of that row's tokens lie under one branch node.
All inputs are finite; a program needn't handle non-finite values. No bound on the sum of `branch_length` or of `leaf_length` on one device may be relied on, other than what follows from the above.
Results may differ from a plain program's by a relative error of at most 0.0065.
Values may be sent and summed in bfloat16 or wider, within the bound.
No kernel may reach another device: no remote copies, remote signals or barrier semaphores. Data moves between devices by JAX's collectives and lax.ppermute only.
A program may use at most 64 MiB of HBM per device.

v0:
```python
import math

import jax
import jax.numpy as jnp
from jax import lax
from jax.sharding import PartitionSpec as P

HEADS = 8
KV_HEADS = 4
HEAD_DIM = 256
LEAF_ROW = 32


NEG = -1e30


def attend(queries, keys_values, usable):
    row_count = queries.shape[0]
    key_count = keys_values.shape[0]
    group_size = HEADS // KV_HEADS
    key_width = KV_HEADS * HEAD_DIM
    query_heads = queries.reshape(row_count, KV_HEADS, group_size, HEAD_DIM)
    key_heads = keys_values[:, :key_width].reshape(key_count, KV_HEADS, HEAD_DIM)
    value_heads = keys_values[:, key_width:].reshape(key_count, KV_HEADS, HEAD_DIM)
    scores = jnp.einsum(
        "rgjd,kgd->rgjk", query_heads, key_heads, preferred_element_type=jnp.float32
    ) * (1.0 / math.sqrt(HEAD_DIM))
    if usable is not None:
        key_mask = usable[:, None, None, :]
        scores = jnp.where(key_mask, scores, NEG)
    highest = jnp.max(scores, axis=-1)
    weights = jnp.exp(scores - highest[..., None])
    if usable is not None:
        weights = jnp.where(key_mask, weights, 0.0)
    totals = jnp.sum(weights, axis=-1)
    summed = jnp.einsum(
        "rgjk,kgd->rgjd",
        weights.astype(jnp.bfloat16),
        value_heads,
        preferred_element_type=jnp.float32,
    )
    return (
        highest.reshape(row_count, HEADS),
        totals.reshape(row_count, HEADS),
        summed.reshape(row_count, HEADS * HEAD_DIM),
    )


def merge_state(earlier, others):
    highest = jnp.maximum(earlier[0], others[0])
    keep_first = jnp.exp(earlier[0] - highest)
    keep_second = jnp.exp(others[0] - highest)
    totals = earlier[1] * keep_first + others[1] * keep_second
    summed = earlier[2] * jnp.repeat(keep_first, HEAD_DIM, axis=1) + others[2] * jnp.repeat(
        keep_second, HEAD_DIM, axis=1
    )
    return (highest, totals, summed)


def slice_heads(values, col_index, feature_width):
    per_slice = max(1, feature_width // HEAD_DIM)
    first_head = col_index * feature_width // HEAD_DIM
    chosen = lax.dynamic_slice_in_dim(values, first_head, per_slice, values.ndim - 1)
    return jnp.repeat(chosen, feature_width // per_slice, axis=values.ndim - 1)


def combine_columns(running):
    highest, totals, summed = running
    overall = lax.pmax(highest, "col")
    factors = jnp.exp(highest - overall)
    slice_sum = lax.psum_scatter(
        summed * jnp.repeat(factors, HEAD_DIM, axis=1), "col", scatter_dimension=1, tiled=True
    )
    overall_total = lax.psum(totals * factors, "col")
    return (overall, overall_total, slice_sum)


def on_device(
    queries,
    suffix_cache,
    suffix_leaf,
    leaf_parent,
    root_cache,
    branch_cache,
    branch_length,
    leaf_cache,
    leaf_length,
):
    col_count = lax.axis_size("col")
    row_count = lax.axis_size("row")
    col_index = lax.axis_index("col")
    full_queries, full_suffix = (
        lax.all_gather(queries, "col", axis=1, tiled=True),
        lax.all_gather(suffix_cache, "col", axis=1, tiled=True),
    )
    token_count = full_queries.shape[0]
    query_width = full_queries.shape[1]
    feature_width = queries.shape[1]
    leaf_local = suffix_leaf[0]
    positions = jnp.arange(token_count, dtype=jnp.int32)
    blank_state = (
        jnp.full((token_count, HEADS), NEG, jnp.float32),
        jnp.zeros((token_count, HEADS), jnp.float32),
        jnp.zeros((token_count, query_width), jnp.float32),
    )
    running = merge_state(
        blank_state,
        attend(full_queries, lax.all_gather(root_cache, "row", axis=0, tiled=True), None),
    )
    leaf_width = leaf_cache.shape[1]
    leaf_keys = leaf_cache.reshape(LEAF_ROW * leaf_width, leaf_cache.shape[2])
    key_slot = jnp.arange(LEAF_ROW * leaf_width, dtype=jnp.int32)
    key_leaf = key_slot // leaf_width
    key_place = col_index * leaf_width + key_slot % leaf_width
    leaf_ids = jnp.arange(LEAF_ROW, dtype=jnp.int32)
    key_live = jnp.any(
        (key_leaf[None, :] == leaf_ids[:, None]) & (key_place[None, :] < leaf_length[:, None]),
        axis=0,
    )
    usable = (leaf_local[:, None] == key_leaf[None, :]) & key_live[None, :]
    running = merge_state(running, attend(full_queries, leaf_keys, usable))
    suffix_width = token_count // col_count
    suffix_start = col_index * suffix_width
    suffix_keys = lax.dynamic_slice_in_dim(full_suffix, suffix_start, suffix_width, 0)
    suffix_owner = lax.dynamic_slice_in_dim(leaf_local, suffix_start, suffix_width, 0)
    suffix_place = suffix_start + jnp.arange(suffix_width, dtype=jnp.int32)
    usable = (leaf_local[:, None] == suffix_owner[None, :]) & (
        suffix_place[None, :] <= positions[:, None]
    )
    running = merge_state(running, attend(full_queries, suffix_keys, usable))
    parents = leaf_parent[0]
    token_node = jnp.sum(
        jnp.where(leaf_local[:, None] == leaf_ids[None, :], parents[None, :], 0), axis=1
    )
    node_ids = jnp.arange(row_count, dtype=jnp.int32)
    node_hits = (token_node[:, None] == node_ids[None, :]).astype(jnp.int32)
    rank_in_node = jnp.sum(node_hits * (jnp.cumsum(node_hits, axis=0) - 1), axis=1)
    capacity = token_count // 16 * (LEAF_ROW // row_count)
    slot_index = token_node * capacity + rank_in_node
    slot_token = (
        jnp.full((row_count * capacity,), token_count, jnp.int32).at[slot_index].set(positions)
    )
    padded = jnp.concatenate(
        [full_queries, jnp.zeros((1, query_width), full_queries.dtype)], axis=0
    )
    outgoing = padded[slot_token].reshape(row_count, capacity, query_width)
    branch_keys = branch_cache[0]
    branch_width = branch_keys.shape[0]
    branch_place = col_index * branch_width + jnp.arange(branch_width, dtype=jnp.int32)
    branch_usable = (branch_place < branch_length[0])[None, :]
    arrived = lax.all_to_all(outgoing, "row", split_axis=0, concat_axis=0, tiled=True)
    sources = arrived.shape[0]
    item_count = arrived.shape[1]
    flat_queries = arrived.reshape(sources * item_count, arrived.shape[2])
    highest, totals, summed = attend(flat_queries, branch_keys, branch_usable)
    returned = (
        lax.all_to_all(
            summed.reshape(sources, item_count, query_width),
            "row",
            split_axis=0,
            concat_axis=0,
            tiled=True,
        ),
        lax.all_to_all(
            highest.reshape(sources, item_count, HEADS),
            "row",
            split_axis=0,
            concat_axis=0,
            tiled=True,
        ),
        lax.all_to_all(
            totals.reshape(sources, item_count, HEADS),
            "row",
            split_axis=0,
            concat_axis=0,
            tiled=True,
        ),
    )
    back_sums = returned[0].reshape(row_count * capacity, returned[0].shape[2])[slot_index]
    back_peaks = returned[1].reshape(row_count * capacity, HEADS)[slot_index]
    back_totals = returned[2].reshape(row_count * capacity, HEADS)[slot_index]
    running = merge_state(running, (back_peaks, back_totals, back_sums))
    highest, totals, summed = combine_columns(running)
    output = summed / slice_heads(totals, col_index, feature_width)
    return output.astype(jnp.bfloat16)


def solution(mesh):
    in_specs = (
        P("row", "col"),
        P("row", "col"),
        P("row", None),
        P("row", None),
        P(("row", "col"), None),
        P("row", "col", None),
        P("row"),
        P("row", "col", None),
        P("row"),
    )
    out_specs = P("row", "col")
    return jax.shard_map(
        on_device, mesh=mesh, in_specs=in_specs, out_specs=out_specs, check_vma=False
    )
```

profile of v0, /device:TPU:6, one launch (start us, length us, event | category | flops | bytes accessed | tf_op | source)
XLA Modules:
  0.0 506.3 jit_solution(7073490267769526668)
XLA Ops:
  8.9 48.9 %all_gather.10 = bf16[128,2048]{1,0:T(8,128)(2,1)S(1)} all-gather(bf16[128,128]{1,0:T(8,128)(2,1)} %param.9), channel_id=1, replica_groups=mesh['row'=32,'col'=16] {'col'}, dimensions={1}, use_global_device_ids=true | all-gather | bytes 557056 | tf_op jit(solution)/shard_map/all_gather | solution.py:93
  57.8 2.3 gather_fusion
  60.2 15.5 %all-to-all-start = ((bf16[32,8,2048]{2,1,0:T(8,128)(2,1)}), bf16[32,8,2048]{2,1,0:T(8,128)(2,1)}, u32[]{:S(2)}, u32[]{:S(2)}) async-start(bf16[32,8,2048]{2,1,0:T(8,128)(2,1)} %bitcast.34), calls=%async_computation | async-start | bytes 2097152 | tf_op jit(solution)/shard_map/all_to_all | solution.py:151
  76.3 2.9 copy.183
  79.2 1.5 fusion.73
  80.7 39.2 %all-to-all-done = bf16[32,8,2048]{2,1,0:T(8,128)(2,1)} async-done(((bf16[32,8,2048]{2,1,0:T(8,128)(2,1)}), bf16[32,8,2048]{2,1,0:T(8,128)(2,1)}, u32[]{:S(2)}, u32[]{:S(2)}) %all-to-all-start) | async-done | bytes 1048608 | tf_op jit(solution)/shard_map/all_to_all | solution.py:151
  119.9 1.8 reshape_reshape.12
  121.8 2.8 bitcast_reduce_fusion
  125.4 10.7 %all-to-all-start.1 = ((f32[32,8,8]{1,2,0:T(8,128)}), f32[32,8,8]{1,2,0:T(8,128)S(1)}, u32[]{:S(2)}, u32[]{:S(2)}) async-start(f32[32,8,8]{1,2,0:T(8,128)} %copy.186), calls=%async_computation.1 | async-start | bytes 262144 | tf_op jit(solution)/shard_map/all_to_all | solution.py:164
  136.1 3.4 fusion.2
  140.4 11.3 %all-to-all-done.1 = f32[32,8,8]{1,2,0:T(8,128)S(1)} async-done(((f32[32,8,8]{1,2,0:T(8,128)}), f32[32,8,8]{1,2,0:T(8,128)S(1)}, u32[]{:S(2)}, u32[]{:S(2)}) %all-to-all-start.1) | async-done | bytes 8224 | tf_op jit(solution)/shard_map/all_to_all | solution.py:164
  151.6 4.9 all-to-all-start.3
  156.6 3.3 fusion.13
  159.9 1.6 copy.191
  161.5 2.7 reshape_reshape.14
  164.2 6.6 %all-to-all-done.3 = f32[32,8,8]{1,2,0:T(8,128)S(1)} async-done(((f32[32,8,8]{1,2,0:T(8,128)}), f32[32,8,8]{1,2,0:T(8,128)S(1)}, u32[]{:S(2)}, u32[]{:S(2)}) %all-to-all-start.3) | async-done | bytes 8224 | tf_op jit(solution)/shard_map/all_to_all | solution.py:171
  170.9 8.1 %all-to-all-start.2 = ((f32[32,8,2048]{2,1,0:T(8,128)}), f32[32,8,2048]{2,1,0:T(8,128)S(1)}, u32[]{:S(2)}, u32[]{:S(2)}) async-start(f32[32,8,2048]{2,1,0:T(8,128)} %reshape_reshape.14), calls=%async_computation.2 | async-start | bytes 4194304 | tf_op jit(solution)/shard_map/all_to_all | solution.py:157
  180.2 130.7 %all_gather.11 = bf16[128,2048]{1,0:T(8,128)(2,1)S(1)} all-gather(bf16[128,128]{1,0:T(8,128)(2,1)S(1)} %copy-done.6), channel_id=1, replica_groups=mesh['row'=32,'col'=16] {'col'}, dimensions={1}, use_global_device_ids=true | all-gather | bytes 557056 | tf_op jit(solution)/shard_map/all_gather | solution.py:94
  311.1 1.4 fusion.38
  312.5 2.5 copy.182
  315.0 3.0 fusion.72
  318.0 2.3 copy.173
  320.3 2.3 copy.169
  323.0 1.8 fusion.12
  324.8 1.3 copy-done
  326.1 1.8 convolution_bitcast_fusion
  327.9 1.5 copy.176
  329.5 1.4 copy.178
  330.9 2.1 fusion.16
  333.0 1.3 fusion.74
  336.3 1.6 fusion.77
  337.9 1.4 convolution_bitcast_fusion.1
  339.3 2.5 copy.166
  341.8 2.5 copy.168
  346.4 38.9 %pmax.7 = f32[128,8]{0,1:T(8,128)S(1)} all-reduce(f32[128,8]{0,1:T(8,128)S(1)} %get-tuple-element.13), channel_id=1, replica_groups=mesh['row'=32,'col'=16] {'col'}, use_global_device_ids=true, to_apply=%region_9.10 | all-reduce | flops 1024 | bytes 8192 | tf_op jit(solution)/shard_map/pmax | solution.py:69
  386.2 1.3 copy.233
  387.7 1.3 copy.232
  389.3 1.3 copy.231
  390.8 1.4 copy.230
  392.4 1.3 copy.229
  393.9 1.3 copy.228
  395.4 1.3 copy.227
  397.0 1.4 copy.225
  398.6 1.3 copy.226
  400.9 7.0 %add_multiply_fusion = f32[128,2048]{1,0:T(8,128)} fusion(f32[128,2048]{1,0:T(8,128)} %bitcast.146, f32[128,2048]{1,0:T(8,128)S(1)} %gather_fusion.2, f32[128,2048]{1,0:T(8,128)} %bitcast.147, f32[128,2048]{1,0:T(8,128)} %bitcast.148, f32[128,2048]{1,0:T(8,128)} %copy.182, f32[128,2048]{1,0:T(8,128)} %bitcast.149, f32[128,2048]{1,0:T(8,128)} %bitcast.150, ...), kind=kLoop, calls=%fused_computation.34 | loop fusion | flops 3145728 | bytes 14680064 | tf_op jit(solution)/shard_map/mul | solution.py:72
  407.9 39.3 %psum.7 = f32[128,8]{0,1:T(8,128)S(1)} all-reduce(f32[128,8]{0,1:T(8,128)S(1)} %get-tuple-element.5), channel_id=1, replica_groups=mesh['row'=32,'col'=16] {'col'}, use_global_device_ids=true, to_apply=%region_15.16 | all-reduce | flops 1024 | bytes 8192 | tf_op jit(solution)/shard_map/psum | solution.py:74
  447.3 50.6 %reduce-scatter.2.cloned.1.call-done = f32[128,128]{1,0:T(8,128)} async-done(((f32[128,2048]{1,0:T(8,128)}), f32[128,128]{1,0:T(8,128)}) %reduce-scatter.2.cloned.1.call-update) | async-done | bytes 65552 | tf_op jit(solution)/shard_map/reduce_scatter | solution.py:71
  497.9 1.5 divide_convert_fusion
  (81 shorter events, 13.3 us)
Async XLA Ops:
  60.2 59.8 %all-to-all-start = ((bf16[32,8,2048]{2,1,0:T(8,128)(2,1)}), bf16[32,8,2048]{2,1,0:T(8,128)(2,1)}, u32[]{:S(2)}, u32[]{:S(2)}) async-start(bf16[32,8,2048]{2,1,0:T(8,128)(2,1)} %bitcast.34), calls=%async_computation | async-start | bytes 2097152 | tf_op jit(solution)/shard_map/all_to_all | solution.py:151
  80.7 41.0 %copy-start.5 = (bf16[512,1024]{0,1:T(8,128)(2,1)S(1)}, bf16[512,1024]{0,1:T(8,128)(2,1)}, u32[]{:S(2)}) copy-start(bf16[512,1024]{0,1:T(8,128)(2,1)} %get-tuple-element.18) | copy-start | bytes 3145732
  125.4 26.2 %all-to-all-start.1 = ((f32[32,8,8]{1,2,0:T(8,128)}), f32[32,8,8]{1,2,0:T(8,128)S(1)}, u32[]{:S(2)}, u32[]{:S(2)}) async-start(f32[32,8,8]{1,2,0:T(8,128)} %copy.186), calls=%async_computation.1 | async-start | bytes 262144 | tf_op jit(solution)/shard_map/all_to_all | solution.py:164
  136.1 20.5 %copy-start.4 = (bf16[512,1024]{0,1:T(8,128)(2,1)S(1)}, bf16[512,1024]{0,1:T(8,128)(2,1)}, u32[]{:S(2)}) copy-start(bf16[512,1024]{0,1:T(8,128)(2,1)} %get-tuple-element.17) | copy-start | bytes 3145732
  151.6 19.2 %all-to-all-start.3 = ((f32[32,8,8]{1,2,0:T(8,128)}), f32[32,8,8]{1,2,0:T(8,128)S(1)}, u32[]{:S(2)}, u32[]{:S(2)}) async-start(f32[32,8,8]{1,2,0:T(8,128)} %copy.195), calls=%async_computation.4 | async-start | bytes 262144 | tf_op jit(solution)/shard_map/all_to_all | solution.py:171
  164.2 15.8 %copy-start.7 = (s32[1,128]{1,0:T(1,128)S(1)}, s32[1,128]{1,0:T(1,128)}, u32[]{:S(2)}) copy-start(s32[1,128]{1,0:T(1,128)} %param.11) | copy-start | bytes 1540
  164.2 15.9 %copy-start.6 = (bf16[128,128]{1,0:T(8,128)(2,1)S(1)}, bf16[128,128]{1,0:T(8,128)(2,1)}, u32[]{:S(2)}) copy-start(bf16[128,128]{1,0:T(8,128)(2,1)} %param.10) | copy-start | bytes 98308
  170.9 229.0 %all-to-all-start.2 = ((f32[32,8,2048]{2,1,0:T(8,128)}), f32[32,8,2048]{2,1,0:T(8,128)S(1)}, u32[]{:S(2)}, u32[]{:S(2)}) async-start(f32[32,8,2048]{2,1,0:T(8,128)} %reshape_reshape.14), calls=%async_computation.2 | async-start | bytes 4194304 | tf_op jit(solution)/shard_map/all_to_all | solution.py:157
  179.0 154.0 %all-gather.2.cloned.1.call-start = ((), (), s32[]{:S(2)}) async-start(), calls=%async_computation.5 | async-start | bytes 1081344 | tf_op jit(solution)/shard_map/all_gather | solution.py:108
  179.7 318.2 %reduce-scatter.2.cloned.1.call-start = ((), (), s32[]{:S(2)}) async-start(), calls=%async_computation.6 | async-start | bytes 1114112 | tf_op jit(solution)/shard_map/reduce_scatter | solution.py:71
  180.0 142.9 %copy-start.1 = (bf16[128,2048]{0,1:T(8,128)(2,1)}, bf16[128,2048]{0,1:T(8,128)(2,1)S(1)}, u32[]{:S(2)}) copy-start(bf16[128,2048]{0,1:T(8,128)(2,1)S(1)} %copy.159) | copy-start | bytes 1572868
  318.0 4.6 copy-start.8
  322.6 3.4 copy-start.3
  324.8 1.3 copy-start
  336.3 1.6 copy-start.2
Sparse Core Ops, SparseCore 0:
  183.0 134.5 all-gather.1
  408.0 89.7 reduce-scatter.1
where the time goes:
time: 507 us; the launch traced here: 506 us
  blocking collectives  258 us (51%)
  waiting for transfers between devices  108 us (21%)
  local copies, waits for them, and re-layouts  56 us (11%)
  starting transfers between devices  39.3 us (8%)
  other arithmetic  16 us (3%)
  between operations  14.5 us (3%)
  matrix products  14.2 us (3%)
    all_gather x1, blocking collectives, on_device(): lax.all_gather(suffix_cache, 'col', axis=1, tiled=True)  131 us
    reduce_scatter x1, waiting for transfers between devices, combine_columns(): lax.psum_scatter(summed * jnp.repeat(factors, HEAD_DIM, axis=1), 'col', s...  50.6 us
    all_gather x1, blocking collectives, on_device(): lax.all_gather(queries, 'col', axis=1, tiled=True)  48.9 us
    psum x1, blocking collectives, combine_columns(): overall_total = lax.psum(totals * factors, 'col')  39.3 us
    all_to_all x1, waiting for transfers between devices, on_device(): lax.all_to_all(outgoing, 'row', split_axis=0, concat_axis=0, tiled=True)  39.2 us
    pmax x1, blocking collectives, combine_columns(): overall = lax.pmax(highest, 'col')  38.9 us
    unnamed x30, local copies, waits for them, and re-layouts  18.3 us
    all_to_all x1, starting transfers between devices, on_device(): lax.all_to_all(outgoing, 'row', split_axis=0, concat_axis=0, tiled=True)  15.5 us
  transfers between devices with their start and end apart: 6, of which 4 were waited for; matrix products, arithmetic and copies ran while one was open for 13% of the time, Pallas kernels for 0%

commit v1 on v0

v1 whole, which is shorter than its diff:
```python
import jax
import jax.numpy as jnp
from jax import lax
from jax.experimental import pallas as pl
from jax.experimental.pallas import tpu as pltpu
from jax.sharding import Mesh, PartitionSpec as P

ROW = ("zh", "x", "core")
COL = ("y", "zl")
XC = ("x", "core")
XCZ = ("x", "core", "zl")
BF = jnp.bfloat16
F32 = jnp.float32
NEG = -1e30
FLOOR = -1e29
VMEM_LIMIT = 50 * 1024 * 1024


def iota(shape, dim):
    return lax.broadcasted_iota(jnp.int32, shape, dim)


def whole(shape):
    return pl.BlockSpec(shape, lambda: (0,) * len(shape))


SMEM = pl.BlockSpec(memory_space=pltpu.SMEM)
ANY = pl.BlockSpec(memory_space=pl.ANY)


def params():
    return pltpu.CompilerParams(vmem_limit_bytes=VMEM_LIMIT)


def slot_kernel(parent, leaf_ref, q_ref, root_ref, out_ref, slot_ref):
    leaf = leaf_ref[...]
    across = jnp.broadcast_to(leaf.astype(F32), (128, 128))
    down = across.T
    before = iota((128, 128), 0) < iota((128, 128), 1)
    rank = jnp.sum(jnp.where((across == down) & before, 1.0, 0.0), axis=0, keepdims=True)
    node = jnp.zeros((1, 128), jnp.int32)
    for leaf_id in range(32):
        node = jnp.where(leaf == leaf_id, parent[0, leaf_id], node)
    slot = node * 8 + rank.astype(jnp.int32)
    slot_ref[...] = slot
    pick = jnp.where(iota((256, 128), 0) == slot, 1.0, 0.0).astype(BF)
    routed = jnp.dot(pick, q_ref[...], preferred_element_type=F32).astype(BF)
    root = root_ref[...].astype(F32)
    blocks = jnp.concatenate([root[:, j * 128 : (j + 1) * 128] for j in range(16)], axis=0).astype(BF)
    for z in range(4):
        out_ref[z, 0:64] = routed[z * 64 : (z + 1) * 64]
        out_ref[z, 64:192] = blocks


def route_slots(parent, leaf, queries, root):
    return pl.pallas_call(
        slot_kernel,
        out_shape=(
            jax.ShapeDtypeStruct((4, 192, 128), BF),
            jax.ShapeDtypeStruct((1, 128), jnp.int32),
        ),
        in_specs=[SMEM, whole((1, 128)), whole((128, 128)), whole((8, 2048))],
        out_specs=(whole((4, 192, 128)), whole((1, 128))),
        compiler_params=params(),
        name="route_slots",
    )(parent, leaf, queries, root)


def pack_cache(where, cache, extra):
    rows = 2048 + (128 if extra is not None else 0)

    def kernel(where_ref, *refs):
        cache_ref = refs[0]
        outs = refs[-4:-1]
        sems = refs[-1]
        copies = []
        for s in range(3):
            target = (where_ref[0] + (s + 1)) & 3
            for part in range(4):
                start = (part // 2) * 1024 + (part % 2) * 128
                lane = pl.multiple_of(target * 256 + start, 128)
                copies.append(
                    pltpu.make_async_copy(
                        cache_ref.at[:, pl.ds(lane, 128)],
                        outs[s].at[pl.ds(part * 512, 512), :],
                        sems.at[s, part],
                    )
                )
            if extra is not None:
                copies.append(
                    pltpu.make_async_copy(refs[1], outs[s].at[pl.ds(2048, 128), :], sems.at[s, 4])
                )
        for copy in copies:
            copy.start()
        for copy in copies:
            copy.wait()

    operands = (where, cache) + ((extra,) if extra is not None else ())
    return pl.pallas_call(
        kernel,
        out_shape=tuple(jax.ShapeDtypeStruct((rows, 128), BF) for _ in range(3)),
        in_specs=[SMEM] + [ANY] * (len(operands) - 1),
        out_specs=(ANY, ANY, ANY),
        scratch_shapes=[pltpu.SemaphoreType.DMA((3, 5))],
        compiler_params=params(),
        name="pack_cache",
    )(*operands)


def softmax_parts(scores, values):
    highest = scores[0].max(axis=1, keepdims=True)
    for part in scores[1:]:
        highest = jnp.maximum(highest, part.max(axis=1, keepdims=True))
    highest = jnp.maximum(highest, FLOOR).astype(BF).astype(F32)
    total = 0.0
    summed = 0.0
    for part, value in zip(scores, values):
        weights = jnp.exp(part - highest)
        total = total + jnp.sum(weights, axis=1, keepdims=True)
        summed = summed + jnp.dot(weights.astype(BF), value, preferred_element_type=F32)
    return highest, total, summed


def score(queries, keys):
    return lax.dot_general(
        queries, keys, (((1,), (1,)), ((), ())), preferred_element_type=F32
    ) * (1.0 / 16.0)


def split_total(total):
    upper = total.astype(BF).astype(F32)
    return upper, total - upper


def lane_stats(highest, total, first):
    upper, lower = split_total(total)
    rows = highest.shape[0]
    lane = iota((rows, 128), 1)
    place = jnp.where(lane == first, highest, 0.0)
    place = jnp.where(lane == first + 1, upper, place)
    return jnp.where(lane == first + 2, lower, place)


def piece(ref, kv):
    base = kv * 1024
    return jnp.concatenate([ref[base : base + 512], ref[base + 512 : base + 1024]], axis=1)


def branch_kernel(info, q_ref, kown, vown, p1, p2, p3, out_ref):
    y = info[0]
    zl = info[1]
    length = info[2]
    loaded = q_ref[...].reshape(8, 4, 32, 128)
    blocks = [loaded[:, z].reshape(256, 128) for z in range(4)]
    keys = [kown[...]] + [piece(ref, 0) for ref in (p1, p2, p3)]
    values = [vown[...]] + [piece(ref, 1) for ref in (p1, p2, p3)]
    row16 = iota((256, 128), 0) & 31
    for h in range(2):
        queries = jnp.concatenate([blocks[2 * h], blocks[2 * h + 1]], axis=1)
        scores = []
        for s in range(4):
            source = (y - s) & 3
            place = (source * 4 + zl) * 512 + iota((256, 512), 1)
            scores.append(jnp.where(place < length, score(queries, keys[s]), NEG))
        highest, total, summed = softmax_parts(scores, values)
        first = jnp.where(row16 < 16, 0, 64)
        stats = lane_stats(highest, total, first)
        for xc in range(8):
            low = xc * 32
            packed = (stats[low : low + 16] + stats[low + 16 : low + 32]).astype(BF)
            for half in range(2):
                out_ref[xc * 4 + 2 * h + half, 0:32] = summed[
                    low : low + 32, half * 128 : (half + 1) * 128
                ].astype(BF)
                out_ref[xc * 4 + 2 * h + half, 32:48] = packed


def branch_attend(info, arrived, cache, pieces):
    head = pl.BlockSpec((512, 256), lambda i, info: (0, info[0]))
    head_value = pl.BlockSpec((512, 256), lambda i, info: (0, 4 + info[0]))
    full = lambda shape: pl.BlockSpec(shape, lambda i, info: (0,) * len(shape))
    rows = pieces[0].shape[0]
    return pl.pallas_call(
        branch_kernel,
        out_shape=jax.ShapeDtypeStruct((32, 48, 128), BF),
        grid_spec=pltpu.PrefetchScalarGridSpec(
            num_scalar_prefetch=1,
            grid=(1,),
            in_specs=[full((32, 32, 128)), head, head_value] + [full((rows, 128))] * 3,
            out_specs=full((32, 48, 128)),
        ),
        compiler_params=params(),
        name="branch_attend",
    )(info, arrived, cache, cache, *pieces)


def merge_kernel(in_ref, out_ref):
    loaded = in_ref[...].astype(F32).reshape(8, 4, 48, 128)
    data = [loaded[:, z, 0:32] for z in range(4)]
    stats = [loaded[:, z, 32:48] for z in range(4)]

    def column(stat, j):
        return jnp.concatenate([stat[:, :, j : j + 1], stat[:, :, 64 + j : 65 + j]], axis=1)

    peaks = [column(stat, 0) for stat in stats]
    highest = jnp.maximum(jnp.maximum(peaks[0], peaks[1]), jnp.maximum(peaks[2], peaks[3]))
    total = 0.0
    summed = 0.0
    for z in range(4):
        factor = jnp.exp(peaks[z] - highest)
        total = total + factor * (column(stats[z], 1) + column(stats[z], 2))
        summed = summed + factor * data[z]
    highest = highest.reshape(8, 4, 8, 1)
    total = total.reshape(8, 4, 8, 1)
    summed = summed.reshape(8, 4, 8, 128)
    first = (iota((64, 128), 0) >> 4) * 32
    for z in range(4):
        out_ref[z, 0:64] = summed[:, z].reshape(64, 128).astype(BF)
        placed = lane_stats(highest[:, z].reshape(64, 1), total[:, z].reshape(64, 1), first)
        out_ref[z, 64:80] = (
            placed[0:16] + placed[16:32] + placed[32:48] + placed[48:64]
        ).astype(BF)


def merge_node(partials):
    return pl.pallas_call(
        merge_kernel,
        out_shape=jax.ShapeDtypeStruct((4, 80, 128), BF),
        in_specs=[whole((32, 48, 128))],
        out_specs=whole((4, 80, 128)),
        compiler_params=params(),
        name="merge_node",
    )(partials)


def local_kernel(
    info, leaf_ref, lengths_ref, kown, vown, p1, p2, p3, root_ref, l0, l1, l2, l3,
    out0, out1, out2, out3, gathered, outgoing,
):
    y = info[0]
    zl = info[1]
    for s, ref in enumerate((l0, l1, l2, l3)):
        gathered[(zl - s) & 3] = ref[...]
    leaf_row = jnp.broadcast_to(leaf_ref[...].astype(F32), (128, 128))
    leaf_col = leaf_row.T
    first_half = (y & 1) * 2
    suffix_k = jnp.concatenate(
        [gathered[first_half, 128:256], gathered[first_half + 1, 128:256]], axis=1
    )
    suffix_v = jnp.concatenate(
        [gathered[first_half, 256:384], gathered[first_half + 1, 256:384]], axis=1
    )
    root = root_ref[...].reshape(8, 4, 4, 32, 128)
    root_parts = [root[:, :, j].reshape(1024, 128) for j in range(4)]
    root_k = jnp.concatenate(root_parts[0:2], axis=1)
    root_v = jnp.concatenate(root_parts[2:4], axis=1)
    leaf_keys = [kown[...]] + [piece(ref, 0) for ref in (p1, p2, p3)]
    leaf_values = [vown[...]] + [piece(ref, 1) for ref in (p1, p2, p3)]
    token = iota((128, 128), 0)
    key_token = iota((128, 128), 1)
    suffix_ok = (leaf_row == leaf_col) & (key_token <= token) & ((key_token & 3) == zl)
    key_slot = iota((1, 512), 1)
    first = (iota((128, 128), 0) >> 4) * 16
    for h in range(2):
        queries = jnp.concatenate([gathered[2 * h, 0:128], gathered[2 * h + 1, 0:128]], axis=1)
        scores = [score(queries, root_k)]
        for s in range(4):
            source = (y - s) & 3
            place = (source * 4 + zl) * 16 + (key_slot & 15)
            key_leaf = jnp.where(place < lengths_ref[...], key_slot >> 4, -1).astype(F32)
            scores.append(
                jnp.where(leaf_col[:, 0:1] == key_leaf, score(queries, leaf_keys[s]), NEG)
            )
        scores.append(jnp.where(suffix_ok, score(queries, suffix_k), NEG))
        highest, total, summed = softmax_parts(scores, [root_v] + leaf_values + [suffix_v])
        stats = lane_stats(highest, total, first)
        packed = stats[0:16]
        for g in range(1, 8):
            packed = packed + stats[g * 16 : (g + 1) * 16]
        for half in range(2):
            outgoing[2 * h + half, 0:128] = summed[:, half * 128 : (half + 1) * 128].astype(BF)
            outgoing[2 * h + half, 128:144] = packed.astype(BF)
    for s, ref in enumerate((out0, out1, out2, out3)):
        ref[...] = outgoing[(zl + s) & 3]


def local_attend(info, leaf, lengths, cache, pieces, root, gathered):
    head = pl.BlockSpec((512, 256), lambda i, info: (0, info[0]))
    head_value = pl.BlockSpec((512, 256), lambda i, info: (0, 4 + info[0]))
    full = lambda shape: pl.BlockSpec(shape, lambda i, info: (0,) * len(shape))
    return pl.pallas_call(
        local_kernel,
        out_shape=tuple(jax.ShapeDtypeStruct((144, 128), BF) for _ in range(4)),
        grid_spec=pltpu.PrefetchScalarGridSpec(
            num_scalar_prefetch=1,
            grid=(1,),
            in_specs=[full((1, 128)), full((1, 512)), head, head_value]
            + [full((2048, 128))] * 3
            + [full((8, 512, 128))]
            + [full((384, 128))] * 4,
            out_specs=tuple(full((144, 128)) for _ in range(4)),
            scratch_shapes=[pltpu.VMEM((4, 384, 128), BF), pltpu.VMEM((4, 144, 128), BF)],
        ),
        compiler_params=params(),
        name="local_attend",
    )(info, leaf, lengths, cache, cache, *pieces, root, *gathered)


def final_kernel(slot_ref, branch_ref, l0, l1, l2, l3, out_ref):
    pick = jnp.where(iota((256, 128), 0) == slot_ref[...], 1.0, 0.0).astype(BF)

    def to_tokens(values):
        return lax.dot_general(
            pick, values, (((0,), (0,)), ((), ())), preferred_element_type=F32
        )

    branch = branch_ref[...]
    branch_sum = to_tokens(branch[:, 0:64].reshape(256, 128))
    lane16 = iota((16, 128), 1) >> 5
    spread = []
    for z in range(4):
        stat = branch[z, 64:80].astype(F32)
        for g in range(4):
            spread.append(jnp.where(lane16 == g, stat, 0.0))
    branch_stat = to_tokens(jnp.concatenate(spread, axis=0).astype(BF))
    lane = iota((128, 128), 1)

    def lane_pick(values, hit):
        return jnp.sum(jnp.where(hit, values, 0.0), axis=1, keepdims=True)

    column = lane & 31
    peaks = [lane_pick(branch_stat, column == 0)]
    totals = [lane_pick(branch_stat, (column == 1) | (column == 2))]
    sums = [branch_sum]
    first = (iota((128, 128), 0) >> 4) * 16
    for ref in (l0, l1, l2, l3):
        sums.append(ref[0:128].astype(F32))
        stat = ref[128:144].astype(F32)
        stat = jnp.concatenate([stat] * 8, axis=0)
        peaks.append(lane_pick(stat, lane == first))
        totals.append(lane_pick(stat, (lane == first + 1) | (lane == first + 2)))
    highest = peaks[0]
    for peak in peaks[1:]:
        highest = jnp.maximum(highest, peak)
    total = 0.0
    summed = 0.0
    for peak, part, value in zip(peaks, totals, sums):
        factor = jnp.exp(peak - highest)
        total = total + factor * part
        summed = summed + factor * value
    out_ref[...] = (summed / total).astype(BF)


def finish(slot, branch, parts):
    return pl.pallas_call(
        final_kernel,
        out_shape=jax.ShapeDtypeStruct((128, 128), BF),
        in_specs=[whole((1, 128)), whole((4, 80, 128))] + [whole((144, 128))] * 4,
        out_specs=whole((128, 128)),
        compiler_params=params(),
        name="finish",
    )(slot, branch, *parts)


def shift(values, axis, step):
    return lax.ppermute(values, axis, [(i, (i + step) % 4) for i in range(4)])


def exchange(values, axis):
    return lax.all_to_all(values, axis, split_axis=0, concat_axis=0, tiled=True)


def on_device(
    queries, suffix_cache, suffix_leaf, leaf_parent, root_cache,
    branch_cache, branch_length, leaf_cache, leaf_length,
):
    y = lax.axis_index("y")
    zl = lax.axis_index("zl")
    info = jnp.stack([y, zl, branch_length[0]]).astype(jnp.int32)
    branch_rows = branch_cache.reshape(512, 2048)
    leaf_rows = leaf_cache.reshape(512, 2048)

    routed, slot = route_slots(leaf_parent, suffix_leaf, queries, root_cache)
    arrived = exchange(routed, "zh")

    branch_out = pack_cache(info, branch_rows, suffix_cache)
    branch_in = [shift(branch_out[s], "y", s + 1) for s in range(3)]
    leaf_out = pack_cache(info, leaf_rows, None)
    leaf_in = [shift(leaf_out[s], "y", s + 1) for s in range(3)]

    onward = arrived[:, 0:64].reshape(4, 8, 8, 128).transpose(1, 0, 2, 3).reshape(8, 1, 32, 128)
    onward = jnp.broadcast_to(onward, (8, 4, 32, 128)).reshape(32, 32, 128)
    node_queries = exchange(onward, XCZ)

    root = arrived[:, 64:192].reshape(4, 2, 4, 2, 8, 128).transpose(2, 1, 3, 0, 4, 5)
    root = root.reshape(4, 4 * 32, 128)
    root_parts = [lax.dynamic_index_in_dim(root, y, 0, keepdims=False)]
    for s in range(3):
        part = lax.dynamic_index_in_dim(root, (y + (s + 1)) & 3, 0, keepdims=False)
        root_parts.append(shift(part, "y", s + 1))
    root_all = lax.all_gather(jnp.concatenate(root_parts, axis=0), XC, axis=0, tiled=False)

    partials = branch_attend(info, node_queries, branch_rows, branch_in)

    blocks = [suffix_cache] + [part[2048:2176] for part in branch_in]

    def chosen(source):
        step = (y - source) & 3
        return lax.select_n(step, *blocks)

    mine = jnp.concatenate([queries, chosen(y // 2), chosen(2 + y // 2)], axis=0)
    gathered = [mine] + [shift(mine, "zl", s + 1) for s in range(3)]

    returned = exchange(partials, XCZ)
    merged = merge_node(returned)
    back = exchange(merged, "zh")

    lengths = jnp.repeat(leaf_length, 16).reshape(1, 512)
    local = local_attend(info, suffix_leaf, lengths, leaf_rows, leaf_in, root_all, gathered)
    parts = [local[0]] + [shift(local[s + 1], "zl", s + 1) for s in range(3)]
    return finish(slot, back, parts)


def solution(mesh):
    fine = Mesh(mesh.devices.reshape(4, 4, 2, 4, 4), ("zh", "x", "core", "y", "zl"))
    in_specs = (
        P(ROW, COL),
        P(ROW, COL),
        P(ROW, None),
        P(ROW, None),
        P(ROW + COL, None),
        P(ROW, COL, None),
        P(ROW),
        P(ROW, COL, None),
        P(ROW),
    )
    return jax.shard_map(
        on_device, mesh=fine, in_specs=in_specs, out_specs=P(ROW, COL), check_vma=False
    )
```

time: 507 us -> 176 us (0.35)
  blocking collectives: 258 us -> 31.8 us
  waiting for transfers between devices: 108 us -> 29 us
  local copies, waits for them, and re-layouts: 56 us -> 7.4 us
  starting transfers between devices: 39.3 us -> 75 us
  Pallas kernels: 0 us -> 16 us
  other arithmetic: 16 us -> 1.53 us
  matrix products: 14.2 us -> 0 us
    all_gather x2 -> x0, blocking collectives: 180 us -> none  [the longest x1 131 us: on_device(): lax.all_gather(suffix_cache, 'col', axis=1, tiled=True)]
    all_to_all x4 -> x3, waiting for transfers between devices: 57.1 us -> 0.01 us  [exchange(): return lax.all_to_all(values, axis, split_axis=0, concat_axis=0, tiled=True)]
    ppermute x0 -> x15, starting transfers between devices: none -> 56.1 us  [shift(): return lax.ppermute(values, axis, [(i, (i + step) % 4) for i in range(4)])]
    reduce_scatter x1 -> x0, waiting for transfers between devices: 50.6 us -> none  [combine_columns(): lax.psum_scatter(summed * jnp.repeat(factors, HEAD_DIM, axis=1), 'col', s...]
    psum x1 -> x0, blocking collectives: 39.3 us -> none  [combine_columns(): overall_total = lax.psum(totals * factors, 'col')]
    pmax x1 -> x0, blocking collectives: 38.9 us -> none  [combine_columns(): overall = lax.pmax(highest, 'col')]
    all_to_all x0 -> x1, blocking collectives: none -> 31.8 us  [exchange(): return lax.all_to_all(values, axis, split_axis=0, concat_axis=0, tiled=True)]
    ppermute x0 -> x15, waiting for transfers between devices: none -> 28.9 us  [shift(): return lax.ppermute(values, axis, [(i, (i + step) % 4) for i in range(4)])]
  transfers between devices with their start and end apart: 6 -> 19, of which waited for: 4 -> 5; matrix products, arithmetic and copies ran while one was open for 13% -> 1% of each run, Pallas kernels for 0% -> 8%
where the time goes in v1:
time: 176 us; the launch traced here: 175 us
  starting transfers between devices  75 us (43%)
  blocking collectives  31.8 us (18%)
  waiting for transfers between devices  29 us (16%)
  Pallas kernels  16 us (9%)
  between operations  14.4 us (8%)
  local copies, waits for them, and re-layouts  7.4 us (4%)
    ppermute x15, starting transfers between devices, shift(): return lax.ppermute(values, axis, [(i, (i + step) % 4) for i in range(4)])  56.1 us
    all_to_all x1, blocking collectives, exchange(): return lax.all_to_all(values, axis, split_axis=0, concat_axis=0, tiled=True)  31.8 us
    ppermute x15, waiting for transfers between devices, shift(): return lax.ppermute(values, axis, [(i, (i + step) % 4) for i in range(4)])  28.9 us
    all_to_all x3, starting transfers between devices, exchange(): return lax.all_to_all(values, axis, split_axis=0, concat_axis=0, tiled=True)  18.9 us
    unnamed x24, local copies, waits for them, and re-layouts  6.42 us
    pallas_call x1, Pallas kernels, branch_attend(): pl.pallas_call(branch_kernel, out_shape=jax.ShapeDtypeStruct((32, 48, 128...  4.97 us
    pallas_call x1, Pallas kernels, local_attend(): pl.pallas_call(local_kernel, out_shape=tuple((jax.ShapeDtypeStruct((144,...  4.16 us
    pallas_call x2, Pallas kernels, pack_cache(): pl.pallas_call(kernel, out_shape=tuple((jax.ShapeDtypeStruct((rows, 128),...  3.7 us
  transfers between devices with their start and end apart: 19, of which 5 were waited for; matrix products, arithmetic and copies ran while one was open for 1% of the time, Pallas kernels for 8%

profile of v1, /device:TPU:6, one launch (start us, length us, event | category | flops | bytes accessed | tf_op | source)
XLA Modules:
  0.0 175.1 jit_solution(2094267517662644479)
XLA Ops:
  6.5 0.8 copy-done.5
  7.3 0.8 copy-done.7
  8.1 0.7 copy-done.8
  8.7 0.7 copy-done.10
  9.4 0.8 route_slots.1
  10.2 31.8 %all_to_all.20 = bf16[4,192,128]{2,1,0:T(8,128)(2,1)S(1)} all-to-all(bf16[4,192,128]{2,1,0:T(8,128)(2,1)S(1)} %get-tuple-element.18), channel_id=1, replica_groups=mesh['zh'=4,'x'=4,'core'=2,'y'=4,'zl'=4] {'zh'}, dimensions={0} | all-to-all | bytes 393216 | tf_op jit(solution)/shard_map/all_to_all | solution.py:370
  42.0 0.8 broadcast_in_dim.11
  42.8 7.8 %all-to-all-start.1 = ((bf16[32,32,128]{2,1,0:T(8,128)(2,1)}), bf16[32,32,128]{2,1,0:T(8,128)(2,1)S(1)}, u32[]{:S(2)}, u32[]{:S(2)}) async-start(bf16[32,32,128]{2,1,0:T(8,128)(2,1)} %bitcast.5), calls=%async_computation.1 | async-start | bytes 524288 | tf_op jit(solution)/shard_map/all_to_all | solution.py:370
  50.5 0.0 all-gather.3.cloned.1.call-start
  51.2 0.1 pad_add_fusion.where_ref.info
  51.3 1.6 copy-done
  52.9 0.8 copy-done.3
  53.6 1.9 %pack_cache.2 = (bf16[2176,128]{1,0:T(8,128)(2,1)}, bf16[2176,128]{1,0:T(8,128)(2,1)}, bf16[2176,128]{1,0:T(8,128)(2,1)}) custom-call(s32[3]{0:T(128)S(1)} %pad_add_fusion.where_ref.info, bf16[512,2048]{1,0:T(8,128)(2,1)S(1)} %bitcast.27, bf16[128,128]{1,0:T(8,128)(2,1)S(1)} %copy-done.3), custom_call_target="tpu_custom_call" | custom-call | tf_op jit(solution)/shard_map/pack_cache/pallas_call | solution.py:99
  55.5 3.5 %collective-permute-start = (bf16[2176,128]{1,0:T(8,128)(2,1)}, bf16[2176,128]{1,0:T(8,128)(2,1)S(1)}, u32[]{:S(2)}, u32[]{:S(2)}) collective-permute-start(bf16[2176,128]{1,0:T(8,128)(2,1)} %get-tuple-element.19), channel_id=1, source_target_pairs={{0,4},{4,8},{8,12},{12,0},{1,5},{5,9},{9,13},{13,1},{2,6},{6,10},{... | collective-permute-start | bytes 1671176 | tf_op jit(solution)/shard_map/ppermute | solution.py:366
  59.0 4.8 %collective-permute-start.1 = (bf16[2176,128]{1,0:T(8,128)(2,1)}, bf16[2176,128]{1,0:T(8,128)(2,1)}, u32[]{:S(2)}, u32[]{:S(2)}) collective-permute-start(bf16[2176,128]{1,0:T(8,128)(2,1)} %get-tuple-element.20), channel_id=1, source_target_pairs={{0,8},{4,12},{8,0},{12,4},{1,9},{5,13},{9,1},{13,5},{2,10},{6,14},... | collective-permute-start | bytes 1671176 | tf_op jit(solution)/shard_map/ppermute | solution.py:366
  63.8 3.3 %collective-permute-start.2 = (bf16[2176,128]{1,0:T(8,128)(2,1)}, bf16[2176,128]{1,0:T(8,128)(2,1)}, u32[]{:S(2)}, u32[]{:S(2)}) collective-permute-start(bf16[2176,128]{1,0:T(8,128)(2,1)} %get-tuple-element.21), channel_id=1, source_target_pairs={{0,12},{4,0},{8,4},{12,8},{1,13},{5,1},{9,5},{13,9},{2,14},{6,2},{... | collective-permute-start | bytes 1671176 | tf_op jit(solution)/shard_map/ppermute | solution.py:366
  67.2 1.9 %collective-permute-start.8 = (bf16[128,128]{1,0:T(8,128)(2,1)S(1)}, bf16[128,128]{1,0:T(8,128)(2,1)S(1)}, u32[]{:S(2)}, u32[]{:S(2)}) collective-permute-start(bf16[128,128]{1,0:T(8,128)(2,1)S(1)} %get-tuple-element.32), channel_id=1, source_target_pairs={{0,12},{4,0},{8,4},{12,8},{1,13},{5,1},{9,5},{13,9},{2,14},{6,2},{... | collective-permute-start | bytes 98312 | tf_op jit(solution)/shard_map/ppermute | solution.py:366
  69.1 4.6 %collective-permute-start.7 = (bf16[128,128]{1,0:T(8,128)(2,1)S(1)}, bf16[128,128]{1,0:T(8,128)(2,1)S(1)}, u32[]{:S(2)}, u32[]{:S(2)}) collective-permute-start(bf16[128,128]{1,0:T(8,128)(2,1)S(1)} %get-tuple-element.33), channel_id=1, source_target_pairs={{0,8},{4,12},{8,0},{12,4},{1,9},{5,13},{9,1},{13,5},{2,10},{6,14},... | collective-permute-start | bytes 98312 | tf_op jit(solution)/shard_map/ppermute | solution.py:366
  73.8 15.4 %collective-permute-done.8 = bf16[128,128]{1,0:T(8,128)(2,1)S(1)} collective-permute-done((bf16[128,128]{1,0:T(8,128)(2,1)S(1)}, bf16[128,128]{1,0:T(8,128)(2,1)S(1)}, u32[]{:S(2)}, u32[]{:S(2)}) %collective-permute-start.8) | collective-permute-done | bytes 32800 | tf_op jit(solution)/shard_map/ppermute | solution.py:366
  89.1 4.4 %collective-permute-start.6 = (bf16[128,128]{1,0:T(8,128)(2,1)S(1)}, bf16[128,128]{1,0:T(8,128)(2,1)S(1)}, u32[]{:S(2)}, u32[]{:S(2)}) collective-permute-start(bf16[128,128]{1,0:T(8,128)(2,1)S(1)} %get-tuple-element.34), channel_id=1, source_target_pairs={{0,4},{4,8},{8,12},{12,0},{1,5},{5,9},{9,13},{13,1},{2,6},{6,10},{... | collective-permute-start | bytes 98312 | tf_op jit(solution)/shard_map/ppermute | solution.py:366
  93.5 2.6 %collective-permute-done.6 = bf16[128,128]{1,0:T(8,128)(2,1)S(1)} collective-permute-done((bf16[128,128]{1,0:T(8,128)(2,1)S(1)}, bf16[128,128]{1,0:T(8,128)(2,1)S(1)}, u32[]{:S(2)}, u32[]{:S(2)}) %collective-permute-start.6) | collective-permute-done | bytes 32800 | tf_op jit(solution)/shard_map/ppermute | solution.py:366
  96.1 0.7 pad_maximum_fusion
  96.8 0.0 all-gather.3.cloned.1.call-update
  96.8 0.0 copy-start.1
  96.9 5.0 %branch_attend.1 = bf16[32,48,128]{2,1,0:T(8,128)(2,1)} custom-call(s32[3]{0:T(128)S(1)} %pad_add_fusion.where_ref.info, bf16[32,32,128]{2,1,0:T(8,128)(2,1)S(1)} %all-to-all-done.1.q_ref, bf16[512,2048]{1,0:T(8,128)(2,1)} %bitcast.25, bf16[512,2048]{1,0:T(8,128)(2,1)} %bitcast.26, bf16[2176,128]{1,0:T(8,128)(2,1)S(1)} %collective-permute-done.p1, ...), custom_call_target="tpu_custom_call" | custom-call | tf_op jit(solution)/shard_map/branch_attend/pallas_call | solution.py:183
  101.9 7.8 %all-to-all-start.2 = ((bf16[32,48,128]{2,1,0:T(8,128)(2,1)}), bf16[32,48,128]{2,1,0:T(8,128)(2,1)S(1)}, u32[]{:S(2)}, u32[]{:S(2)}) async-start(bf16[32,48,128]{2,1,0:T(8,128)(2,1)} %branch_attend.1), calls=%async_computation.2 | async-start | bytes 786432 | tf_op jit(solution)/shard_map/all_to_all | solution.py:370
  109.7 1.8 %pack_cache.3 = (bf16[2048,128]{1,0:T(8,128)(2,1)}, bf16[2048,128]{1,0:T(8,128)(2,1)}, bf16[2048,128]{1,0:T(8,128)(2,1)}) custom-call(s32[3]{0:T(128)S(1)} %pad_add_fusion.where_ref.info, bf16[512,2048]{1,0:T(8,128)(2,1)S(1)} %bitcast.30), custom_call_target="tpu_custom_call" | custom-call | tf_op jit(solution)/shard_map/pack_cache/pallas_call | solution.py:99
  111.5 3.2 %collective-permute-start.3 = (bf16[2048,128]{1,0:T(8,128)(2,1)}, bf16[2048,128]{1,0:T(8,128)(2,1)S(1)}, u32[]{:S(2)}, u32[]{:S(2)}) collective-permute-start(bf16[2048,128]{1,0:T(8,128)(2,1)} %get-tuple-element.22), channel_id=1, source_target_pairs={{0,4},{4,8},{8,12},{12,0},{1,5},{5,9},{9,13},{13,1},{2,6},{6,10},{... | collective-permute-start | bytes 1572872 | tf_op jit(solution)/shard_map/ppermute | solution.py:366
  114.7 3.5 %collective-permute-start.4 = (bf16[2048,128]{1,0:T(8,128)(2,1)}, bf16[2048,128]{1,0:T(8,128)(2,1)S(1)}, u32[]{:S(2)}, u32[]{:S(2)}) collective-permute-start(bf16[2048,128]{1,0:T(8,128)(2,1)} %get-tuple-element.23), channel_id=1, source_target_pairs={{0,8},{4,12},{8,0},{12,4},{1,9},{5,13},{9,1},{13,5},{2,10},{6,14},... | collective-permute-start | bytes 1572872 | tf_op jit(solution)/shard_map/ppermute | solution.py:366
  118.2 3.6 %collective-permute-start.5 = (bf16[2048,128]{1,0:T(8,128)(2,1)}, bf16[2048,128]{1,0:T(8,128)(2,1)S(1)}, u32[]{:S(2)}, u32[]{:S(2)}) collective-permute-start(bf16[2048,128]{1,0:T(8,128)(2,1)} %get-tuple-element.24), channel_id=1, source_target_pairs={{0,12},{4,0},{8,4},{12,8},{1,13},{5,1},{9,5},{13,9},{2,14},{6,2},{... | collective-permute-start | bytes 1572872 | tf_op jit(solution)/shard_map/ppermute | solution.py:366
  121.8 0.8 select_select_fusion.1
  122.7 1.4 merge_node.1
  124.0 3.3 %all-to-all-start.3 = ((bf16[4,80,128]{2,1,0:T(8,128)(2,1)}), bf16[4,80,128]{2,1,0:T(8,128)(2,1)S(1)}, u32[]{:S(2)}, u32[]{:S(2)}) async-start(bf16[4,80,128]{2,1,0:T(8,128)(2,1)} %merge_node.1), calls=%async_computation.3 | async-start | bytes 163840 | tf_op jit(solution)/shard_map/all_to_all | solution.py:370
  127.4 3.4 %collective-permute-start.9 = (bf16[384,128]{1,0:T(8,128)(2,1)S(1)}, bf16[384,128]{1,0:T(8,128)(2,1)S(1)}, u32[]{:S(2)}, u32[]{:S(2)}) collective-permute-start(bf16[384,128]{1,0:T(8,128)(2,1)S(1)} %pad_maximum_fusion.1.l0), channel_id=1, source_target_pairs={{0,1},{1,2},{2,3},{3,0},{4,5},{5,6},{6,7},{7,4},{8,9},{9,10},{10,1... | collective-permute-start | bytes 294920 | tf_op jit(solution)/shard_map/ppermute | solution.py:366
  130.7 4.3 %collective-permute-start.10 = (bf16[384,128]{1,0:T(8,128)(2,1)S(1)}, bf16[384,128]{1,0:T(8,128)(2,1)S(1)}, u32[]{:S(2)}, u32[]{:S(2)}) collective-permute-start(bf16[384,128]{1,0:T(8,128)(2,1)S(1)} %pad_maximum_fusion.1.l0), channel_id=1, source_target_pairs={{0,2},{1,3},{2,0},{3,1},{4,6},{5,7},{6,4},{7,5},{8,10},{9,11},{10,... | collective-permute-start | bytes 294920 | tf_op jit(solution)/shard_map/ppermute | solution.py:366
  135.0 5.0 %collective-permute-done.3.p1 = bf16[2048,128]{1,0:T(8,128)(2,1)S(1)} collective-permute-done((bf16[2048,128]{1,0:T(8,128)(2,1)}, bf16[2048,128]{1,0:T(8,128)(2,1)S(1)}, u32[]{:S(2)}, u32[]{:S(2)}) %collective-permute-start.3) | collective-permute-done | bytes 524320 | tf_op jit(solution)/shard_map/ppermute | solution.py:366
  140.1 5.2 %collective-permute-start.11 = (bf16[384,128]{1,0:T(8,128)(2,1)S(1)}, bf16[384,128]{1,0:T(8,128)(2,1)S(1)}, u32[]{:S(2)}, u32[]{:S(2)}) collective-permute-start(bf16[384,128]{1,0:T(8,128)(2,1)S(1)} %pad_maximum_fusion.1.l0), channel_id=1, source_target_pairs={{0,3},{1,0},{2,1},{3,2},{4,7},{5,4},{6,5},{7,6},{8,11},{9,8},{10,9... | collective-permute-start | bytes 294920 | tf_op jit(solution)/shard_map/ppermute | solution.py:366
  145.3 0.1 broadcast_in_dim.12
  145.3 0.1 reshape_reshape.3.lengths_ref
  145.4 2.0 %collective-permute-done.11.l3 = bf16[384,128]{1,0:T(8,128)(2,1)S(1)} collective-permute-done((bf16[384,128]{1,0:T(8,128)(2,1)S(1)}, bf16[384,128]{1,0:T(8,128)(2,1)S(1)}, u32[]{:S(2)}, u32[]{:S(2)}) %collective-permute-start.11) | collective-permute-done | bytes 98336 | tf_op jit(solution)/shard_map/ppermute | solution.py:366
  147.4 1.2 copy-done.2
  148.7 4.2 %local_attend.1 = (bf16[144,128]{1,0:T(8,128)(2,1)S(1)}, bf16[144,128]{1,0:T(8,128)(2,1)S(1)}, bf16[144,128]{1,0:T(8,128)(2,1)S(1)}, bf16[144,128]{1,0:T(8,128)(2,1)S(1)}) custom-call(s32[3]{0:T(128)S(1)} %pad_add_fusion.where_ref.info, s32[1,128]{1,0:T(1,128)S(1)} %copy-done.9, s32[1,512]{1,0:T(1,128)S(1)} %reshape_reshape.3.lengths_ref, ...), custom_call_target="tpu_custom_call" | custom-call | tf_op jit(solution)/shard_map/local_attend/pallas_call | solution.py:291
  152.8 2.5 %collective-permute-start.12 = (bf16[144,128]{1,0:T(8,128)(2,1)S(1)}, bf16[144,128]{1,0:T(8,128)(2,1)S(1)}, u32[]{:S(2)}, u32[]{:S(2)}) collective-permute-start(bf16[144,128]{1,0:T(8,128)(2,1)S(1)} %get-tuple-element.26), channel_id=1, source_target_pairs={{0,1},{1,2},{2,3},{3,0},{4,5},{5,6},{6,7},{7,4},{8,9},{9,10},{10,1... | collective-permute-start | bytes 110600 | tf_op jit(solution)/shard_map/ppermute | solution.py:366
  155.3 6.1 %collective-permute-start.13 = (bf16[144,128]{1,0:T(8,128)(2,1)S(1)}, bf16[144,128]{1,0:T(8,128)(2,1)S(1)}, u32[]{:S(2)}, u32[]{:S(2)}) collective-permute-start(bf16[144,128]{1,0:T(8,128)(2,1)S(1)} %get-tuple-element.27), channel_id=1, source_target_pairs={{0,2},{1,3},{2,0},{3,1},{4,6},{5,7},{6,4},{7,5},{8,10},{9,11},{10,... | collective-permute-start | bytes 110600 | tf_op jit(solution)/shard_map/ppermute | solution.py:366
  161.4 1.9 %collective-permute-start.14 = (bf16[144,128]{1,0:T(8,128)(2,1)S(1)}, bf16[144,128]{1,0:T(8,128)(2,1)S(1)}, u32[]{:S(2)}, u32[]{:S(2)}) collective-permute-start(bf16[144,128]{1,0:T(8,128)(2,1)S(1)} %get-tuple-element.28), channel_id=1, source_target_pairs={{0,3},{1,0},{2,1},{3,2},{4,7},{5,4},{6,5},{7,6},{8,11},{9,8},{10,9... | collective-permute-start | bytes 110600 | tf_op jit(solution)/shard_map/ppermute | solution.py:366
  163.4 0.0 collective-permute-done.13.l2
  163.4 3.9 %collective-permute-done.14.l3 = bf16[144,128]{1,0:T(8,128)(2,1)S(1)} collective-permute-done((bf16[144,128]{1,0:T(8,128)(2,1)S(1)}, bf16[144,128]{1,0:T(8,128)(2,1)S(1)}, u32[]{:S(2)}, u32[]{:S(2)}) %collective-permute-start.14) | collective-permute-done | bytes 36896 | tf_op jit(solution)/shard_map/ppermute | solution.py:366
  167.3 1.0 finish.1
  (34 shorter events, 0.1 us)
Async XLA Ops:
  6.5 0.8 copy-start.5
  7.3 0.8 copy-start.7
  8.1 0.7 copy-start.8
  8.7 0.7 copy-start.10
  42.8 54.1 %all-to-all-start.1 = ((bf16[32,32,128]{2,1,0:T(8,128)(2,1)}), bf16[32,32,128]{2,1,0:T(8,128)(2,1)S(1)}, u32[]{:S(2)}, u32[]{:S(2)}) async-start(bf16[32,32,128]{2,1,0:T(8,128)(2,1)} %bitcast.5), calls=%async_computation.1 | async-start | bytes 524288 | tf_op jit(solution)/shard_map/all_to_all | solution.py:370
  50.5 96.9 %all-gather.3.cloned.1.call-start = ((), (), s32[]{:S(2)}) async-start(), calls=%async_computation.4 | async-start | bytes 1179648 | tf_op jit(solution)/shard_map/all_gather | solution.py:401
  51.3 1.6 copy-start
  52.9 0.8 copy-start.3
  55.5 41.3 %collective-permute-start = (bf16[2176,128]{1,0:T(8,128)(2,1)}, bf16[2176,128]{1,0:T(8,128)(2,1)S(1)}, u32[]{:S(2)}, u32[]{:S(2)}) collective-permute-start(bf16[2176,128]{1,0:T(8,128)(2,1)} %get-tuple-element.19), channel_id=1, source_target_pairs={{0,4},{4,8},{8,12},{12,0},{1,5},{5,9},{9,13},{13,1},{2,6},{6,10},{... | collective-permute-start | bytes 1671176 | tf_op jit(solution)/shard_map/ppermute | solution.py:366
  59.0 37.8 %collective-permute-start.1 = (bf16[2176,128]{1,0:T(8,128)(2,1)}, bf16[2176,128]{1,0:T(8,128)(2,1)}, u32[]{:S(2)}, u32[]{:S(2)}) collective-permute-start(bf16[2176,128]{1,0:T(8,128)(2,1)} %get-tuple-element.20), channel_id=1, source_target_pairs={{0,8},{4,12},{8,0},{12,4},{1,9},{5,13},{9,1},{13,5},{2,10},{6,14},... | collective-permute-start | bytes 1671176 | tf_op jit(solution)/shard_map/ppermute | solution.py:366
  63.8 33.0 %collective-permute-start.2 = (bf16[2176,128]{1,0:T(8,128)(2,1)}, bf16[2176,128]{1,0:T(8,128)(2,1)}, u32[]{:S(2)}, u32[]{:S(2)}) collective-permute-start(bf16[2176,128]{1,0:T(8,128)(2,1)} %get-tuple-element.21), channel_id=1, source_target_pairs={{0,12},{4,0},{8,4},{12,8},{1,13},{5,1},{9,5},{13,9},{2,14},{6,2},{... | collective-permute-start | bytes 1671176 | tf_op jit(solution)/shard_map/ppermute | solution.py:366
  67.2 21.9 %collective-permute-start.8 = (bf16[128,128]{1,0:T(8,128)(2,1)S(1)}, bf16[128,128]{1,0:T(8,128)(2,1)S(1)}, u32[]{:S(2)}, u32[]{:S(2)}) collective-permute-start(bf16[128,128]{1,0:T(8,128)(2,1)S(1)} %get-tuple-element.32), channel_id=1, source_target_pairs={{0,12},{4,0},{8,4},{12,8},{1,13},{5,1},{9,5},{13,9},{2,14},{6,2},{... | collective-permute-start | bytes 98312 | tf_op jit(solution)/shard_map/ppermute | solution.py:366
  69.1 24.4 %collective-permute-start.7 = (bf16[128,128]{1,0:T(8,128)(2,1)S(1)}, bf16[128,128]{1,0:T(8,128)(2,1)S(1)}, u32[]{:S(2)}, u32[]{:S(2)}) collective-permute-start(bf16[128,128]{1,0:T(8,128)(2,1)S(1)} %get-tuple-element.33), channel_id=1, source_target_pairs={{0,8},{4,12},{8,0},{12,4},{1,9},{5,13},{9,1},{13,5},{2,10},{6,14},... | collective-permute-start | bytes 98312 | tf_op jit(solution)/shard_map/ppermute | solution.py:366
  89.1 7.0 %collective-permute-start.6 = (bf16[128,128]{1,0:T(8,128)(2,1)S(1)}, bf16[128,128]{1,0:T(8,128)(2,1)S(1)}, u32[]{:S(2)}, u32[]{:S(2)}) collective-permute-start(bf16[128,128]{1,0:T(8,128)(2,1)S(1)} %get-tuple-element.34), channel_id=1, source_target_pairs={{0,4},{4,8},{8,12},{12,0},{1,5},{5,9},{9,13},{13,1},{2,6},{6,10},{... | collective-permute-start | bytes 98312 | tf_op jit(solution)/shard_map/ppermute | solution.py:366
  96.8 12.9 %copy-start.1 = (bf16[32,16,2048]{2,1,0:T(8,128)(2,1)S(1)}, bf16[32,16,2048]{2,1,0:T(8,128)(2,1)}, u32[]{:S(2)}) copy-start(bf16[32,16,2048]{2,1,0:T(8,128)(2,1)} %param.16) | copy-start | bytes 6291460
  101.8 20.0 %copy-start.4 = (bf16[128,128]{1,0:T(8,128)(2,1)S(1)}, bf16[128,128]{1,0:T(8,128)(2,1)}, u32[]{:S(2)}) copy-start(bf16[128,128]{1,0:T(8,128)(2,1)} %refs_1_.1) | copy-start | bytes 98308
  101.8 25.5 %copy-start.6 = (bf16[128,128]{1,0:T(8,128)(2,1)S(1)}, bf16[128,128]{1,0:T(8,128)(2,1)}, u32[]{:S(2)}) copy-start(bf16[128,128]{1,0:T(8,128)(2,1)} %q_ref.1) | copy-start | bytes 98308
  101.8 43.4 %copy-start.11 = (s32[32]{0:T(128)S(1)}, s32[32]{0:T(128)}, u32[]{:S(2)}) copy-start(s32[32]{0:T(128)} %param.17) | copy-start | bytes 388
  101.8 45.6 %copy-start.9 = (s32[1,128]{1,0:T(1,128)S(1)}, s32[1,128]{1,0:T(1,128)}, u32[]{:S(2)}) copy-start(s32[1,128]{1,0:T(1,128)} %leaf_ref.3) | copy-start | bytes 1540
  101.9 20.8 %all-to-all-start.2 = ((bf16[32,48,128]{2,1,0:T(8,128)(2,1)}), bf16[32,48,128]{2,1,0:T(8,128)(2,1)S(1)}, u32[]{:S(2)}, u32[]{:S(2)}) async-start(bf16[32,48,128]{2,1,0:T(8,128)(2,1)} %branch_attend.1), calls=%async_computation.2 | async-start | bytes 786432 | tf_op jit(solution)/shard_map/all_to_all | solution.py:370
  111.5 28.5 %collective-permute-start.3 = (bf16[2048,128]{1,0:T(8,128)(2,1)}, bf16[2048,128]{1,0:T(8,128)(2,1)S(1)}, u32[]{:S(2)}, u32[]{:S(2)}) collective-permute-start(bf16[2048,128]{1,0:T(8,128)(2,1)} %get-tuple-element.22), channel_id=1, source_target_pairs={{0,4},{4,8},{8,12},{12,0},{1,5},{5,9},{9,13},{13,1},{2,6},{6,10},{... | collective-permute-start | bytes 1572872 | tf_op jit(solution)/shard_map/ppermute | solution.py:366
  114.7 30.7 %collective-permute-start.4 = (bf16[2048,128]{1,0:T(8,128)(2,1)}, bf16[2048,128]{1,0:T(8,128)(2,1)S(1)}, u32[]{:S(2)}, u32[]{:S(2)}) collective-permute-start(bf16[2048,128]{1,0:T(8,128)(2,1)} %get-tuple-element.23), channel_id=1, source_target_pairs={{0,8},{4,12},{8,0},{12,4},{1,9},{5,13},{9,1},{13,5},{2,10},{6,14},... | collective-permute-start | bytes 1572872 | tf_op jit(solution)/shard_map/ppermute | solution.py:366
  118.2 27.2 %collective-permute-start.5 = (bf16[2048,128]{1,0:T(8,128)(2,1)}, bf16[2048,128]{1,0:T(8,128)(2,1)S(1)}, u32[]{:S(2)}, u32[]{:S(2)}) collective-permute-start(bf16[2048,128]{1,0:T(8,128)(2,1)} %get-tuple-element.24), channel_id=1, source_target_pairs={{0,12},{4,0},{8,4},{12,8},{1,13},{5,1},{9,5},{13,9},{2,14},{6,2},{... | collective-permute-start | bytes 1572872 | tf_op jit(solution)/shard_map/ppermute | solution.py:366
  124.0 43.3 %all-to-all-start.3 = ((bf16[4,80,128]{2,1,0:T(8,128)(2,1)}), bf16[4,80,128]{2,1,0:T(8,128)(2,1)S(1)}, u32[]{:S(2)}, u32[]{:S(2)}) async-start(bf16[4,80,128]{2,1,0:T(8,128)(2,1)} %merge_node.1), calls=%async_computation.3 | async-start | bytes 163840 | tf_op jit(solution)/shard_map/all_to_all | solution.py:370
  127.4 18.1 %collective-permute-start.9 = (bf16[384,128]{1,0:T(8,128)(2,1)S(1)}, bf16[384,128]{1,0:T(8,128)(2,1)S(1)}, u32[]{:S(2)}, u32[]{:S(2)}) collective-permute-start(bf16[384,128]{1,0:T(8,128)(2,1)S(1)} %pad_maximum_fusion.1.l0), channel_id=1, source_target_pairs={{0,1},{1,2},{2,3},{3,0},{4,5},{5,6},{6,7},{7,4},{8,9},{9,10},{10,1... | collective-permute-start | bytes 294920 | tf_op jit(solution)/shard_map/ppermute | solution.py:366
  130.7 14.7 %collective-permute-start.10 = (bf16[384,128]{1,0:T(8,128)(2,1)S(1)}, bf16[384,128]{1,0:T(8,128)(2,1)S(1)}, u32[]{:S(2)}, u32[]{:S(2)}) collective-permute-start(bf16[384,128]{1,0:T(8,128)(2,1)S(1)} %pad_maximum_fusion.1.l0), channel_id=1, source_target_pairs={{0,2},{1,3},{2,0},{3,1},{4,6},{5,7},{6,4},{7,5},{8,10},{9,11},{10,... | collective-permute-start | bytes 294920 | tf_op jit(solution)/shard_map/ppermute | solution.py:366
  140.1 7.4 %collective-permute-start.11 = (bf16[384,128]{1,0:T(8,128)(2,1)S(1)}, bf16[384,128]{1,0:T(8,128)(2,1)S(1)}, u32[]{:S(2)}, u32[]{:S(2)}) collective-permute-start(bf16[384,128]{1,0:T(8,128)(2,1)S(1)} %pad_maximum_fusion.1.l0), channel_id=1, source_target_pairs={{0,3},{1,0},{2,1},{3,2},{4,7},{5,4},{6,5},{7,6},{8,11},{9,8},{10,9... | collective-permute-start | bytes 294920 | tf_op jit(solution)/shard_map/ppermute | solution.py:366
  147.4 1.2 copy-start.2
  152.8 10.5 %collective-permute-start.12 = (bf16[144,128]{1,0:T(8,128)(2,1)S(1)}, bf16[144,128]{1,0:T(8,128)(2,1)S(1)}, u32[]{:S(2)}, u32[]{:S(2)}) collective-permute-start(bf16[144,128]{1,0:T(8,128)(2,1)S(1)} %get-tuple-element.26), channel_id=1, source_target_pairs={{0,1},{1,2},{2,3},{3,0},{4,5},{5,6},{6,7},{7,4},{8,9},{9,10},{10,1... | collective-permute-start | bytes 110600 | tf_op jit(solution)/shard_map/ppermute | solution.py:366
  155.3 8.1 %collective-permute-start.13 = (bf16[144,128]{1,0:T(8,128)(2,1)S(1)}, bf16[144,128]{1,0:T(8,128)(2,1)S(1)}, u32[]{:S(2)}, u32[]{:S(2)}) collective-permute-start(bf16[144,128]{1,0:T(8,128)(2,1)S(1)} %get-tuple-element.27), channel_id=1, source_target_pairs={{0,2},{1,3},{2,0},{3,1},{4,6},{5,7},{6,4},{7,5},{8,10},{9,11},{10,... | collective-permute-start | bytes 110600 | tf_op jit(solution)/shard_map/ppermute | solution.py:366
  161.4 5.9 %collective-permute-start.14 = (bf16[144,128]{1,0:T(8,128)(2,1)S(1)}, bf16[144,128]{1,0:T(8,128)(2,1)S(1)}, u32[]{:S(2)}, u32[]{:S(2)}) collective-permute-start(bf16[144,128]{1,0:T(8,128)(2,1)S(1)} %get-tuple-element.28), channel_id=1, source_target_pairs={{0,3},{1,0},{2,1},{3,2},{4,7},{5,4},{6,5},{7,6},{8,11},{9,8},{10,9... | collective-permute-start | bytes 110600 | tf_op jit(solution)/shard_map/ppermute | solution.py:366
Sparse Core Ops, SparseCore 0:
  96.9 24.8 all-gather.2

commit v2 on v1

--- a/solution.py
+++ b/solution.py
@@ -13,6 +13,7 @@
 F32 = jnp.float32
 NEG = -1e30
 FLOOR = -1e29
+COST_FLOPS = 30_000_000_000
 VMEM_LIMIT = 50 * 1024 * 1024
 
 
@@ -25,14 +26,51 @@
 
 
 SMEM = pl.BlockSpec(memory_space=pltpu.SMEM)
-ANY = pl.BlockSpec(memory_space=pl.ANY)
+HBM = pl.BlockSpec(memory_space=pltpu.HBM)
 
 
 def params():
     return pltpu.CompilerParams(vmem_limit_bytes=VMEM_LIMIT)
 
 
-def slot_kernel(parent, leaf_ref, q_ref, root_ref, out_ref, slot_ref):
+def first_kernel(
+    parent, leaf_hbm, q_hbm, root_hbm, cache_hbm, out_ref, slot_ref, sent_hbm,
+    leaf_ref, q_ref, root_ref, split_ref, sems, bulk,
+):
+    copies = [
+        pltpu.make_async_copy(source, target, sems.at[i])
+        for i, (source, target) in enumerate(
+            ((root_hbm, root_ref), (leaf_hbm, leaf_ref), (q_hbm, q_ref))
+        )
+    ]
+    for copy in copies:
+        copy.start()
+    moves = []
+    for target in range(4):
+        for part in range(4):
+            lane = (part // 2) * 1024 + target * 256 + (part % 2) * 128
+            moves.append(
+                pltpu.make_async_copy(
+                    cache_hbm.at[:, pl.ds(lane, 128)],
+                    sent_hbm.at[target, pl.ds(part * 512, 512), :],
+                    bulk.at[target, part],
+                )
+            )
+    for move in moves:
+        move.start()
+    for copy in copies:
+        copy.wait()
+    root = root_ref[...].astype(F32)
+    splits = []
+    for target in range(4):
+        lanes = [kv * 1024 + target * 256 + half * 128 for kv in range(2) for half in range(2)]
+        split_ref[target] = jnp.concatenate([root[:, l : l + 128] for l in lanes], axis=0).astype(BF)
+        splits.append(
+            pltpu.make_async_copy(
+                split_ref.at[target], sent_hbm.at[target, pl.ds(2048, 32), :], sems.at[3 + target]
+            )
+        )
+        splits[-1].start()
     leaf = leaf_ref[...]
     across = jnp.broadcast_to(leaf.astype(F32), (128, 128))
     down = across.T
@@ -45,66 +83,92 @@
     slot_ref[...] = slot
     pick = jnp.where(iota((256, 128), 0) == slot, 1.0, 0.0).astype(BF)
     routed = jnp.dot(pick, q_ref[...], preferred_element_type=F32).astype(BF)
-    root = root_ref[...].astype(F32)
-    blocks = jnp.concatenate([root[:, j * 128 : (j + 1) * 128] for j in range(16)], axis=0).astype(BF)
-    for z in range(4):
-        out_ref[z, 0:64] = routed[z * 64 : (z + 1) * 64]
-        out_ref[z, 64:192] = blocks
-
-
-def route_slots(parent, leaf, queries, root):
+    out_ref[...] = routed.reshape(4, 64, 128)
+    for copy in moves + splits:
+        copy.wait()
+
+
+def first_stage(parent, leaf, queries, root, cache):
     return pl.pallas_call(
-        slot_kernel,
+        first_kernel,
         out_shape=(
-            jax.ShapeDtypeStruct((4, 192, 128), BF),
+            jax.ShapeDtypeStruct((4, 64, 128), BF),
             jax.ShapeDtypeStruct((1, 128), jnp.int32),
+            jax.ShapeDtypeStruct((4, 2080, 128), BF),
         ),
-        in_specs=[SMEM, whole((1, 128)), whole((128, 128)), whole((8, 2048))],
-        out_specs=(whole((4, 192, 128)), whole((1, 128))),
+        in_specs=[SMEM, HBM, HBM, HBM, HBM],
+        out_specs=(whole((4, 64, 128)), whole((1, 128)), HBM),
+        scratch_shapes=[
+            pltpu.VMEM((1, 128), jnp.int32),
+            pltpu.VMEM((128, 128), BF),
+            pltpu.VMEM((8, 2048), BF),
+            pltpu.VMEM((4, 32, 128), BF),
+            pltpu.SemaphoreType.DMA((7,)),
+            pltpu.SemaphoreType.DMA((4, 4)),
+        ],
         compiler_params=params(),
-        name="route_slots",
-    )(parent, leaf, queries, root)
-
-
-def pack_cache(where, cache, extra):
-    rows = 2048 + (128 if extra is not None else 0)
-
-    def kernel(where_ref, *refs):
-        cache_ref = refs[0]
-        outs = refs[-4:-1]
-        sems = refs[-1]
-        copies = []
-        for s in range(3):
-            target = (where_ref[0] + (s + 1)) & 3
-            for part in range(4):
-                start = (part // 2) * 1024 + (part % 2) * 128
-                lane = pl.multiple_of(target * 256 + start, 128)
-                copies.append(
-                    pltpu.make_async_copy(
-                        cache_ref.at[:, pl.ds(lane, 128)],
-                        outs[s].at[pl.ds(part * 512, 512), :],
-                        sems.at[s, part],
-                    )
+        name="first_stage",
+    )(parent, leaf, queries, root, cache)
+
+
+def pack_kernel(info, cache_hbm, g0, g1, g2, g3, out1, out2, out3, own, blocks, sems, bulk):
+    y = info[0]
+    zl = info[1]
+    moves = []
+    for s, out in enumerate((out1, out2, out3)):
+        target = (y + (s + 1)) & 3
+        for part in range(4):
+            start = (part // 2) * 1024 + (part % 2) * 128
+            lane = pl.multiple_of(target * 256 + start, 128)
+            moves.append(
+                pltpu.make_async_copy(
+                    cache_hbm.at[:, pl.ds(lane, 128)],
+                    out.at[pl.ds(part * 512, 512), :],
+                    bulk.at[s, part],
                 )
-            if extra is not None:
-                copies.append(
-                    pltpu.make_async_copy(refs[1], outs[s].at[pl.ds(2048, 128), :], sems.at[s, 4])
+            )
+    for move in moves:
+        move.start()
+    firsts = [
+        pltpu.make_async_copy(ref.at[pl.ds(128, 128), :], blocks.at[(zl - s) & 3], sems.at[0, s])
+        for s, ref in enumerate((g0, g1, g2, g3))
+    ]
+    for copy in firsts:
+        copy.start()
+    for copy in firsts:
+        copy.wait()
+    seconds = []
+    for s, (out, row) in enumerate(((own, 0), (out1, 2048), (out2, 2048), (out3, 2048))):
+        first = (((y + s) & 3) & 1) * 2
+        for half in range(2):
+            seconds.append(
+                pltpu.make_async_copy(
+                    blocks.at[first + half],
+                    out.at[pl.ds(row + half * 128, 128), :],
+                    sems.at[1 + half, s],
                 )
-        for copy in copies:
-            copy.start()
-        for copy in copies:
-            copy.wait()
-
-    operands = (where, cache) + ((extra,) if extra is not None else ())
+            )
+    for copy in seconds:
+        copy.start()
+    for copy in moves + seconds:
+        copy.wait()
+
+
+def pack_leaf(info, cache, gathered):
     return pl.pallas_call(
-        kernel,
-        out_shape=tuple(jax.ShapeDtypeStruct((rows, 128), BF) for _ in range(3)),
-        in_specs=[SMEM] + [ANY] * (len(operands) - 1),
-        out_specs=(ANY, ANY, ANY),
-        scratch_shapes=[pltpu.SemaphoreType.DMA((3, 5))],
+        pack_kernel,
+        out_shape=tuple(jax.ShapeDtypeStruct((2304, 128), BF) for _ in range(3))
+        + (jax.ShapeDtypeStruct((256, 128), BF),),
+        in_specs=[SMEM] + [HBM] * 5,
+        out_specs=(HBM, HBM, HBM, HBM),
+        scratch_shapes=[
+            pltpu.VMEM((4, 128, 128), BF),
+            pltpu.SemaphoreType.DMA((3, 4)),
+            pltpu.SemaphoreType.DMA((3, 4)),
+        ],
         compiler_params=params(),
-        name="pack_cache",
-    )(*operands)
+        name="pack_leaf",
+    )(info, cache, *gathered)
 
 
 def softmax_parts(scores, values):
@@ -146,21 +210,19 @@
     return jnp.concatenate([ref[base : base + 512], ref[base + 512 : base + 1024]], axis=1)
 
 
-def branch_kernel(info, q_ref, kown, vown, p1, p2, p3, out_ref):
-    y = info[0]
+def branch_kernel(info, q_ref, sent_ref, out_ref):
     zl = info[1]
     length = info[2]
     loaded = q_ref[...].reshape(8, 4, 32, 128)
     blocks = [loaded[:, z].reshape(256, 128) for z in range(4)]
-    keys = [kown[...]] + [piece(ref, 0) for ref in (p1, p2, p3)]
-    values = [vown[...]] + [piece(ref, 1) for ref in (p1, p2, p3)]
+    keys = [piece(sent_ref.at[s], 0) for s in range(4)]
+    values = [piece(sent_ref.at[s], 1) for s in range(4)]
     row16 = iota((256, 128), 0) & 31
     for h in range(2):
         queries = jnp.concatenate([blocks[2 * h], blocks[2 * h + 1]], axis=1)
         scores = []
         for s in range(4):
-            source = (y - s) & 3
-            place = (source * 4 + zl) * 512 + iota((256, 512), 1)
+            place = (s * 4 + zl) * 512 + iota((256, 512), 1)
             scores.append(jnp.where(place < length, score(queries, keys[s]), NEG))
         highest, total, summed = softmax_parts(scores, values)
         first = jnp.where(row16 < 16, 0, 64)
@@ -175,23 +237,20 @@
                 out_ref[xc * 4 + 2 * h + half, 32:48] = packed
 
 
-def branch_attend(info, arrived, cache, pieces):
-    head = pl.BlockSpec((512, 256), lambda i, info: (0, info[0]))
-    head_value = pl.BlockSpec((512, 256), lambda i, info: (0, 4 + info[0]))
+def branch_attend(info, arrived, sent):
     full = lambda shape: pl.BlockSpec(shape, lambda i, info: (0,) * len(shape))
-    rows = pieces[0].shape[0]
     return pl.pallas_call(
         branch_kernel,
         out_shape=jax.ShapeDtypeStruct((32, 48, 128), BF),
         grid_spec=pltpu.PrefetchScalarGridSpec(
             num_scalar_prefetch=1,
             grid=(1,),
-            in_specs=[full((32, 32, 128)), head, head_value] + [full((rows, 128))] * 3,
+            in_specs=[full((32, 32, 128)), full((4, 2080, 128))],
             out_specs=full((32, 48, 128)),
         ),
         compiler_params=params(),
         name="branch_attend",
-    )(info, arrived, cache, cache, *pieces)
+    )(info, arrived, sent)
 
 
 def merge_kernel(in_ref, out_ref):
@@ -234,22 +293,22 @@
 
 
 def local_kernel(
-    info, leaf_ref, lengths_ref, kown, vown, p1, p2, p3, root_ref, l0, l1, l2, l3,
-    out0, out1, out2, out3, gathered, outgoing,
+    info, leaf_ref, lengths_ref, kown, vown, p1, p2, p3, own, root_ref, l0, l1, l2, l3,
+    out0, out1, out2, out3, gathered, suffix, outgoing,
 ):
     y = info[0]
     zl = info[1]
     for s, ref in enumerate((l0, l1, l2, l3)):
-        gathered[(zl - s) & 3] = ref[...]
+        gathered[(zl - s) & 3] = ref[0:128]
+    suffix[0] = own[...]
+    for s, ref in enumerate((p1, p2, p3)):
+        suffix[s + 1] = ref[2048:2304]
     leaf_row = jnp.broadcast_to(leaf_ref[...].astype(F32), (128, 128))
     leaf_col = leaf_row.T
-    first_half = (y & 1) * 2
-    suffix_k = jnp.concatenate(
-        [gathered[first_half, 128:256], gathered[first_half + 1, 128:256]], axis=1
-    )
-    suffix_v = jnp.concatenate(
-        [gathered[first_half, 256:384], gathered[first_half + 1, 256:384]], axis=1
-    )
+    key_step = (y - (y >> 1)) & 3
+    value_step = (y - 2 - (y >> 1)) & 3
+    suffix_k = jnp.concatenate([suffix[key_step, 0:128], suffix[key_step, 128:256]], axis=1)
+    suffix_v = jnp.concatenate([suffix[value_step, 0:128], suffix[value_step, 128:256]], axis=1)
     root = root_ref[...].reshape(8, 4, 4, 32, 128)
     root_parts = [root[:, :, j].reshape(1024, 128) for j in range(4)]
     root_k = jnp.concatenate(root_parts[0:2], axis=1)
@@ -262,7 +321,7 @@
     key_slot = iota((1, 512), 1)
     first = (iota((128, 128), 0) >> 4) * 16
     for h in range(2):
-        queries = jnp.concatenate([gathered[2 * h, 0:128], gathered[2 * h + 1, 0:128]], axis=1)
+        queries = jnp.concatenate([gathered[2 * h], gathered[2 * h + 1]], axis=1)
         scores = [score(queries, root_k)]
         for s in range(4):
             source = (y - s) & 3
@@ -284,7 +343,7 @@
         ref[...] = outgoing[(zl + s) & 3]
 
 
-def local_attend(info, leaf, lengths, cache, pieces, root, gathered):
+def local_attend(info, leaf, lengths, cache, pieces, own, root, gathered):
     head = pl.BlockSpec((512, 256), lambda i, info: (0, info[0]))
     head_value = pl.BlockSpec((512, 256), lambda i, info: (0, 4 + info[0]))
     full = lambda shape: pl.BlockSpec(shape, lambda i, info: (0,) * len(shape))
@@ -295,15 +354,22 @@
             num_scalar_prefetch=1,
             grid=(1,),
             in_specs=[full((1, 128)), full((1, 512)), head, head_value]
-            + [full((2048, 128))] * 3
-            + [full((8, 512, 128))]
-            + [full((384, 128))] * 4,
+            + [full((2304, 128))] * 3
+            + [full((256, 128)), full((8, 512, 128))]
+            + [full((256, 128))] * 4,
             out_specs=tuple(full((144, 128)) for _ in range(4)),
-            scratch_shapes=[pltpu.VMEM((4, 384, 128), BF), pltpu.VMEM((4, 144, 128), BF)],
+            scratch_shapes=[
+                pltpu.VMEM((4, 128, 128), BF),
+                pltpu.VMEM((4, 256, 128), BF),
+                pltpu.VMEM((4, 144, 128), BF),
+            ],
         ),
         compiler_params=params(),
+        cost_estimate=pl.CostEstimate(
+            flops=COST_FLOPS, transcendentals=1_000_000, bytes_accessed=8_000_000
+        ),
         name="local_attend",
-    )(info, leaf, lengths, cache, cache, *pieces, root, *gathered)
+    )(info, leaf, lengths, cache, cache, *pieces, own, root, *gathered)
 
 
 def final_kernel(slot_ref, branch_ref, l0, l1, l2, l3, out_ref):
@@ -380,43 +446,38 @@
     branch_rows = branch_cache.reshape(512, 2048)
     leaf_rows = leaf_cache.reshape(512, 2048)
 
-    routed, slot = route_slots(leaf_parent, suffix_leaf, queries, root_cache)
-    arrived = exchange(routed, "zh")
-
-    branch_out = pack_cache(info, branch_rows, suffix_cache)
-    branch_in = [shift(branch_out[s], "y", s + 1) for s in range(3)]
-    leaf_out = pack_cache(info, leaf_rows, None)
-    leaf_in = [shift(leaf_out[s], "y", s + 1) for s in range(3)]
+    tie = lax.optimization_barrier
+    routed, slot, sent = first_stage(
+        leaf_parent, suffix_leaf, queries, root_cache, branch_rows
+    )
+    sent = exchange(sent, "y")
+    mine = jnp.concatenate([queries, suffix_cache], axis=0)
+    gathered = [mine] + [shift(mine, "zl", s + 1) for s in range(3)]
+    packed = pack_leaf(info, leaf_rows, gathered)
+    own = packed[3]
+    onward = jnp.concatenate(
+        [routed, jnp.broadcast_to(sent[:, 2048:2080].reshape(1, 128, 128), (4, 128, 128))], axis=1
+    )
+    onward, packed = tie((onward, packed))
+    arrived = exchange(onward, "zh")
+    leaf_in = [shift(packed[s], "y", s + 1) for s in range(3)]
 
     onward = arrived[:, 0:64].reshape(4, 8, 8, 128).transpose(1, 0, 2, 3).reshape(8, 1, 32, 128)
     onward = jnp.broadcast_to(onward, (8, 4, 32, 128)).reshape(32, 32, 128)
     node_queries = exchange(onward, XCZ)
 
-    root = arrived[:, 64:192].reshape(4, 2, 4, 2, 8, 128).transpose(2, 1, 3, 0, 4, 5)
-    root = root.reshape(4, 4 * 32, 128)
-    root_parts = [lax.dynamic_index_in_dim(root, y, 0, keepdims=False)]
-    for s in range(3):
-        part = lax.dynamic_index_in_dim(root, (y + (s + 1)) & 3, 0, keepdims=False)
-        root_parts.append(shift(part, "y", s + 1))
-    root_all = lax.all_gather(jnp.concatenate(root_parts, axis=0), XC, axis=0, tiled=False)
-
-    partials = branch_attend(info, node_queries, branch_rows, branch_in)
-
-    blocks = [suffix_cache] + [part[2048:2176] for part in branch_in]
-
-    def chosen(source):
-        step = (y - source) & 3
-        return lax.select_n(step, *blocks)
-
-    mine = jnp.concatenate([queries, chosen(y // 2), chosen(2 + y // 2)], axis=0)
-    gathered = [mine] + [shift(mine, "zl", s + 1) for s in range(3)]
-
+    root = arrived[:, 64:192].reshape(4, 4, 4, 8, 128).transpose(1, 2, 0, 3, 4)
+    root_all = lax.all_gather(root.reshape(512, 128), XC, axis=0, tiled=False)
+
+    partials = branch_attend(info, node_queries, sent)
     returned = exchange(partials, XCZ)
     merged = merge_node(returned)
+    lengths = jnp.repeat(leaf_length, 16).reshape(1, 512)
+    local = local_attend(
+        info, suffix_leaf, lengths, leaf_rows, leaf_in, own, root_all, gathered
+    )
+    merged, local = tie((merged, local))
     back = exchange(merged, "zh")
-
-    lengths = jnp.repeat(leaf_length, 16).reshape(1, 512)
-    local = local_attend(info, suffix_leaf, lengths, leaf_rows, leaf_in, root_all, gathered)
     parts = [local[0]] + [shift(local[s + 1], "zl", s + 1) for s in range(3)]
     return finish(slot, back, parts)
 

time: 176 us -> 153 us (0.87)
  starting transfers between devices: 75 us -> 55.2 us
  waiting for transfers between devices: 29 us -> 27 us
    ppermute x15 -> x9, starting transfers between devices: 56.1 us -> 32 us  [shift(): return lax.ppermute(values, axis, [(i, (i + step) % 4) for i in range(4)])]
    ppermute x15 -> x9, waiting for transfers between devices: 28.9 us -> 18.5 us  [shift(): return lax.ppermute(values, axis, [(i, (i + step) % 4) for i in range(4)])]
    all_to_all x3 -> x4, waiting for transfers between devices: 0.01 us -> 8.54 us  [exchange(): return lax.all_to_all(values, axis, split_axis=0, concat_axis=0, tiled=True)]
    all_to_all x3 -> x4, starting transfers between devices: 18.9 us -> 23.3 us  [exchange(): return lax.all_to_all(values, axis, split_axis=0, concat_axis=0, tiled=True)]
    unnamed x24 -> x25, local copies, waits for them, and re-layouts: 6.42 us -> 7.3 us
    pallas_call x3 -> x2, Pallas kernels: 4.49 us -> 4.42 us  [the longest x1 2.26 us: pack_leaf(): pl.pallas_call(pack_kernel, out_shape=tuple((jax.ShapeDtypeStruct((2304,...]
  transfers between devices with their start and end apart: 19 -> 14, of which waited for: 5 -> 6; matrix products, arithmetic and copies ran while one was open for 1% -> 1% of each run, Pallas kernels for 8% -> 7%
where the time goes in v2:
time: 153 us; the launch traced here: 151 us
  starting transfers between devices  55.2 us (36%)
  blocking collectives  30.7 us (20%)
  waiting for transfers between devices  27 us (18%)
  Pallas kernels  15.2 us (10%)
  between operations  14.3 us (9%)
  local copies, waits for them, and re-layouts  8.94 us (6%)
    ppermute x9, starting transfers between devices, shift(): return lax.ppermute(values, axis, [(i, (i + step) % 4) for i in range(4)])  32 us
    all_to_all x1, blocking collectives, exchange(): return lax.all_to_all(values, axis, split_axis=0, concat_axis=0, tiled=True)  30.7 us
    all_to_all x4, starting transfers between devices, exchange(): return lax.all_to_all(values, axis, split_axis=0, concat_axis=0, tiled=True)  23.3 us
    ppermute x9, waiting for transfers between devices, shift(): return lax.ppermute(values, axis, [(i, (i + step) % 4) for i in range(4)])  18.5 us
    all_to_all x4, waiting for transfers between devices, exchange(): return lax.all_to_all(values, axis, split_axis=0, concat_axis=0, tiled=True)  8.54 us
    unnamed x25, local copies, waits for them, and re-layouts  7.3 us
    pallas_call x1, Pallas kernels, local_attend(): pl.pallas_call(local_kernel, out_shape=tuple((jax.ShapeDtypeStruct((144,...  4.72 us
    pallas_call x1, Pallas kernels, branch_attend(): pl.pallas_call(branch_kernel, out_shape=jax.ShapeDtypeStruct((32, 48, 128...  3.64 us
  transfers between devices with their start and end apart: 14, of which 6 were waited for; matrix products, arithmetic and copies ran while one was open for 1% of the time, Pallas kernels for 7%

profile of v2, /device:TPU:6, one launch (start us, length us, event | category | flops | bytes accessed | tf_op | source)
XLA Modules:
  0.0 151.4 jit_solution(16481917068465279663)
XLA Ops:
  6.5 1.6 %copy-done = bf16[1,512,2048]{2,1,0:T(8,128)(2,1)S(1)} copy-done((bf16[1,512,2048]{2,1,0:T(8,128)(2,1)S(1)}, bf16[1,512,2048]{2,1,0:T(8,128)(2,1)}, u32[]{:S(2)}) %copy-start) | copy-done | bytes 2097176
  8.1 0.8 copy-done.1
  8.9 0.8 copy-done.3
  9.6 0.7 copy-done.4
  10.3 0.7 copy-done.5
  11.0 2.2 %first_stage.1 = (bf16[4,64,128]{2,1,0:T(8,128)(2,1)S(1)}, s32[1,128]{1,0:T(1,128)S(1)}, bf16[4,2080,128]{2,1,0:T(8,128)(2,1)}) custom-call(s32[1,32]{1,0:T(1,128)S(1)} %copy-done.4, s32[1,128]{1,0:T(1,128)S(1)} %copy-done.5, bf16[128,128]{1,0:T(8,128)(2,1)S(1)} %copy-done.1, bf16[8,2048]{1,0:T(8,128)(2,1)S(1)} %copy-done.3, bf16[512,2048]{1,0:T(8,128)(2,1)S(1)} %bitcast.17), custom_call_target="tpu_custom_call" | custom-call | tf_op jit(solution)/shard_map/first_stage/pallas_call | solution.py:92
  13.1 0.0 copy-start.2
  13.1 0.0 copy-start.10
  13.1 4.5 %all-to-all-start = ((bf16[4,2080,128]{2,1,0:T(8,128)(2,1)}), bf16[4,2080,128]{2,1,0:T(8,128)(2,1)S(1)}, u32[]{:S(2)}, u32[]{:S(2)}) async-start(bf16[4,2080,128]{2,1,0:T(8,128)(2,1)} %get-tuple-element.27), calls=%async_computation | async-start | bytes 4259840 | tf_op jit(solution)/shard_map/all_to_all | solution.py:436
  17.7 3.8 %collective-permute-start = (bf16[256,128]{1,0:T(8,128)(2,1)S(1)}, bf16[256,128]{1,0:T(8,128)(2,1)S(1)}, u32[]{:S(2)}, u32[]{:S(2)}) collective-permute-start(bf16[256,128]{1,0:T(8,128)(2,1)S(1)} %constant_dynamic-update-slice_fusion.g0.l0), channel_id=1, source_target_pairs={{0,1},{1,2},{2,3},{3,0},{4,5},{5,6},{6,7},{7,4},{8,9},{9,10},{10,1... | collective-permute-start | bytes 196616 | tf_op jit(solution)/shard_map/ppermute | solution.py:432
  21.5 5.2 %collective-permute-start.1 = (bf16[256,128]{1,0:T(8,128)(2,1)S(1)}, bf16[256,128]{1,0:T(8,128)(2,1)S(1)}, u32[]{:S(2)}, u32[]{:S(2)}) collective-permute-start(bf16[256,128]{1,0:T(8,128)(2,1)S(1)} %constant_dynamic-update-slice_fusion.g0.l0), channel_id=1, source_target_pairs={{0,2},{1,3},{2,0},{3,1},{4,6},{5,7},{6,4},{7,5},{8,10},{9,11},{10,... | collective-permute-start | bytes 196616 | tf_op jit(solution)/shard_map/ppermute | solution.py:432
  26.7 2.9 %collective-permute-start.2 = (bf16[256,128]{1,0:T(8,128)(2,1)S(1)}, bf16[256,128]{1,0:T(8,128)(2,1)S(1)}, u32[]{:S(2)}, u32[]{:S(2)}) collective-permute-start(bf16[256,128]{1,0:T(8,128)(2,1)S(1)} %constant_dynamic-update-slice_fusion.g0.l0), channel_id=1, source_target_pairs={{0,3},{1,0},{2,1},{3,2},{4,7},{5,4},{6,5},{7,6},{8,11},{9,8},{10,9... | collective-permute-start | bytes 196616 | tf_op jit(solution)/shard_map/ppermute | solution.py:432
  30.3 0.1 pad_add_fusion.info
  30.3 0.0 collective-permute-done.g1.l1
  30.3 0.0 collective-permute-done.1.g2.l2
  30.3 2.5 %collective-permute-done.2.g3.l3 = bf16[256,128]{1,0:T(8,128)(2,1)S(1)} collective-permute-done((bf16[256,128]{1,0:T(8,128)(2,1)S(1)}, bf16[256,128]{1,0:T(8,128)(2,1)S(1)}, u32[]{:S(2)}, u32[]{:S(2)}) %collective-permute-start.2) | collective-permute-done | bytes 65568 | tf_op jit(solution)/shard_map/ppermute | solution.py:432
  32.8 2.3 %pack_leaf.1 = (bf16[2304,128]{1,0:T(8,128)(2,1)S(1)}, bf16[2304,128]{1,0:T(8,128)(2,1)S(1)}, bf16[2304,128]{1,0:T(8,128)(2,1)S(1)}, bf16[256,128]{1,0:T(8,128)(2,1)S(1)}) custom-call(s32[3]{0:T(128)S(1)} %pad_add_fusion.info, bf16[512,2048]{1,0:T(8,128)(2,1)} %bitcast.18, bf16[256,128]{1,0:T(8,128)(2,1)S(1)} %constant_dynamic-update-slice_fusion.g0.l0, ...), custom_call_target="tpu_custom_call" | custom-call | tf_op jit(solution)/shard_map/pack_leaf/pallas_call | solution.py:158
  35.1 0.8 copy-done.8
  35.9 0.8 copy-done.9
  36.8 7.6 %all-to-all-done.sent_ref = bf16[4,2080,128]{2,1,0:T(8,128)(2,1)S(1)} async-done(((bf16[4,2080,128]{2,1,0:T(8,128)(2,1)}), bf16[4,2080,128]{2,1,0:T(8,128)(2,1)S(1)}, u32[]{:S(2)}, u32[]{:S(2)}) %all-to-all-start) | async-done | bytes 2129952 | tf_op jit(solution)/shard_map/all_to_all | solution.py:436
  44.4 30.7 %all_to_all.25 = bf16[4,192,128]{2,1,0:T(8,128)(2,1)S(1)} all-to-all(bf16[4,192,128]{2,1,0:T(8,128)(2,1)S(1)} %pad_maximum_fusion), channel_id=1, replica_groups=mesh['zh'=4,'x'=4,'core'=2,'y'=4,'zl'=4] {'zh'}, dimensions={0} | all-to-all | bytes 393216 | tf_op jit(solution)/shard_map/all_to_all | solution.py:436
  75.1 0.7 copy.15
  75.7 0.0 all-gather.2.cloned.1.call-update
  75.8 0.8 broadcast_in_dim.20
  76.5 7.8 %all-to-all-start.2 = ((bf16[32,32,128]{2,1,0:T(8,128)(2,1)}), bf16[32,32,128]{2,1,0:T(8,128)(2,1)S(1)}, u32[]{:S(2)}, u32[]{:S(2)}) async-start(bf16[32,32,128]{2,1,0:T(8,128)(2,1)} %bitcast.21), calls=%async_computation.2 | async-start | bytes 524288 | tf_op jit(solution)/shard_map/all_to_all | solution.py:436
  84.4 2.5 %collective-permute-start.3 = (bf16[2304,128]{1,0:T(8,128)(2,1)}, bf16[2304,128]{1,0:T(8,128)(2,1)}, u32[]{:S(2)}, u32[]{:S(2)}) collective-permute-start(bf16[2304,128]{1,0:T(8,128)(2,1)} %copy-done.9), channel_id=1, source_target_pairs={{0,4},{4,8},{8,12},{12,0},{1,5},{5,9},{9,13},{13,1},{2,6},{6,10},{... | collective-permute-start | bytes 1769480 | tf_op jit(solution)/shard_map/ppermute | solution.py:432
  86.9 4.0 %collective-permute-start.4 = (bf16[2304,128]{1,0:T(8,128)(2,1)}, bf16[2304,128]{1,0:T(8,128)(2,1)}, u32[]{:S(2)}, u32[]{:S(2)}) collective-permute-start(bf16[2304,128]{1,0:T(8,128)(2,1)} %copy-done.8), channel_id=1, source_target_pairs={{0,8},{4,12},{8,0},{12,4},{1,9},{5,13},{9,1},{13,5},{2,10},{6,14},... | collective-permute-start | bytes 1769480 | tf_op jit(solution)/shard_map/ppermute | solution.py:432
  90.9 2.6 %collective-permute-start.5 = (bf16[2304,128]{1,0:T(8,128)(2,1)S(1)}, bf16[2304,128]{1,0:T(8,128)(2,1)}, u32[]{:S(2)}, u32[]{:S(2)}) collective-permute-start(bf16[2304,128]{1,0:T(8,128)(2,1)S(1)} %get-tuple-element.35), channel_id=1, source_target_pairs={{0,12},{4,0},{8,4},{12,8},{1,13},{5,1},{9,5},{13,9},{2,14},{6,2},{... | collective-permute-start | bytes 1769480 | tf_op jit(solution)/shard_map/ppermute | solution.py:432
  93.4 0.1 broadcast_in_dim.21
  93.5 0.1 reshape_reshape.3.lengths_ref
  93.6 0.0 all-to-all-done.2.q_ref
  93.6 3.6 %branch_attend.1 = bf16[32,48,128]{2,1,0:T(8,128)(2,1)} custom-call(s32[3]{0:T(128)S(1)} %pad_add_fusion.info, bf16[32,32,128]{2,1,0:T(8,128)(2,1)S(1)} %all-to-all-done.2.q_ref, bf16[4,2080,128]{2,1,0:T(8,128)(2,1)S(1)} %all-to-all-done.sent_ref), custom_call_target="tpu_custom_call" | custom-call | tf_op jit(solution)/shard_map/branch_attend/pallas_call | solution.py:242
  97.2 7.7 %all-to-all-start.3 = ((bf16[32,48,128]{2,1,0:T(8,128)(2,1)}), bf16[32,48,128]{2,1,0:T(8,128)(2,1)S(1)}, u32[]{:S(2)}, u32[]{:S(2)}) async-start(bf16[32,48,128]{2,1,0:T(8,128)(2,1)} %branch_attend.1), calls=%async_computation.3 | async-start | bytes 786432 | tf_op jit(solution)/shard_map/all_to_all | solution.py:436
  104.9 10.9 %collective-permute-done.3.p1 = bf16[2304,128]{1,0:T(8,128)(2,1)} collective-permute-done((bf16[2304,128]{1,0:T(8,128)(2,1)}, bf16[2304,128]{1,0:T(8,128)(2,1)}, u32[]{:S(2)}, u32[]{:S(2)}) %collective-permute-start.3) | collective-permute-done | bytes 589856 | tf_op jit(solution)/shard_map/ppermute | solution.py:432
  115.8 0.0 collective-permute-done.4.p2
  115.9 2.5 %collective-permute-done.5.p3 = bf16[2304,128]{1,0:T(8,128)(2,1)} collective-permute-done((bf16[2304,128]{1,0:T(8,128)(2,1)S(1)}, bf16[2304,128]{1,0:T(8,128)(2,1)}, u32[]{:S(2)}, u32[]{:S(2)}) %collective-permute-start.5) | collective-permute-done | bytes 589856 | tf_op jit(solution)/shard_map/ppermute | solution.py:432
  118.4 1.2 copy-done.7
  119.6 4.7 %local_attend.1 = (bf16[144,128]{1,0:T(8,128)(2,1)S(1)}, bf16[144,128]{1,0:T(8,128)(2,1)S(1)}, bf16[144,128]{1,0:T(8,128)(2,1)S(1)}, bf16[144,128]{1,0:T(8,128)(2,1)S(1)}) custom-call(s32[3]{0:T(128)S(1)} %pad_add_fusion.info, s32[1,128]{1,0:T(1,128)S(1)} %copy-done.6, s32[1,512]{1,0:T(1,128)S(1)} %reshape_reshape.3.lengths_ref, bf16[512,2048]{1,0:T(8,128)(2,1)} %bitcast.19, ...), custom_call_target="tpu_custom_call" | custom-call | flops 30000001024 | bytes 8000000 | tf_op jit(solution)/shard_map/local_attend/pallas_call | solution.py:350
  124.3 0.0 all-to-all-done.3.in_ref
  124.4 1.4 merge_node.1
  125.7 3.3 %all-to-all-start.4 = ((bf16[4,80,128]{2,1,0:T(8,128)(2,1)}), bf16[4,80,128]{2,1,0:T(8,128)(2,1)S(1)}, u32[]{:S(2)}, u32[]{:S(2)}) async-start(bf16[4,80,128]{2,1,0:T(8,128)(2,1)} %merge_node.1), calls=%async_computation.4 | async-start | bytes 163840 | tf_op jit(solution)/shard_map/all_to_all | solution.py:436
  129.0 3.4 %collective-permute-start.6 = (bf16[144,128]{1,0:T(8,128)(2,1)S(1)}, bf16[144,128]{1,0:T(8,128)(2,1)S(1)}, u32[]{:S(2)}, u32[]{:S(2)}) collective-permute-start(bf16[144,128]{1,0:T(8,128)(2,1)S(1)} %get-tuple-element.42), channel_id=1, source_target_pairs={{0,1},{1,2},{2,3},{3,0},{4,5},{5,6},{6,7},{7,4},{8,9},{9,10},{10,1... | collective-permute-start | bytes 110600 | tf_op jit(solution)/shard_map/ppermute | solution.py:432
  132.4 4.3 %collective-permute-start.7 = (bf16[144,128]{1,0:T(8,128)(2,1)S(1)}, bf16[144,128]{1,0:T(8,128)(2,1)S(1)}, u32[]{:S(2)}, u32[]{:S(2)}) collective-permute-start(bf16[144,128]{1,0:T(8,128)(2,1)S(1)} %get-tuple-element.43), channel_id=1, source_target_pairs={{0,2},{1,3},{2,0},{3,1},{4,6},{5,7},{6,4},{7,5},{8,10},{9,11},{10,... | collective-permute-start | bytes 110600 | tf_op jit(solution)/shard_map/ppermute | solution.py:432
  136.7 3.4 %collective-permute-start.8 = (bf16[144,128]{1,0:T(8,128)(2,1)S(1)}, bf16[144,128]{1,0:T(8,128)(2,1)S(1)}, u32[]{:S(2)}, u32[]{:S(2)}) collective-permute-start(bf16[144,128]{1,0:T(8,128)(2,1)S(1)} %get-tuple-element.44), channel_id=1, source_target_pairs={{0,3},{1,0},{2,1},{3,2},{4,7},{5,4},{6,5},{7,6},{8,11},{9,8},{10,9... | collective-permute-start | bytes 110600 | tf_op jit(solution)/shard_map/ppermute | solution.py:432
  140.1 0.0 collective-permute-done.6.l1
  140.1 2.5 %collective-permute-done.8.l3 = bf16[144,128]{1,0:T(8,128)(2,1)S(1)} collective-permute-done((bf16[144,128]{1,0:T(8,128)(2,1)S(1)}, bf16[144,128]{1,0:T(8,128)(2,1)S(1)}, u32[]{:S(2)}, u32[]{:S(2)}) %collective-permute-start.8) | collective-permute-done | bytes 36896 | tf_op jit(solution)/shard_map/ppermute | solution.py:432
  142.6 1.0 all-to-all-done.4.branch_ref
  143.6 1.0 finish.1
  (24 shorter events, 0.1 us)
Async XLA Ops:
  6.5 1.6 %copy-start = (bf16[1,512,2048]{2,1,0:T(8,128)(2,1)S(1)}, bf16[1,512,2048]{2,1,0:T(8,128)(2,1)}, u32[]{:S(2)}) copy-start(bf16[1,512,2048]{2,1,0:T(8,128)(2,1)} %param.14) | copy-start | bytes 6291460
  8.1 0.8 copy-start.1
  8.9 0.8 copy-start.3
  9.6 0.7 copy-start.4
  10.3 0.7 copy-start.5
  13.1 4.5 %copy-start.2 = (bf16[128,128]{1,0:T(8,128)(2,1)S(1)}, bf16[128,128]{1,0:T(8,128)(2,1)}, u32[]{:S(2)}) copy-start(bf16[128,128]{1,0:T(8,128)(2,1)} %q_hbm.1) | copy-start | bytes 98308
  13.1 4.5 %copy-start.10 = (bf16[128,128]{1,0:T(8,128)(2,1)S(1)}, bf16[128,128]{1,0:T(8,128)(2,1)}, u32[]{:S(2)}) copy-start(bf16[128,128]{1,0:T(8,128)(2,1)} %param.10) | copy-start | bytes 98308
  13.1 31.2 %all-to-all-start = ((bf16[4,2080,128]{2,1,0:T(8,128)(2,1)}), bf16[4,2080,128]{2,1,0:T(8,128)(2,1)S(1)}, u32[]{:S(2)}, u32[]{:S(2)}) async-start(bf16[4,2080,128]{2,1,0:T(8,128)(2,1)} %get-tuple-element.27), calls=%async_computation | async-start | bytes 4259840 | tf_op jit(solution)/shard_map/all_to_all | solution.py:436
  17.6 100.8 %all-gather.2.cloned.1.call-start = ((), (), s32[]{:S(2)}) async-start(), calls=%async_computation.5 | async-start | bytes 1179648 | tf_op jit(solution)/shard_map/all_gather | solution.py:470
  17.7 12.7 %collective-permute-start = (bf16[256,128]{1,0:T(8,128)(2,1)S(1)}, bf16[256,128]{1,0:T(8,128)(2,1)S(1)}, u32[]{:S(2)}, u32[]{:S(2)}) collective-permute-start(bf16[256,128]{1,0:T(8,128)(2,1)S(1)} %constant_dynamic-update-slice_fusion.g0.l0), channel_id=1, source_target_pairs={{0,1},{1,2},{2,3},{3,0},{4,5},{5,6},{6,7},{7,4},{8,9},{9,10},{10,1... | collective-permute-start | bytes 196616 | tf_op jit(solution)/shard_map/ppermute | solution.py:432
  21.5 8.8 %collective-permute-start.1 = (bf16[256,128]{1,0:T(8,128)(2,1)S(1)}, bf16[256,128]{1,0:T(8,128)(2,1)S(1)}, u32[]{:S(2)}, u32[]{:S(2)}) collective-permute-start(bf16[256,128]{1,0:T(8,128)(2,1)S(1)} %constant_dynamic-update-slice_fusion.g0.l0), channel_id=1, source_target_pairs={{0,2},{1,3},{2,0},{3,1},{4,6},{5,7},{6,4},{7,5},{8,10},{9,11},{10,... | collective-permute-start | bytes 196616 | tf_op jit(solution)/shard_map/ppermute | solution.py:432
  26.7 6.2 %collective-permute-start.2 = (bf16[256,128]{1,0:T(8,128)(2,1)S(1)}, bf16[256,128]{1,0:T(8,128)(2,1)S(1)}, u32[]{:S(2)}, u32[]{:S(2)}) collective-permute-start(bf16[256,128]{1,0:T(8,128)(2,1)S(1)} %constant_dynamic-update-slice_fusion.g0.l0), channel_id=1, source_target_pairs={{0,3},{1,0},{2,1},{3,2},{4,7},{5,4},{6,5},{7,6},{8,11},{9,8},{10,9... | collective-permute-start | bytes 196616 | tf_op jit(solution)/shard_map/ppermute | solution.py:432
  32.8 60.6 %copy-start.11 = (s32[32]{0:T(128)S(1)}, s32[32]{0:T(128)}, u32[]{:S(2)}) copy-start(s32[32]{0:T(128)} %param.17) | copy-start | bytes 388
  35.1 0.8 copy-start.8
  35.9 0.8 copy-start.9
  76.5 41.8 %copy-start.6 = (s32[1,128]{1,0:T(1,128)S(1)}, s32[1,128]{1,0:T(1,128)}, u32[]{:S(2)}) copy-start(s32[1,128]{1,0:T(1,128)} %leaf_ref.1) | copy-start | bytes 1540
  76.5 17.0 %all-to-all-start.2 = ((bf16[32,32,128]{2,1,0:T(8,128)(2,1)}), bf16[32,32,128]{2,1,0:T(8,128)(2,1)S(1)}, u32[]{:S(2)}, u32[]{:S(2)}) async-start(bf16[32,32,128]{2,1,0:T(8,128)(2,1)} %bitcast.21), calls=%async_computation.2 | async-start | bytes 524288 | tf_op jit(solution)/shard_map/all_to_all | solution.py:436
  84.4 31.5 %collective-permute-start.3 = (bf16[2304,128]{1,0:T(8,128)(2,1)}, bf16[2304,128]{1,0:T(8,128)(2,1)}, u32[]{:S(2)}, u32[]{:S(2)}) collective-permute-start(bf16[2304,128]{1,0:T(8,128)(2,1)} %copy-done.9), channel_id=1, source_target_pairs={{0,4},{4,8},{8,12},{12,0},{1,5},{5,9},{9,13},{13,1},{2,6},{6,10},{... | collective-permute-start | bytes 1769480 | tf_op jit(solution)/shard_map/ppermute | solution.py:432
  86.9 29.0 %collective-permute-start.4 = (bf16[2304,128]{1,0:T(8,128)(2,1)}, bf16[2304,128]{1,0:T(8,128)(2,1)}, u32[]{:S(2)}, u32[]{:S(2)}) collective-permute-start(bf16[2304,128]{1,0:T(8,128)(2,1)} %copy-done.8), channel_id=1, source_target_pairs={{0,8},{4,12},{8,0},{12,4},{1,9},{5,13},{9,1},{13,5},{2,10},{6,14},... | collective-permute-start | bytes 1769480 | tf_op jit(solution)/shard_map/ppermute | solution.py:432
  90.9 27.5 %collective-permute-start.5 = (bf16[2304,128]{1,0:T(8,128)(2,1)S(1)}, bf16[2304,128]{1,0:T(8,128)(2,1)}, u32[]{:S(2)}, u32[]{:S(2)}) collective-permute-start(bf16[2304,128]{1,0:T(8,128)(2,1)S(1)} %get-tuple-element.35), channel_id=1, source_target_pairs={{0,12},{4,0},{8,4},{12,8},{1,13},{5,1},{9,5},{13,9},{2,14},{6,2},{... | collective-permute-start | bytes 1769480 | tf_op jit(solution)/shard_map/ppermute | solution.py:432
  97.2 27.1 %all-to-all-start.3 = ((bf16[32,48,128]{2,1,0:T(8,128)(2,1)}), bf16[32,48,128]{2,1,0:T(8,128)(2,1)S(1)}, u32[]{:S(2)}, u32[]{:S(2)}) async-start(bf16[32,48,128]{2,1,0:T(8,128)(2,1)} %branch_attend.1), calls=%async_computation.3 | async-start | bytes 786432 | tf_op jit(solution)/shard_map/all_to_all | solution.py:436
  118.4 1.2 copy-start.7
  125.7 17.8 %all-to-all-start.4 = ((bf16[4,80,128]{2,1,0:T(8,128)(2,1)}), bf16[4,80,128]{2,1,0:T(8,128)(2,1)S(1)}, u32[]{:S(2)}, u32[]{:S(2)}) async-start(bf16[4,80,128]{2,1,0:T(8,128)(2,1)} %merge_node.1), calls=%async_computation.4 | async-start | bytes 163840 | tf_op jit(solution)/shard_map/all_to_all | solution.py:436
  129.0 11.1 %collective-permute-start.6 = (bf16[144,128]{1,0:T(8,128)(2,1)S(1)}, bf16[144,128]{1,0:T(8,128)(2,1)S(1)}, u32[]{:S(2)}, u32[]{:S(2)}) collective-permute-start(bf16[144,128]{1,0:T(8,128)(2,1)S(1)} %get-tuple-element.42), channel_id=1, source_target_pairs={{0,1},{1,2},{2,3},{3,0},{4,5},{5,6},{6,7},{7,4},{8,9},{9,10},{10,1... | collective-permute-start | bytes 110600 | tf_op jit(solution)/shard_map/ppermute | solution.py:432
  132.4 7.7 %collective-permute-start.7 = (bf16[144,128]{1,0:T(8,128)(2,1)S(1)}, bf16[144,128]{1,0:T(8,128)(2,1)S(1)}, u32[]{:S(2)}, u32[]{:S(2)}) collective-permute-start(bf16[144,128]{1,0:T(8,128)(2,1)S(1)} %get-tuple-element.43), channel_id=1, source_target_pairs={{0,2},{1,3},{2,0},{3,1},{4,6},{5,7},{6,4},{7,5},{8,10},{9,11},{10,... | collective-permute-start | bytes 110600 | tf_op jit(solution)/shard_map/ppermute | solution.py:432
  136.7 5.9 %collective-permute-start.8 = (bf16[144,128]{1,0:T(8,128)(2,1)S(1)}, bf16[144,128]{1,0:T(8,128)(2,1)S(1)}, u32[]{:S(2)}, u32[]{:S(2)}) collective-permute-start(bf16[144,128]{1,0:T(8,128)(2,1)S(1)} %get-tuple-element.44), channel_id=1, source_target_pairs={{0,3},{1,0},{2,1},{3,2},{4,7},{5,4},{6,5},{7,6},{8,11},{9,8},{10,9... | collective-permute-start | bytes 110600 | tf_op jit(solution)/shard_map/ppermute | solution.py:432
Sparse Core Ops, SparseCore 0:
  75.9 22.8 all-gather.1

commit v3 on v1

--- a/solution.py
+++ b/solution.py
@@ -13,6 +13,9 @@
 F32 = jnp.float32
 NEG = -1e30
 FLOOR = -1e29
+COST_FLOPS = 15_000_000_000
+LOCAL_FLOPS = 30_000_000_000
+LENGTH_FLOPS = 6_000_000_000
 VMEM_LIMIT = 50 * 1024 * 1024
 
 
@@ -25,14 +28,36 @@
 
 
 SMEM = pl.BlockSpec(memory_space=pltpu.SMEM)
-ANY = pl.BlockSpec(memory_space=pl.ANY)
+HBM = pl.BlockSpec(memory_space=pltpu.HBM)
+
+
+def in_hbm(value):
+    return pltpu.with_memory_space_constraint(value, pltpu.HBM)
 
 
 def params():
     return pltpu.CompilerParams(vmem_limit_bytes=VMEM_LIMIT)
 
 
-def slot_kernel(parent, leaf_ref, q_ref, root_ref, out_ref, slot_ref):
+def first_kernel(
+    parent, leaf_hbm, q_hbm, root_hbm, suffix_hbm, out_ref, slot_ref, split_ref,
+    leaf_ref, q_ref, root_ref, suffix_ref, sems,
+):
+    copies = [
+        pltpu.make_async_copy(source, target, sems.at[i])
+        for i, (source, target) in enumerate(
+            ((root_hbm, root_ref), (leaf_hbm, leaf_ref), (q_hbm, q_ref), (suffix_hbm, suffix_ref))
+        )
+    ]
+    for copy in copies:
+        copy.start()
+    for copy in copies:
+        copy.wait()
+    root = root_ref[...].astype(F32)
+    for target in range(4):
+        lanes = [kv * 1024 + target * 256 + half * 128 for kv in range(2) for half in range(2)]
+        split_ref[target, 32:160] = suffix_ref[...]
+        split_ref[target, 0:32] = jnp.concatenate([root[:, l : l + 128] for l in lanes], axis=0).astype(BF)
     leaf = leaf_ref[...]
     across = jnp.broadcast_to(leaf.astype(F32), (128, 128))
     down = across.T
@@ -45,66 +70,114 @@
     slot_ref[...] = slot
     pick = jnp.where(iota((256, 128), 0) == slot, 1.0, 0.0).astype(BF)
     routed = jnp.dot(pick, q_ref[...], preferred_element_type=F32).astype(BF)
-    root = root_ref[...].astype(F32)
-    blocks = jnp.concatenate([root[:, j * 128 : (j + 1) * 128] for j in range(16)], axis=0).astype(BF)
-    for z in range(4):
-        out_ref[z, 0:64] = routed[z * 64 : (z + 1) * 64]
-        out_ref[z, 64:192] = blocks
-
-
-def route_slots(parent, leaf, queries, root):
-    return pl.pallas_call(
-        slot_kernel,
+    out_ref[...] = routed.reshape(4, 64, 128)
+
+
+def first_stage(parent, leaf, queries, root, suffix):
+    return pl.pallas_call(
+        first_kernel,
         out_shape=(
-            jax.ShapeDtypeStruct((4, 192, 128), BF),
+            jax.ShapeDtypeStruct((4, 64, 128), BF),
             jax.ShapeDtypeStruct((1, 128), jnp.int32),
+            jax.ShapeDtypeStruct((4, 160, 128), BF),
         ),
-        in_specs=[SMEM, whole((1, 128)), whole((128, 128)), whole((8, 2048))],
-        out_specs=(whole((4, 192, 128)), whole((1, 128))),
-        compiler_params=params(),
-        name="route_slots",
-    )(parent, leaf, queries, root)
-
-
-def pack_cache(where, cache, extra):
-    rows = 2048 + (128 if extra is not None else 0)
-
-    def kernel(where_ref, *refs):
-        cache_ref = refs[0]
-        outs = refs[-4:-1]
-        sems = refs[-1]
-        copies = []
-        for s in range(3):
-            target = (where_ref[0] + (s + 1)) & 3
+        in_specs=[SMEM, HBM, HBM, HBM, HBM],
+        out_specs=(whole((4, 64, 128)), whole((1, 128)), whole((4, 160, 128))),
+        scratch_shapes=[
+            pltpu.VMEM((1, 128), jnp.int32),
+            pltpu.VMEM((128, 128), BF),
+            pltpu.VMEM((8, 2048), BF),
+            pltpu.VMEM((128, 128), BF),
+            pltpu.SemaphoreType.DMA((4,)),
+        ],
+        compiler_params=params(),
+        name="first_stage",
+    )(parent, in_hbm(leaf), in_hbm(queries), in_hbm(root), in_hbm(suffix))
+
+
+def pack_kernel(info, branch, leaf, sent1, sent2, sent3, branch_buf, leaf_buf, loads, stores):
+    pairs = ((branch, branch_buf), (leaf, leaf_buf))
+    fetches = [
+        pltpu.make_async_copy(cache, buf, loads.at[i]) for i, (cache, buf) in enumerate(pairs)
+    ]
+    for fetch in fetches:
+        fetch.start()
+    moves = []
+    for i, (_, buf) in enumerate(pairs):
+        fetches[i].wait()
+        for s, sent in enumerate((sent1, sent2, sent3)):
+            target = (info[0] + (s + 1)) & 3
             for part in range(4):
                 start = (part // 2) * 1024 + (part % 2) * 128
                 lane = pl.multiple_of(target * 256 + start, 128)
-                copies.append(
+                moves.append(
                     pltpu.make_async_copy(
-                        cache_ref.at[:, pl.ds(lane, 128)],
-                        outs[s].at[pl.ds(part * 512, 512), :],
-                        sems.at[s, part],
+                        buf.at[:, pl.ds(lane, 128)],
+                        sent.at[pl.ds(i * 2048 + part * 512, 512), :],
+                        stores.at[i, s, part],
                     )
                 )
-            if extra is not None:
-                copies.append(
-                    pltpu.make_async_copy(refs[1], outs[s].at[pl.ds(2048, 128), :], sems.at[s, 4])
-                )
-        for copy in copies:
-            copy.start()
-        for copy in copies:
-            copy.wait()
-
-    operands = (where, cache) + ((extra,) if extra is not None else ())
-    return pl.pallas_call(
-        kernel,
-        out_shape=tuple(jax.ShapeDtypeStruct((rows, 128), BF) for _ in range(3)),
-        in_specs=[SMEM] + [ANY] * (len(operands) - 1),
-        out_specs=(ANY, ANY, ANY),
-        scratch_shapes=[pltpu.SemaphoreType.DMA((3, 5))],
-        compiler_params=params(),
-        name="pack_cache",
-    )(*operands)
+                moves[-1].start()
+    for move in moves:
+        move.wait()
+
+
+def pack_caches(info, branch, leaf):
+    return pl.pallas_call(
+        pack_kernel,
+        out_shape=tuple(jax.ShapeDtypeStruct((4096, 128), BF) for _ in range(3)),
+        in_specs=[SMEM, HBM, HBM],
+        out_specs=(HBM, HBM, HBM),
+        scratch_shapes=[
+            pltpu.VMEM((512, 2048), BF),
+            pltpu.VMEM((512, 2048), BF),
+            pltpu.SemaphoreType.DMA((2,)),
+            pltpu.SemaphoreType.DMA((2, 3, 4)),
+        ],
+        compiler_params=params(),
+        name="pack_caches",
+    )(info, in_hbm(branch), in_hbm(leaf))
+
+
+def lengths_kernel(lengths, out):
+    leaf = iota((1, 512), 1) >> 4
+    row = jnp.zeros((1, 512), jnp.int32)
+    for i in range(32):
+        row = jnp.where(leaf == i, lengths[i], row)
+    out[...] = row
+
+
+def key_lengths(lengths):
+    return pl.pallas_call(
+        lengths_kernel,
+        out_shape=jax.ShapeDtypeStruct((1, 512), jnp.int32),
+        in_specs=[SMEM],
+        out_specs=whole((1, 512)),
+        compiler_params=params(),
+        cost_estimate=pl.CostEstimate(
+            flops=LENGTH_FLOPS, transcendentals=1_000_000, bytes_accessed=8_000_000
+        ),
+        name="key_lengths",
+    )(lengths)
+
+
+def arrive_kernel(info, p1, p2, p3, out):
+    for i in range(3):
+        out[i] = info[i]
+
+
+def arrive(info, pieces):
+    return pl.pallas_call(
+        arrive_kernel,
+        out_shape=jax.ShapeDtypeStruct((3,), jnp.int32),
+        in_specs=[SMEM, HBM, HBM, HBM],
+        out_specs=SMEM,
+        compiler_params=params(),
+        cost_estimate=pl.CostEstimate(
+            flops=COST_FLOPS, transcendentals=1_000_000, bytes_accessed=8_000_000
+        ),
+        name="arrive",
+    )(info, *pieces)
 
 
 def softmax_parts(scores, values):
@@ -159,8 +232,7 @@
         queries = jnp.concatenate([blocks[2 * h], blocks[2 * h + 1]], axis=1)
         scores = []
         for s in range(4):
-            source = (y - s) & 3
-            place = (source * 4 + zl) * 512 + iota((256, 512), 1)
+            place = (((y - s) & 3) * 4 + zl) * 512 + iota((256, 512), 1)
             scores.append(jnp.where(place < length, score(queries, keys[s]), NEG))
         highest, total, summed = softmax_parts(scores, values)
         first = jnp.where(row16 < 16, 0, 64)
@@ -179,14 +251,13 @@
     head = pl.BlockSpec((512, 256), lambda i, info: (0, info[0]))
     head_value = pl.BlockSpec((512, 256), lambda i, info: (0, 4 + info[0]))
     full = lambda shape: pl.BlockSpec(shape, lambda i, info: (0,) * len(shape))
-    rows = pieces[0].shape[0]
     return pl.pallas_call(
         branch_kernel,
         out_shape=jax.ShapeDtypeStruct((32, 48, 128), BF),
         grid_spec=pltpu.PrefetchScalarGridSpec(
             num_scalar_prefetch=1,
             grid=(1,),
-            in_specs=[full((32, 32, 128)), head, head_value] + [full((rows, 128))] * 3,
+            in_specs=[full((32, 32, 128)), head, head_value] + [pl.BlockSpec((2048, 128), lambda i, info: (0, 0))] * 3,
             out_specs=full((32, 48, 128)),
         ),
         compiler_params=params(),
@@ -295,15 +366,18 @@
             num_scalar_prefetch=1,
             grid=(1,),
             in_specs=[full((1, 128)), full((1, 512)), head, head_value]
-            + [full((2048, 128))] * 3
+            + [pl.BlockSpec((2048, 128), lambda i, info: (1, 0))] * 3
             + [full((8, 512, 128))]
             + [full((384, 128))] * 4,
             out_specs=tuple(full((144, 128)) for _ in range(4)),
             scratch_shapes=[pltpu.VMEM((4, 384, 128), BF), pltpu.VMEM((4, 144, 128), BF)],
         ),
         compiler_params=params(),
+        cost_estimate=pl.CostEstimate(
+            flops=LOCAL_FLOPS, transcendentals=1_000_000, bytes_accessed=8_000_000
+        ),
         name="local_attend",
-    )(info, leaf, lengths, cache, cache, *pieces, root, *gathered)
+    )(info, leaf, lengths, cache, cache, *pieces, in_hbm(root), *gathered)
 
 
 def final_kernel(slot_ref, branch_ref, l0, l1, l2, l3, out_ref):
@@ -380,44 +454,38 @@
     branch_rows = branch_cache.reshape(512, 2048)
     leaf_rows = leaf_cache.reshape(512, 2048)
 
-    routed, slot = route_slots(leaf_parent, suffix_leaf, queries, root_cache)
-    arrived = exchange(routed, "zh")
-
-    branch_out = pack_cache(info, branch_rows, suffix_cache)
-    branch_in = [shift(branch_out[s], "y", s + 1) for s in range(3)]
-    leaf_out = pack_cache(info, leaf_rows, None)
-    leaf_in = [shift(leaf_out[s], "y", s + 1) for s in range(3)]
+    tie = lax.optimization_barrier
+    routed, slot, split = first_stage(
+        leaf_parent, suffix_leaf, queries, root_cache, suffix_cache
+    )
+    own = exchange(split, "y")
+    sent = pack_caches(info, branch_rows, leaf_rows)
+    pieces = [shift(sent[s], "y", s + 1) for s in range(3)]
+    onward = jnp.concatenate(
+        [routed, jnp.broadcast_to(own[:, 0:32].reshape(1, 128, 128), (4, 128, 128))], axis=1
+    )
+    arrived = exchange(onward, "zh")
+    def chosen(source):
+        return lax.dynamic_index_in_dim(own, source, 0, keepdims=False)[32:160]
+
+    mine = jnp.concatenate([queries, chosen(y >> 1), chosen(2 + (y >> 1))], axis=0)
+    gathered = [mine] + [shift(mine, "zl", s + 1) for s in range(3)]
+    arrived, lengths, gathered[1], gathered[2] = tie((arrived, key_lengths(leaf_length), gathered[1], gathered[2]))
 
     onward = arrived[:, 0:64].reshape(4, 8, 8, 128).transpose(1, 0, 2, 3).reshape(8, 1, 32, 128)
     onward = jnp.broadcast_to(onward, (8, 4, 32, 128)).reshape(32, 32, 128)
+    root = arrived[:, 64:192].reshape(4, 4, 4, 8, 128).transpose(1, 2, 0, 3, 4)
+    onward, root = tie((onward, root.reshape(512, 128)))
+    root_all = lax.all_gather(root, XC, axis=0, tiled=False)
     node_queries = exchange(onward, XCZ)
 
-    root = arrived[:, 64:192].reshape(4, 2, 4, 2, 8, 128).transpose(2, 1, 3, 0, 4, 5)
-    root = root.reshape(4, 4 * 32, 128)
-    root_parts = [lax.dynamic_index_in_dim(root, y, 0, keepdims=False)]
-    for s in range(3):
-        part = lax.dynamic_index_in_dim(root, (y + (s + 1)) & 3, 0, keepdims=False)
-        root_parts.append(shift(part, "y", s + 1))
-    root_all = lax.all_gather(jnp.concatenate(root_parts, axis=0), XC, axis=0, tiled=False)
-
-    partials = branch_attend(info, node_queries, branch_rows, branch_in)
-
-    blocks = [suffix_cache] + [part[2048:2176] for part in branch_in]
-
-    def chosen(source):
-        step = (y - source) & 3
-        return lax.select_n(step, *blocks)
-
-    mine = jnp.concatenate([queries, chosen(y // 2), chosen(2 + y // 2)], axis=0)
-    gathered = [mine] + [shift(mine, "zl", s + 1) for s in range(3)]
-
+    partials = branch_attend(arrive(info, pieces), node_queries, branch_rows, pieces)
     returned = exchange(partials, XCZ)
     merged = merge_node(returned)
+    local = local_attend(info, suffix_leaf, lengths, leaf_rows, pieces, root_all, gathered)
+    merged, own_part = tie((merged, local[0]))
     back = exchange(merged, "zh")
-
-    lengths = jnp.repeat(leaf_length, 16).reshape(1, 512)
-    local = local_attend(info, suffix_leaf, lengths, leaf_rows, leaf_in, root_all, gathered)
-    parts = [local[0]] + [shift(local[s + 1], "zl", s + 1) for s in range(3)]
+    parts = [own_part] + [shift(local[s + 1], "zl", s + 1) for s in range(3)]
     return finish(slot, back, parts)
 
 

time: 176 us -> 142 us (0.81)
  the two profiles are of different devices: /device:TPU:6 before, /device:TPU:1 now
where the time goes in v3:
time: 142 us; the launch traced here: 141 us
  starting transfers between devices  68.7 us (48%)
  waiting for transfers between devices  27.7 us (20%)
  Pallas kernels  19.7 us (14%)
  between operations  14.3 us (10%)
  local copies, waits for them, and re-layouts  9.18 us (6%)
  other arithmetic  1.42 us (1%)
    all_to_all x5, starting transfers between devices, exchange(): return lax.all_to_all(values, axis, split_axis=0, concat_axis=0, tiled=True)  40.3 us
    ppermute x9, starting transfers between devices, shift(): return lax.ppermute(values, axis, [(i, (i + step) % 4) for i in range(4)])  28.3 us
    all_to_all x5, waiting for transfers between devices, exchange(): return lax.all_to_all(values, axis, split_axis=0, concat_axis=0, tiled=True)  16.2 us
    ppermute x9, waiting for transfers between devices, shift(): return lax.ppermute(values, axis, [(i, (i + step) % 4) for i in range(4)])  11.4 us
    unnamed x28, local copies, waits for them, and re-layouts  6.91 us
    pallas_call x1, Pallas kernels, branch_attend(): pl.pallas_call(branch_kernel, out_shape=jax.ShapeDtypeStruct((32, 48, 128...  4.66 us
    pallas_call x1, Pallas kernels, local_attend(): pl.pallas_call(local_kernel, out_shape=tuple((jax.ShapeDtypeStruct((144,...  4.59 us
    pallas_call x1, Pallas kernels, pack_caches(): pl.pallas_call(pack_kernel, out_shape=tuple((jax.ShapeDtypeStruct((4096,...  4.17 us
  transfers between devices with their start and end apart: 15, of which 6 were waited for; matrix products, arithmetic and copies ran while one was open for 3% of the time, Pallas kernels for 11%

profile of v3, /device:TPU:1, one launch (start us, length us, event | category | flops | bytes accessed | tf_op | source)
XLA Modules:
  0.0 140.9 jit_solution(15575966781157885493)
XLA Ops:
  6.5 0.7 copy-done.2
  7.2 2.2 %first_stage.1 = (bf16[4,64,128]{2,1,0:T(8,128)(2,1)S(1)}, s32[1,128]{1,0:T(1,128)S(1)}, bf16[4,160,128]{2,1,0:T(8,128)(2,1)}) custom-call(s32[1,32]{1,0:T(1,128)S(1)} %copy-done.2, s32[1,128]{1,0:T(1,128)} %leaf_ref.1, bf16[128,128]{1,0:T(8,128)(2,1)} %q_hbm.1, bf16[8,2048]{1,0:T(8,128)(2,1)} %root_hbm.1, bf16[128,128]{1,0:T(8,128)(2,1)} %suffix_hbm.1), custom_call_target="tpu_custom_call" | custom-call | tf_op jit(solution)/shard_map/first_stage/pallas_call | solution.py:77
  9.4 5.0 %all-to-all-start = ((bf16[4,160,128]{2,1,0:T(8,128)(2,1)}), bf16[4,160,128]{2,1,0:T(8,128)(2,1)S(1)}, u32[]{:S(2)}, u32[]{:S(2)}) async-start(bf16[4,160,128]{2,1,0:T(8,128)(2,1)} %get-tuple-element.28), calls=%async_computation | async-start | bytes 327680 | tf_op jit(solution)/shard_map/all_to_all | solution.py:444
  15.0 0.1 pad_add_fusion.info
  15.1 4.2 %pack_caches.1 = (bf16[4096,128]{1,0:T(8,128)(2,1)}, bf16[4096,128]{1,0:T(8,128)(2,1)}, bf16[4096,128]{1,0:T(8,128)(2,1)}) custom-call(s32[3]{0:T(128)S(1)} %pad_add_fusion.info, bf16[512,2048]{1,0:T(8,128)(2,1)} %bitcast.22, bf16[512,2048]{1,0:T(8,128)(2,1)} %bitcast.25), custom_call_target="tpu_custom_call" | custom-call | tf_op jit(solution)/shard_map/pack_caches/pallas_call | solution.py:126
  19.3 3.4 %collective-permute-start = (bf16[4096,128]{1,0:T(8,128)(2,1)}, bf16[4096,128]{1,0:T(8,128)(2,1)S(1)}, u32[]{:S(2)}, u32[]{:S(2)}) collective-permute-start(bf16[4096,128]{1,0:T(8,128)(2,1)} %get-tuple-element.24), channel_id=1, source_target_pairs={{0,4},{4,8},{8,12},{12,0},{1,5},{5,9},{9,13},{13,1},{2,6},{6,10},{... | collective-permute-start | bytes 3145736 | tf_op jit(solution)/shard_map/ppermute | solution.py:440
  22.7 4.3 %collective-permute-start.1 = (bf16[4096,128]{1,0:T(8,128)(2,1)}, bf16[4096,128]{1,0:T(8,128)(2,1)S(1)}, u32[]{:S(2)}, u32[]{:S(2)}) collective-permute-start(bf16[4096,128]{1,0:T(8,128)(2,1)} %get-tuple-element.25), channel_id=1, source_target_pairs={{0,8},{4,12},{8,0},{12,4},{1,9},{5,13},{9,1},{13,5},{2,10},{6,14},... | collective-permute-start | bytes 3145736 | tf_op jit(solution)/shard_map/ppermute | solution.py:440
  27.0 3.1 %collective-permute-start.2 = (bf16[4096,128]{1,0:T(8,128)(2,1)}, bf16[4096,128]{1,0:T(8,128)(2,1)S(1)}, u32[]{:S(2)}, u32[]{:S(2)}) collective-permute-start(bf16[4096,128]{1,0:T(8,128)(2,1)} %get-tuple-element.26), channel_id=1, source_target_pairs={{0,12},{4,0},{8,4},{12,8},{1,13},{5,1},{9,5},{13,9},{2,14},{6,2},{... | collective-permute-start | bytes 3145736 | tf_op jit(solution)/shard_map/ppermute | solution.py:440
  30.1 0.0 all-to-all-done
  30.1 0.7 pad_maximum_fusion
  30.8 14.8 %all-to-all-start.1 = ((bf16[4,192,128]{2,1,0:T(8,128)(2,1)}), bf16[4,192,128]{2,1,0:T(8,128)(2,1)S(1)}, u32[]{:S(2)}, u32[]{:S(2)}) async-start(bf16[4,192,128]{2,1,0:T(8,128)(2,1)} %pad_maximum_fusion), calls=%async_computation.1 | async-start | bytes 393216 | tf_op jit(solution)/shard_map/all_to_all | solution.py:444
  45.6 0.8 dynamic-slice_bitcast_fusion.1
  46.4 0.6 pad_maximum_fusion.1.l0
  47.1 2.6 %collective-permute-start.3 = (bf16[384,128]{1,0:T(8,128)(2,1)}, bf16[384,128]{1,0:T(8,128)(2,1)S(1)}, u32[]{:S(2)}, u32[]{:S(2)}) collective-permute-start(bf16[384,128]{1,0:T(8,128)(2,1)} %pad_maximum_fusion.1.l0), channel_id=1, source_target_pairs={{0,1},{1,2},{2,3},{3,0},{4,5},{5,6},{6,7},{7,4},{8,9},{9,10},{10,1... | collective-permute-start | bytes 294920 | tf_op jit(solution)/shard_map/ppermute | solution.py:440
  49.7 3.1 %collective-permute-start.4 = (bf16[384,128]{1,0:T(8,128)(2,1)}, bf16[384,128]{1,0:T(8,128)(2,1)S(1)}, u32[]{:S(2)}, u32[]{:S(2)}) collective-permute-start(bf16[384,128]{1,0:T(8,128)(2,1)} %pad_maximum_fusion.1.l0), channel_id=1, source_target_pairs={{0,2},{1,3},{2,0},{3,1},{4,6},{5,7},{6,4},{7,5},{8,10},{9,11},{10,... | collective-permute-start | bytes 294920 | tf_op jit(solution)/shard_map/ppermute | solution.py:440
  52.8 0.6 key_lengths.1.lengths_ref
  53.4 5.4 %collective-permute-done.3.l1 = bf16[384,128]{1,0:T(8,128)(2,1)S(1)} collective-permute-done((bf16[384,128]{1,0:T(8,128)(2,1)}, bf16[384,128]{1,0:T(8,128)(2,1)S(1)}, u32[]{:S(2)}, u32[]{:S(2)}) %collective-permute-start.3) | collective-permute-done | bytes 98336 | tf_op jit(solution)/shard_map/ppermute | solution.py:440
  58.9 0.6 copy-done.4
  59.5 3.9 %collective-permute-done.4.l2 = bf16[384,128]{1,0:T(8,128)(2,1)S(1)} collective-permute-done((bf16[384,128]{1,0:T(8,128)(2,1)}, bf16[384,128]{1,0:T(8,128)(2,1)S(1)}, u32[]{:S(2)}, u32[]{:S(2)}) %collective-permute-start.4) | collective-permute-done | bytes 98336 | tf_op jit(solution)/shard_map/ppermute | solution.py:440
  63.4 0.6 copy-done.6
  64.0 0.7 copy.11
  64.7 0.8 broadcast_in_dim.17
  65.5 0.0 all-gather.3.cloned.1.call-update
  65.5 2.8 %collective-permute-start.5 = (bf16[384,128]{1,0:T(8,128)(2,1)}, bf16[384,128]{1,0:T(8,128)(2,1)}, u32[]{:S(2)}, u32[]{:S(2)}) collective-permute-start(bf16[384,128]{1,0:T(8,128)(2,1)} %pad_maximum_fusion.1.l0), channel_id=1, source_target_pairs={{0,3},{1,0},{2,1},{3,2},{4,7},{5,4},{6,5},{7,6},{8,11},{9,8},{10,9... | collective-permute-start | bytes 294920 | tf_op jit(solution)/shard_map/ppermute | solution.py:440
  68.3 8.4 %all-to-all-start.2 = ((bf16[32,32,128]{2,1,0:T(8,128)(2,1)}), bf16[32,32,128]{2,1,0:T(8,128)(2,1)S(1)}, u32[]{:S(2)}, u32[]{:S(2)}) async-start(bf16[32,32,128]{2,1,0:T(8,128)(2,1)} %bitcast.28), calls=%async_computation.2 | async-start | bytes 524288 | tf_op jit(solution)/shard_map/all_to_all | solution.py:444
  76.8 1.1 arrive.1.info
  77.9 0.0 copy-start.3
  77.9 9.9 %all-to-all-done.2.q_ref = bf16[32,32,128]{2,1,0:T(8,128)(2,1)S(1)} async-done(((bf16[32,32,128]{2,1,0:T(8,128)(2,1)}), bf16[32,32,128]{2,1,0:T(8,128)(2,1)S(1)}, u32[]{:S(2)}, u32[]{:S(2)}) %all-to-all-start.2) | async-done | bytes 262176 | tf_op jit(solution)/shard_map/all_to_all | solution.py:444
  87.8 4.7 %branch_attend.1 = bf16[32,48,128]{2,1,0:T(8,128)(2,1)} custom-call(s32[3]{0:T(128)S(1)} %arrive.1.info, bf16[32,32,128]{2,1,0:T(8,128)(2,1)S(1)} %all-to-all-done.2.q_ref, bf16[512,2048]{1,0:T(8,128)(2,1)} %bitcast.23, bf16[512,2048]{1,0:T(8,128)(2,1)} %bitcast.24, bf16[4096,128]{1,0:T(8,128)(2,1)S(1)} %collective-permute-done.p1, ...), custom_call_target="tpu_custom_call" | custom-call | tf_op jit(solution)/shard_map/branch_attend/pallas_call | solution.py:254
  92.5 4.4 %all-to-all-start.3 = ((bf16[32,48,128]{2,1,0:T(8,128)(2,1)}), bf16[32,48,128]{2,1,0:T(8,128)(2,1)S(1)}, u32[]{:S(2)}, u32[]{:S(2)}) async-start(bf16[32,48,128]{2,1,0:T(8,128)(2,1)} %branch_attend.1), calls=%async_computation.3 | async-start | bytes 786432 | tf_op jit(solution)/shard_map/all_to_all | solution.py:444
  96.9 0.0 all-gather.3.cloned.1.call-done
  97.0 0.9 copy-done.5
  97.9 0.9 copy-done.7
  98.7 4.6 %local_attend.1 = (bf16[144,128]{1,0:T(8,128)(2,1)S(1)}, bf16[144,128]{1,0:T(8,128)(2,1)S(1)}, bf16[144,128]{1,0:T(8,128)(2,1)S(1)}, bf16[144,128]{1,0:T(8,128)(2,1)S(1)}) custom-call(s32[3]{0:T(128)S(1)} %pad_add_fusion.info, s32[1,128]{1,0:T(1,128)S(1)} %copy-done.3, s32[1,512]{1,0:T(1,128)S(1)} %key_lengths.1.lengths_ref, bf16[512,2048]{1,0:T(8,128)(2,1)} %bitcast.26, ...), custom_call_target="tpu_custom_call" | custom-call | flops 30000001024 | bytes 8000000 | tf_op jit(solution)/shard_map/local_attend/pallas_call | solution.py:362
  103.3 0.6 copy-done
  104.0 0.6 copy-done.8
  104.6 0.6 copy-done.9
  105.2 0.6 copy-done.10
  105.8 4.9 %all-to-all-done.3.in_ref = bf16[32,48,128]{2,1,0:T(8,128)(2,1)S(1)} async-done(((bf16[32,48,128]{2,1,0:T(8,128)(2,1)}), bf16[32,48,128]{2,1,0:T(8,128)(2,1)S(1)}, u32[]{:S(2)}, u32[]{:S(2)}) %all-to-all-start.3) | async-done | bytes 393248 | tf_op jit(solution)/shard_map/all_to_all | solution.py:444
  110.7 1.4 merge_node.1
  112.1 7.7 %all-to-all-start.4 = ((bf16[4,80,128]{2,1,0:T(8,128)(2,1)}), bf16[4,80,128]{2,1,0:T(8,128)(2,1)S(1)}, u32[]{:S(2)}, u32[]{:S(2)}) async-start(bf16[4,80,128]{2,1,0:T(8,128)(2,1)} %merge_node.1), calls=%async_computation.4 | async-start | bytes 163840 | tf_op jit(solution)/shard_map/all_to_all | solution.py:444
  119.8 1.9 %collective-permute-start.6 = (bf16[144,128]{1,0:T(8,128)(2,1)}, bf16[144,128]{1,0:T(8,128)(2,1)S(1)}, u32[]{:S(2)}, u32[]{:S(2)}) collective-permute-start(bf16[144,128]{1,0:T(8,128)(2,1)} %copy-done.10), channel_id=1, source_target_pairs={{0,1},{1,2},{2,3},{3,0},{4,5},{5,6},{6,7},{7,4},{8,9},{9,10},{10,1... | collective-permute-start | bytes 110600 | tf_op jit(solution)/shard_map/ppermute | solution.py:440
  121.7 2.7 %collective-permute-start.7 = (bf16[144,128]{1,0:T(8,128)(2,1)}, bf16[144,128]{1,0:T(8,128)(2,1)S(1)}, u32[]{:S(2)}, u32[]{:S(2)}) collective-permute-start(bf16[144,128]{1,0:T(8,128)(2,1)} %copy-done.9), channel_id=1, source_target_pairs={{0,2},{1,3},{2,0},{3,1},{4,6},{5,7},{6,4},{7,5},{8,10},{9,11},{10,... | collective-permute-start | bytes 110600 | tf_op jit(solution)/shard_map/ppermute | solution.py:440
  124.4 4.3 %collective-permute-start.8 = (bf16[144,128]{1,0:T(8,128)(2,1)}, bf16[144,128]{1,0:T(8,128)(2,1)S(1)}, u32[]{:S(2)}, u32[]{:S(2)}) collective-permute-start(bf16[144,128]{1,0:T(8,128)(2,1)} %copy-done.8), channel_id=1, source_target_pairs={{0,3},{1,0},{2,1},{3,2},{4,7},{5,4},{6,5},{7,6},{8,11},{9,8},{10,9... | collective-permute-start | bytes 110600 | tf_op jit(solution)/shard_map/ppermute | solution.py:440
  128.8 2.1 %collective-permute-done.8.l3 = bf16[144,128]{1,0:T(8,128)(2,1)S(1)} collective-permute-done((bf16[144,128]{1,0:T(8,128)(2,1)}, bf16[144,128]{1,0:T(8,128)(2,1)S(1)}, u32[]{:S(2)}, u32[]{:S(2)}) %collective-permute-start.8) | collective-permute-done | bytes 36896 | tf_op jit(solution)/shard_map/ppermute | solution.py:440
  130.9 1.4 all-to-all-done.4.branch_ref
  132.3 0.8 copy-done.1
  133.1 1.0 finish.1
  (29 shorter events, 0.1 us)
Async XLA Ops:
  6.5 0.7 copy-start.2
  9.4 20.7 %all-to-all-start = ((bf16[4,160,128]{2,1,0:T(8,128)(2,1)}), bf16[4,160,128]{2,1,0:T(8,128)(2,1)S(1)}, u32[]{:S(2)}, u32[]{:S(2)}) async-start(bf16[4,160,128]{2,1,0:T(8,128)(2,1)} %get-tuple-element.28), calls=%async_computation | async-start | bytes 327680 | tf_op jit(solution)/shard_map/all_to_all | solution.py:444
  15.1 31.3 %copy-start.13 = (bf16[128,128]{1,0:T(8,128)(2,1)S(1)}, bf16[128,128]{1,0:T(8,128)(2,1)}, u32[]{:S(2)}) copy-start(bf16[128,128]{1,0:T(8,128)(2,1)} %q_hbm.1) | copy-start | bytes 98308
  15.1 37.7 %copy-start.11 = (s32[32]{0:T(128)S(1)}, s32[32]{0:T(128)}, u32[]{:S(2)}) copy-start(s32[32]{0:T(128)} %lengths.1) | copy-start | bytes 388
  19.3 57.4 %collective-permute-start = (bf16[4096,128]{1,0:T(8,128)(2,1)}, bf16[4096,128]{1,0:T(8,128)(2,1)S(1)}, u32[]{:S(2)}, u32[]{:S(2)}) collective-permute-start(bf16[4096,128]{1,0:T(8,128)(2,1)} %get-tuple-element.24), channel_id=1, source_target_pairs={{0,4},{4,8},{8,12},{12,0},{1,5},{5,9},{9,13},{13,1},{2,6},{6,10},{... | collective-permute-start | bytes 3145736 | tf_op jit(solution)/shard_map/ppermute | solution.py:440
  22.7 54.1 %collective-permute-start.1 = (bf16[4096,128]{1,0:T(8,128)(2,1)}, bf16[4096,128]{1,0:T(8,128)(2,1)S(1)}, u32[]{:S(2)}, u32[]{:S(2)}) collective-permute-start(bf16[4096,128]{1,0:T(8,128)(2,1)} %get-tuple-element.25), channel_id=1, source_target_pairs={{0,8},{4,12},{8,0},{12,4},{1,9},{5,13},{9,1},{13,5},{2,10},{6,14},... | collective-permute-start | bytes 3145736 | tf_op jit(solution)/shard_map/ppermute | solution.py:440
  27.0 49.8 %collective-permute-start.2 = (bf16[4096,128]{1,0:T(8,128)(2,1)}, bf16[4096,128]{1,0:T(8,128)(2,1)S(1)}, u32[]{:S(2)}, u32[]{:S(2)}) collective-permute-start(bf16[4096,128]{1,0:T(8,128)(2,1)} %get-tuple-element.26), channel_id=1, source_target_pairs={{0,12},{4,0},{8,4},{12,8},{1,13},{5,1},{9,5},{13,9},{2,14},{6,2},{... | collective-permute-start | bytes 3145736 | tf_op jit(solution)/shard_map/ppermute | solution.py:440
  30.1 0.7 copy-start.12
  30.8 33.2 %all-to-all-start.1 = ((bf16[4,192,128]{2,1,0:T(8,128)(2,1)}), bf16[4,192,128]{2,1,0:T(8,128)(2,1)S(1)}, u32[]{:S(2)}, u32[]{:S(2)}) async-start(bf16[4,192,128]{2,1,0:T(8,128)(2,1)} %pad_maximum_fusion), calls=%async_computation.1 | async-start | bytes 393216 | tf_op jit(solution)/shard_map/all_to_all | solution.py:444
  45.6 51.3 %all-gather.3.cloned.1.call-start = ((), (), s32[]{:S(2)}) async-start(), calls=%async_computation.5 | async-start | bytes 1179648 | tf_op jit(solution)/shard_map/all_gather | solution.py:479
  47.1 11.8 %collective-permute-start.3 = (bf16[384,128]{1,0:T(8,128)(2,1)}, bf16[384,128]{1,0:T(8,128)(2,1)S(1)}, u32[]{:S(2)}, u32[]{:S(2)}) collective-permute-start(bf16[384,128]{1,0:T(8,128)(2,1)} %pad_maximum_fusion.1.l0), channel_id=1, source_target_pairs={{0,1},{1,2},{2,3},{3,0},{4,5},{5,6},{6,7},{7,4},{8,9},{9,10},{10,1... | collective-permute-start | bytes 294920 | tf_op jit(solution)/shard_map/ppermute | solution.py:440
  49.7 13.6 %collective-permute-start.4 = (bf16[384,128]{1,0:T(8,128)(2,1)}, bf16[384,128]{1,0:T(8,128)(2,1)S(1)}, u32[]{:S(2)}, u32[]{:S(2)}) collective-permute-start(bf16[384,128]{1,0:T(8,128)(2,1)} %pad_maximum_fusion.1.l0), channel_id=1, source_target_pairs={{0,2},{1,3},{2,0},{3,1},{4,6},{5,7},{6,4},{7,5},{8,10},{9,11},{10,... | collective-permute-start | bytes 294920 | tf_op jit(solution)/shard_map/ppermute | solution.py:440
  58.9 0.6 copy-start.4
  63.4 0.6 copy-start.6
  65.5 31.4 %collective-permute-start.5 = (bf16[384,128]{1,0:T(8,128)(2,1)}, bf16[384,128]{1,0:T(8,128)(2,1)}, u32[]{:S(2)}, u32[]{:S(2)}) collective-permute-start(bf16[384,128]{1,0:T(8,128)(2,1)} %pad_maximum_fusion.1.l0), channel_id=1, source_target_pairs={{0,3},{1,0},{2,1},{3,2},{4,7},{5,4},{6,5},{7,6},{8,11},{9,8},{10,9... | collective-permute-start | bytes 294920 | tf_op jit(solution)/shard_map/ppermute | solution.py:440
  68.3 19.5 %all-to-all-start.2 = ((bf16[32,32,128]{2,1,0:T(8,128)(2,1)}), bf16[32,32,128]{2,1,0:T(8,128)(2,1)S(1)}, u32[]{:S(2)}, u32[]{:S(2)}) async-start(bf16[32,32,128]{2,1,0:T(8,128)(2,1)} %bitcast.28), calls=%async_computation.2 | async-start | bytes 524288 | tf_op jit(solution)/shard_map/all_to_all | solution.py:444
  77.9 19.0 %copy-start.3 = (s32[1,128]{1,0:T(1,128)S(1)}, s32[1,128]{1,0:T(1,128)}, u32[]{:S(2)}) copy-start(s32[1,128]{1,0:T(1,128)} %leaf_ref.1) | copy-start | bytes 1540
  92.5 18.2 %all-to-all-start.3 = ((bf16[32,48,128]{2,1,0:T(8,128)(2,1)}), bf16[32,48,128]{2,1,0:T(8,128)(2,1)S(1)}, u32[]{:S(2)}, u32[]{:S(2)}) async-start(bf16[32,48,128]{2,1,0:T(8,128)(2,1)} %branch_attend.1), calls=%async_computation.3 | async-start | bytes 786432 | tf_op jit(solution)/shard_map/all_to_all | solution.py:444
  97.0 0.9 copy-start.5
  97.9 0.9 copy-start.7
  103.3 0.6 copy-start
  104.0 0.6 copy-start.8
  104.6 0.6 copy-start.9
  105.2 0.6 copy-start.10
  112.1 20.2 %all-to-all-start.4 = ((bf16[4,80,128]{2,1,0:T(8,128)(2,1)}), bf16[4,80,128]{2,1,0:T(8,128)(2,1)S(1)}, u32[]{:S(2)}, u32[]{:S(2)}) async-start(bf16[4,80,128]{2,1,0:T(8,128)(2,1)} %merge_node.1), calls=%async_computation.4 | async-start | bytes 163840 | tf_op jit(solution)/shard_map/all_to_all | solution.py:444
  119.8 9.0 %collective-permute-start.6 = (bf16[144,128]{1,0:T(8,128)(2,1)}, bf16[144,128]{1,0:T(8,128)(2,1)S(1)}, u32[]{:S(2)}, u32[]{:S(2)}) collective-permute-start(bf16[144,128]{1,0:T(8,128)(2,1)} %copy-done.10), channel_id=1, source_target_pairs={{0,1},{1,2},{2,3},{3,0},{4,5},{5,6},{6,7},{7,4},{8,9},{9,10},{10,1... | collective-permute-start | bytes 110600 | tf_op jit(solution)/shard_map/ppermute | solution.py:440
  121.7 7.1 %collective-permute-start.7 = (bf16[144,128]{1,0:T(8,128)(2,1)}, bf16[144,128]{1,0:T(8,128)(2,1)S(1)}, u32[]{:S(2)}, u32[]{:S(2)}) collective-permute-start(bf16[144,128]{1,0:T(8,128)(2,1)} %copy-done.9), channel_id=1, source_target_pairs={{0,2},{1,3},{2,0},{3,1},{4,6},{5,7},{6,4},{7,5},{8,10},{9,11},{10,... | collective-permute-start | bytes 110600 | tf_op jit(solution)/shard_map/ppermute | solution.py:440
  124.4 6.5 %collective-permute-start.8 = (bf16[144,128]{1,0:T(8,128)(2,1)}, bf16[144,128]{1,0:T(8,128)(2,1)S(1)}, u32[]{:S(2)}, u32[]{:S(2)}) collective-permute-start(bf16[144,128]{1,0:T(8,128)(2,1)} %copy-done.8), channel_id=1, source_target_pairs={{0,3},{1,0},{2,1},{3,2},{4,7},{5,4},{6,5},{7,6},{8,11},{9,8},{10,9... | collective-permute-start | bytes 110600 | tf_op jit(solution)/shard_map/ppermute | solution.py:440
  132.3 0.8 copy-start.1
Sparse Core Ops, SparseCore 0:
  65.6 28.7 all-gather.2

commit v4 on v3

--- a/solution.py
+++ b/solution.py
@@ -16,7 +16,7 @@
 COST_FLOPS = 15_000_000_000
 LOCAL_FLOPS = 30_000_000_000
 LENGTH_FLOPS = 6_000_000_000
-VMEM_LIMIT = 50 * 1024 * 1024
+VMEM_LIMIT = 32 * 1024 * 1024
 
 
 def iota(shape, dim):

time: 142 us -> 141 us (level)
  starting transfers between devices: 68.7 us -> 73.1 us
  local copies, waits for them, and re-layouts: 9.18 us -> 5.55 us
  waiting for transfers between devices: 27.7 us -> 26 us
    ppermute x9, starting transfers between devices: 28.3 us -> 33 us  [shift(): return lax.ppermute(values, axis, [(i, (i + step) % 4) for i in range(4)])]
    unnamed x28 -> x20, local copies, waits for them, and re-layouts: 6.91 us -> 4.05 us
    ppermute x9, waiting for transfers between devices: 11.4 us -> 8.74 us  [shift(): return lax.ppermute(values, axis, [(i, (i + step) % 4) for i in range(4)])]
  transfers between devices with their start and end apart: 15 -> 15, of which waited for: 6 -> 5; matrix products, arithmetic and copies ran while one was open for 3% -> 2% of each run, Pallas kernels for 11% -> 11%
where the time goes in v4:
time: 141 us; the launch traced here: 140 us
  starting transfers between devices  73.1 us (52%)
  waiting for transfers between devices  26 us (18%)
  Pallas kernels  19.8 us (14%)
  between operations  14.3 us (10%)
  local copies, waits for them, and re-layouts  5.55 us (4%)
    all_to_all x5, starting transfers between devices, exchange(): return lax.all_to_all(values, axis, split_axis=0, concat_axis=0, tiled=True)  40.1 us
    ppermute x9, starting transfers between devices, shift(): return lax.ppermute(values, axis, [(i, (i + step) % 4) for i in range(4)])  33 us
    all_to_all x5, waiting for transfers between devices, exchange(): return lax.all_to_all(values, axis, split_axis=0, concat_axis=0, tiled=True)  17.2 us
    ppermute x9, waiting for transfers between devices, shift(): return lax.ppermute(values, axis, [(i, (i + step) % 4) for i in range(4)])  8.74 us
    pallas_call x1, Pallas kernels, branch_attend(): pl.pallas_call(branch_kernel, out_shape=jax.ShapeDtypeStruct((32, 48, 128...  4.75 us
    pallas_call x1, Pallas kernels, local_attend(): pl.pallas_call(local_kernel, out_shape=tuple((jax.ShapeDtypeStruct((144,...  4.65 us
    pallas_call x1, Pallas kernels, pack_caches(): pl.pallas_call(pack_kernel, out_shape=tuple((jax.ShapeDtypeStruct((4096,...  4.16 us
    unnamed x20, local copies, waits for them, and re-layouts  4.05 us
  transfers between devices with their start and end apart: 15, of which 5 were waited for; matrix products, arithmetic and copies ran while one was open for 2% of the time, Pallas kernels for 11%

profile of v4, /device:TPU:1, one launch (start us, length us, event | category | flops | bytes accessed | tf_op | source)
XLA Modules:
  0.0 139.6 jit_solution(813795034802487448)
XLA Ops:
  6.5 0.7 copy-done.2
  7.2 2.2 %first_stage.1 = (bf16[4,64,128]{2,1,0:T(8,128)(2,1)S(1)}, s32[1,128]{1,0:T(1,128)S(1)}, bf16[4,160,128]{2,1,0:T(8,128)(2,1)}) custom-call(s32[1,32]{1,0:T(1,128)S(1)} %copy-done.2, s32[1,128]{1,0:T(1,128)} %leaf_ref.1, bf16[128,128]{1,0:T(8,128)(2,1)} %q_hbm.1, bf16[8,2048]{1,0:T(8,128)(2,1)} %root_hbm.1, bf16[128,128]{1,0:T(8,128)(2,1)} %suffix_hbm.1), custom_call_target="tpu_custom_call" | custom-call | tf_op jit(solution)/shard_map/first_stage/pallas_call | solution.py:77
  9.4 5.0 %all-to-all-start = ((bf16[4,160,128]{2,1,0:T(8,128)(2,1)}), bf16[4,160,128]{2,1,0:T(8,128)(2,1)S(1)}, u32[]{:S(2)}, u32[]{:S(2)}) async-start(bf16[4,160,128]{2,1,0:T(8,128)(2,1)} %get-tuple-element.28), calls=%async_computation | async-start | bytes 327680 | tf_op jit(solution)/shard_map/all_to_all | solution.py:444
  15.1 0.1 pad_add_fusion.info
  15.1 4.2 %pack_caches.1 = (bf16[4096,128]{1,0:T(8,128)(2,1)}, bf16[4096,128]{1,0:T(8,128)(2,1)}, bf16[4096,128]{1,0:T(8,128)(2,1)}) custom-call(s32[3]{0:T(128)S(1)} %pad_add_fusion.info, bf16[512,2048]{1,0:T(8,128)(2,1)} %bitcast.22, bf16[512,2048]{1,0:T(8,128)(2,1)} %bitcast.25), custom_call_target="tpu_custom_call" | custom-call | tf_op jit(solution)/shard_map/pack_caches/pallas_call | solution.py:126
  19.3 3.4 %collective-permute-start = (bf16[4096,128]{1,0:T(8,128)(2,1)}, bf16[4096,128]{1,0:T(8,128)(2,1)S(1)}, u32[]{:S(2)}, u32[]{:S(2)}) collective-permute-start(bf16[4096,128]{1,0:T(8,128)(2,1)} %get-tuple-element.24), channel_id=1, source_target_pairs={{0,4},{4,8},{8,12},{12,0},{1,5},{5,9},{9,13},{13,1},{2,6},{6,10},{... | collective-permute-start | bytes 3145736 | tf_op jit(solution)/shard_map/ppermute | solution.py:440
  22.7 4.3 %collective-permute-start.1 = (bf16[4096,128]{1,0:T(8,128)(2,1)}, bf16[4096,128]{1,0:T(8,128)(2,1)}, u32[]{:S(2)}, u32[]{:S(2)}) collective-permute-start(bf16[4096,128]{1,0:T(8,128)(2,1)} %get-tuple-element.25), channel_id=1, source_target_pairs={{0,8},{4,12},{8,0},{12,4},{1,9},{5,13},{9,1},{13,5},{2,10},{6,14},... | collective-permute-start | bytes 3145736 | tf_op jit(solution)/shard_map/ppermute | solution.py:440
  27.0 3.1 %collective-permute-start.2 = (bf16[4096,128]{1,0:T(8,128)(2,1)}, bf16[4096,128]{1,0:T(8,128)(2,1)}, u32[]{:S(2)}, u32[]{:S(2)}) collective-permute-start(bf16[4096,128]{1,0:T(8,128)(2,1)} %get-tuple-element.26), channel_id=1, source_target_pairs={{0,12},{4,0},{8,4},{12,8},{1,13},{5,1},{9,5},{13,9},{2,14},{6,2},{... | collective-permute-start | bytes 3145736 | tf_op jit(solution)/shard_map/ppermute | solution.py:440
  30.1 0.0 all-to-all-done
  30.1 0.7 pad_maximum_fusion
  30.8 14.8 %all-to-all-start.1 = ((bf16[4,192,128]{2,1,0:T(8,128)(2,1)}), bf16[4,192,128]{2,1,0:T(8,128)(2,1)S(1)}, u32[]{:S(2)}, u32[]{:S(2)}) async-start(bf16[4,192,128]{2,1,0:T(8,128)(2,1)} %pad_maximum_fusion), calls=%async_computation.1 | async-start | bytes 393216 | tf_op jit(solution)/shard_map/all_to_all | solution.py:444
  45.7 2.6 %collective-permute-start.3 = (bf16[384,128]{1,0:T(8,128)(2,1)S(1)}, bf16[384,128]{1,0:T(8,128)(2,1)S(1)}, u32[]{:S(2)}, u32[]{:S(2)}) collective-permute-start(bf16[384,128]{1,0:T(8,128)(2,1)S(1)} %pad_maximum_fusion.1.l0), channel_id=1, source_target_pairs={{0,1},{1,2},{2,3},{3,0},{4,5},{5,6},{6,7},{7,4},{8,9},{9,10},{10,1... | collective-permute-start | bytes 294920 | tf_op jit(solution)/shard_map/ppermute | solution.py:440
  48.3 3.1 %collective-permute-start.4 = (bf16[384,128]{1,0:T(8,128)(2,1)S(1)}, bf16[384,128]{1,0:T(8,128)(2,1)S(1)}, u32[]{:S(2)}, u32[]{:S(2)}) collective-permute-start(bf16[384,128]{1,0:T(8,128)(2,1)S(1)} %pad_maximum_fusion.1.l0), channel_id=1, source_target_pairs={{0,2},{1,3},{2,0},{3,1},{4,6},{5,7},{6,4},{7,5},{8,10},{9,11},{10,... | collective-permute-start | bytes 294920 | tf_op jit(solution)/shard_map/ppermute | solution.py:440
  51.5 0.6 key_lengths.1.lengths_ref
  52.1 6.8 %collective-permute-done.3.l1 = bf16[384,128]{1,0:T(8,128)(2,1)S(1)} collective-permute-done((bf16[384,128]{1,0:T(8,128)(2,1)S(1)}, bf16[384,128]{1,0:T(8,128)(2,1)S(1)}, u32[]{:S(2)}, u32[]{:S(2)}) %collective-permute-start.3) | collective-permute-done | bytes 98336 | tf_op jit(solution)/shard_map/ppermute | solution.py:440
  58.9 0.0 collective-permute-done.4.l2
  58.9 0.0 all-to-all-done.1
  58.9 0.7 copy.11
  59.6 0.8 broadcast_in_dim.17
  60.4 0.0 all-gather.3.cloned.1.call-update
  60.4 7.5 %collective-permute-start.5 = (bf16[384,128]{1,0:T(8,128)(2,1)S(1)}, bf16[384,128]{1,0:T(8,128)(2,1)}, u32[]{:S(2)}, u32[]{:S(2)}) collective-permute-start(bf16[384,128]{1,0:T(8,128)(2,1)S(1)} %pad_maximum_fusion.1.l0), channel_id=1, source_target_pairs={{0,3},{1,0},{2,1},{3,2},{4,7},{5,4},{6,5},{7,6},{8,11},{9,8},{10,9... | collective-permute-start | bytes 294920 | tf_op jit(solution)/shard_map/ppermute | solution.py:440
  68.0 9.0 %all-to-all-start.2 = ((bf16[32,32,128]{2,1,0:T(8,128)(2,1)}), bf16[32,32,128]{2,1,0:T(8,128)(2,1)S(1)}, u32[]{:S(2)}, u32[]{:S(2)}) async-start(bf16[32,32,128]{2,1,0:T(8,128)(2,1)} %bitcast.10), calls=%async_computation.2 | async-start | bytes 524288 | tf_op jit(solution)/shard_map/all_to_all | solution.py:444
  77.0 0.0 copy-start
  77.0 0.0 collective-permute-done.p1
  77.0 0.0 collective-permute-done.1.p2
  77.0 0.0 collective-permute-done.2.p3
  77.0 1.1 arrive.1.info
  78.1 0.0 copy-start.3
  78.2 9.9 %all-to-all-done.2.q_ref = bf16[32,32,128]{2,1,0:T(8,128)(2,1)S(1)} async-done(((bf16[32,32,128]{2,1,0:T(8,128)(2,1)}), bf16[32,32,128]{2,1,0:T(8,128)(2,1)S(1)}, u32[]{:S(2)}, u32[]{:S(2)}) %all-to-all-start.2) | async-done | bytes 262176 | tf_op jit(solution)/shard_map/all_to_all | solution.py:444
  88.1 4.7 %branch_attend.1 = bf16[32,48,128]{2,1,0:T(8,128)(2,1)} custom-call(s32[3]{0:T(128)S(1)} %arrive.1.info, bf16[32,32,128]{2,1,0:T(8,128)(2,1)S(1)} %all-to-all-done.2.q_ref, bf16[512,2048]{1,0:T(8,128)(2,1)S(1)} %bitcast.23, bf16[512,2048]{1,0:T(8,128)(2,1)S(1)} %bitcast.24, bf16[4096,128]{1,0:T(8,128)(2,1)S(1)} %collective-permute-done.p1, ...), custom_call_target="tpu_custom_call" | custom-call | tf_op jit(solution)/shard_map/branch_attend/pallas_call | solution.py:254
  92.8 4.4 %all-to-all-start.3 = ((bf16[32,48,128]{2,1,0:T(8,128)(2,1)}), bf16[32,48,128]{2,1,0:T(8,128)(2,1)S(1)}, u32[]{:S(2)}, u32[]{:S(2)}) async-start(bf16[32,48,128]{2,1,0:T(8,128)(2,1)} %branch_attend.1), calls=%async_computation.3 | async-start | bytes 786432 | tf_op jit(solution)/shard_map/all_to_all | solution.py:444
  97.2 0.0 collective-permute-done.5.l3
  97.2 0.0 all-gather.3.cloned.1.call-done
  97.3 0.0 copy-start.1
  97.3 1.6 %copy-done.1 = bf16[32,16,2048]{2,1,0:T(8,128)(2,1)S(1)} copy-done((bf16[32,16,2048]{2,1,0:T(8,128)(2,1)S(1)}, bf16[32,16,2048]{2,1,0:T(8,128)(2,1)}, u32[]{:S(2)}) %copy-start.1) | copy-done | bytes 2097176
  98.9 0.9 copy-done.5
  99.8 0.9 copy-done.7
  100.7 4.7 %local_attend.1 = (bf16[144,128]{1,0:T(8,128)(2,1)S(1)}, bf16[144,128]{1,0:T(8,128)(2,1)S(1)}, bf16[144,128]{1,0:T(8,128)(2,1)S(1)}, bf16[144,128]{1,0:T(8,128)(2,1)S(1)}) custom-call(s32[3]{0:T(128)S(1)} %pad_add_fusion.info, s32[1,128]{1,0:T(1,128)S(1)} %copy-done.3, s32[1,512]{1,0:T(1,128)S(1)} %key_lengths.1.lengths_ref, bf16[512,2048]{1,0:T(8,128)(2,1)S(1)} %bitcast.26, ...), custom_call_target="tpu_custom_call" | custom-call | flops 30000001024 | bytes 8000000 | tf_op jit(solution)/shard_map/local_attend/pallas_call | solution.py:362
  105.3 5.7 %all-to-all-done.3.in_ref = bf16[32,48,128]{2,1,0:T(8,128)(2,1)S(1)} async-done(((bf16[32,48,128]{2,1,0:T(8,128)(2,1)}), bf16[32,48,128]{2,1,0:T(8,128)(2,1)S(1)}, u32[]{:S(2)}, u32[]{:S(2)}) %all-to-all-start.3) | async-done | bytes 393248 | tf_op jit(solution)/shard_map/all_to_all | solution.py:444
  111.0 1.4 merge_node.1
  112.4 6.9 %all-to-all-start.4 = ((bf16[4,80,128]{2,1,0:T(8,128)(2,1)}), bf16[4,80,128]{2,1,0:T(8,128)(2,1)S(1)}, u32[]{:S(2)}, u32[]{:S(2)}) async-start(bf16[4,80,128]{2,1,0:T(8,128)(2,1)} %merge_node.1), calls=%async_computation.4 | async-start | bytes 163840 | tf_op jit(solution)/shard_map/all_to_all | solution.py:444
  119.3 1.9 %collective-permute-start.6 = (bf16[144,128]{1,0:T(8,128)(2,1)S(1)}, bf16[144,128]{1,0:T(8,128)(2,1)S(1)}, u32[]{:S(2)}, u32[]{:S(2)}) collective-permute-start(bf16[144,128]{1,0:T(8,128)(2,1)S(1)} %get-tuple-element.38), channel_id=1, source_target_pairs={{0,1},{1,2},{2,3},{3,0},{4,5},{5,6},{6,7},{7,4},{8,9},{9,10},{10,1... | collective-permute-start | bytes 110600 | tf_op jit(solution)/shard_map/ppermute | solution.py:440
  121.2 2.7 %collective-permute-start.7 = (bf16[144,128]{1,0:T(8,128)(2,1)S(1)}, bf16[144,128]{1,0:T(8,128)(2,1)S(1)}, u32[]{:S(2)}, u32[]{:S(2)}) collective-permute-start(bf16[144,128]{1,0:T(8,128)(2,1)S(1)} %get-tuple-element.39), channel_id=1, source_target_pairs={{0,2},{1,3},{2,0},{3,1},{4,6},{5,7},{6,4},{7,5},{8,10},{9,11},{10,... | collective-permute-start | bytes 110600 | tf_op jit(solution)/shard_map/ppermute | solution.py:440
  123.9 4.3 %collective-permute-start.8 = (bf16[144,128]{1,0:T(8,128)(2,1)S(1)}, bf16[144,128]{1,0:T(8,128)(2,1)S(1)}, u32[]{:S(2)}, u32[]{:S(2)}) collective-permute-start(bf16[144,128]{1,0:T(8,128)(2,1)S(1)} %get-tuple-element.40), channel_id=1, source_target_pairs={{0,3},{1,0},{2,1},{3,2},{4,7},{5,4},{6,5},{7,6},{8,11},{9,8},{10,9... | collective-permute-start | bytes 110600 | tf_op jit(solution)/shard_map/ppermute | solution.py:440
  128.3 0.0 collective-permute-done.7.l2
  128.3 1.9 %collective-permute-done.8.l3 = bf16[144,128]{1,0:T(8,128)(2,1)S(1)} collective-permute-done((bf16[144,128]{1,0:T(8,128)(2,1)S(1)}, bf16[144,128]{1,0:T(8,128)(2,1)S(1)}, u32[]{:S(2)}, u32[]{:S(2)}) %collective-permute-start.8) | collective-permute-done | bytes 36896 | tf_op jit(solution)/shard_map/ppermute | solution.py:440
  130.2 1.6 %all-to-all-done.4.branch_ref = bf16[4,80,128]{2,1,0:T(8,128)(2,1)S(1)} async-done(((bf16[4,80,128]{2,1,0:T(8,128)(2,1)}), bf16[4,80,128]{2,1,0:T(8,128)(2,1)S(1)}, u32[]{:S(2)}, u32[]{:S(2)}) %all-to-all-start.4) | async-done | bytes 81952 | tf_op jit(solution)/shard_map/all_to_all | solution.py:444
  131.8 1.0 finish.1
  (21 shorter events, 0.1 us)
Async XLA Ops:
  6.5 0.7 copy-start.2
  9.4 20.7 %all-to-all-start = ((bf16[4,160,128]{2,1,0:T(8,128)(2,1)}), bf16[4,160,128]{2,1,0:T(8,128)(2,1)S(1)}, u32[]{:S(2)}, u32[]{:S(2)}) async-start(bf16[4,160,128]{2,1,0:T(8,128)(2,1)} %get-tuple-element.28), calls=%async_computation | async-start | bytes 327680 | tf_op jit(solution)/shard_map/all_to_all | solution.py:444
  15.1 30.5 %copy-start.9 = (bf16[128,128]{1,0:T(8,128)(2,1)S(1)}, bf16[128,128]{1,0:T(8,128)(2,1)}, u32[]{:S(2)}) copy-start(bf16[128,128]{1,0:T(8,128)(2,1)} %q_hbm.1) | copy-start | bytes 98308
  15.1 36.3 %copy-start.8 = (s32[32]{0:T(128)S(1)}, s32[32]{0:T(128)}, u32[]{:S(2)}) copy-start(s32[32]{0:T(128)} %lengths.1) | copy-start | bytes 388
  19.3 57.7 %collective-permute-start = (bf16[4096,128]{1,0:T(8,128)(2,1)}, bf16[4096,128]{1,0:T(8,128)(2,1)S(1)}, u32[]{:S(2)}, u32[]{:S(2)}) collective-permute-start(bf16[4096,128]{1,0:T(8,128)(2,1)} %get-tuple-element.24), channel_id=1, source_target_pairs={{0,4},{4,8},{8,12},{12,0},{1,5},{5,9},{9,13},{13,1},{2,6},{6,10},{... | collective-permute-start | bytes 3145736 | tf_op jit(solution)/shard_map/ppermute | solution.py:440
  22.7 54.3 %collective-permute-start.1 = (bf16[4096,128]{1,0:T(8,128)(2,1)}, bf16[4096,128]{1,0:T(8,128)(2,1)}, u32[]{:S(2)}, u32[]{:S(2)}) collective-permute-start(bf16[4096,128]{1,0:T(8,128)(2,1)} %get-tuple-element.25), channel_id=1, source_target_pairs={{0,8},{4,12},{8,0},{12,4},{1,9},{5,13},{9,1},{13,5},{2,10},{6,14},... | collective-permute-start | bytes 3145736 | tf_op jit(solution)/shard_map/ppermute | solution.py:440
  27.0 50.0 %collective-permute-start.2 = (bf16[4096,128]{1,0:T(8,128)(2,1)}, bf16[4096,128]{1,0:T(8,128)(2,1)}, u32[]{:S(2)}, u32[]{:S(2)}) collective-permute-start(bf16[4096,128]{1,0:T(8,128)(2,1)} %get-tuple-element.26), channel_id=1, source_target_pairs={{0,12},{4,0},{8,4},{12,8},{1,13},{5,1},{9,5},{13,9},{2,14},{6,2},{... | collective-permute-start | bytes 3145736 | tf_op jit(solution)/shard_map/ppermute | solution.py:440
  30.8 28.1 %all-to-all-start.1 = ((bf16[4,192,128]{2,1,0:T(8,128)(2,1)}), bf16[4,192,128]{2,1,0:T(8,128)(2,1)S(1)}, u32[]{:S(2)}, u32[]{:S(2)}) async-start(bf16[4,192,128]{2,1,0:T(8,128)(2,1)} %pad_maximum_fusion), calls=%async_computation.1 | async-start | bytes 393216 | tf_op jit(solution)/shard_map/all_to_all | solution.py:444
  45.7 51.6 %all-gather.3.cloned.1.call-start = ((), (), s32[]{:S(2)}) async-start(), calls=%async_computation.5 | async-start | bytes 1179648 | tf_op jit(solution)/shard_map/all_gather | solution.py:479
  45.7 13.2 %collective-permute-start.3 = (bf16[384,128]{1,0:T(8,128)(2,1)S(1)}, bf16[384,128]{1,0:T(8,128)(2,1)S(1)}, u32[]{:S(2)}, u32[]{:S(2)}) collective-permute-start(bf16[384,128]{1,0:T(8,128)(2,1)S(1)} %pad_maximum_fusion.1.l0), channel_id=1, source_target_pairs={{0,1},{1,2},{2,3},{3,0},{4,5},{5,6},{6,7},{7,4},{8,9},{9,10},{10,1... | collective-permute-start | bytes 294920 | tf_op jit(solution)/shard_map/ppermute | solution.py:440
  48.3 10.6 %collective-permute-start.4 = (bf16[384,128]{1,0:T(8,128)(2,1)S(1)}, bf16[384,128]{1,0:T(8,128)(2,1)S(1)}, u32[]{:S(2)}, u32[]{:S(2)}) collective-permute-start(bf16[384,128]{1,0:T(8,128)(2,1)S(1)} %pad_maximum_fusion.1.l0), channel_id=1, source_target_pairs={{0,2},{1,3},{2,0},{3,1},{4,6},{5,7},{6,4},{7,5},{8,10},{9,11},{10,... | collective-permute-start | bytes 294920 | tf_op jit(solution)/shard_map/ppermute | solution.py:440
  58.9 9.0 %copy-start.4 = (bf16[384,128]{1,0:T(8,128)(2,1)}, bf16[384,128]{1,0:T(8,128)(2,1)S(1)}, u32[]{:S(2)}) copy-start(bf16[384,128]{1,0:T(8,128)(2,1)S(1)} %collective-permute-done.3.l1) | copy-start | bytes 294916
  58.9 9.0 %copy-start.6 = (bf16[384,128]{1,0:T(8,128)(2,1)}, bf16[384,128]{1,0:T(8,128)(2,1)S(1)}, u32[]{:S(2)}) copy-start(bf16[384,128]{1,0:T(8,128)(2,1)S(1)} %collective-permute-done.4.l2) | copy-start | bytes 294916
  60.4 36.8 %collective-permute-start.5 = (bf16[384,128]{1,0:T(8,128)(2,1)S(1)}, bf16[384,128]{1,0:T(8,128)(2,1)}, u32[]{:S(2)}, u32[]{:S(2)}) collective-permute-start(bf16[384,128]{1,0:T(8,128)(2,1)S(1)} %pad_maximum_fusion.1.l0), channel_id=1, source_target_pairs={{0,3},{1,0},{2,1},{3,2},{4,7},{5,4},{6,5},{7,6},{8,11},{9,8},{10,9... | collective-permute-start | bytes 294920 | tf_op jit(solution)/shard_map/ppermute | solution.py:440
  68.0 20.1 %all-to-all-start.2 = ((bf16[32,32,128]{2,1,0:T(8,128)(2,1)}), bf16[32,32,128]{2,1,0:T(8,128)(2,1)S(1)}, u32[]{:S(2)}, u32[]{:S(2)}) async-start(bf16[32,32,128]{2,1,0:T(8,128)(2,1)} %bitcast.10), calls=%async_computation.2 | async-start | bytes 524288 | tf_op jit(solution)/shard_map/all_to_all | solution.py:444
  77.0 11.1 %copy-start = (bf16[1,512,2048]{2,1,0:T(8,128)(2,1)S(1)}, bf16[1,512,2048]{2,1,0:T(8,128)(2,1)}, u32[]{:S(2)}) copy-start(bf16[1,512,2048]{2,1,0:T(8,128)(2,1)} %param.14) | copy-start | bytes 6291460
  78.1 19.1 %copy-start.3 = (s32[1,128]{1,0:T(1,128)S(1)}, s32[1,128]{1,0:T(1,128)}, u32[]{:S(2)}) copy-start(s32[1,128]{1,0:T(1,128)} %leaf_ref.1) | copy-start | bytes 1540
  92.8 18.2 %all-to-all-start.3 = ((bf16[32,48,128]{2,1,0:T(8,128)(2,1)}), bf16[32,48,128]{2,1,0:T(8,128)(2,1)S(1)}, u32[]{:S(2)}, u32[]{:S(2)}) async-start(bf16[32,48,128]{2,1,0:T(8,128)(2,1)} %branch_attend.1), calls=%async_computation.3 | async-start | bytes 786432 | tf_op jit(solution)/shard_map/all_to_all | solution.py:444
  97.3 1.6 %copy-start.1 = (bf16[32,16,2048]{2,1,0:T(8,128)(2,1)S(1)}, bf16[32,16,2048]{2,1,0:T(8,128)(2,1)}, u32[]{:S(2)}) copy-start(bf16[32,16,2048]{2,1,0:T(8,128)(2,1)} %param.16) | copy-start | bytes 6291460
  98.9 0.9 copy-start.5
  99.8 0.9 copy-start.7
  112.4 19.4 %all-to-all-start.4 = ((bf16[4,80,128]{2,1,0:T(8,128)(2,1)}), bf16[4,80,128]{2,1,0:T(8,128)(2,1)S(1)}, u32[]{:S(2)}, u32[]{:S(2)}) async-start(bf16[4,80,128]{2,1,0:T(8,128)(2,1)} %merge_node.1), calls=%async_computation.4 | async-start | bytes 163840 | tf_op jit(solution)/shard_map/all_to_all | solution.py:444
  119.3 9.0 %collective-permute-start.6 = (bf16[144,128]{1,0:T(8,128)(2,1)S(1)}, bf16[144,128]{1,0:T(8,128)(2,1)S(1)}, u32[]{:S(2)}, u32[]{:S(2)}) collective-permute-start(bf16[144,128]{1,0:T(8,128)(2,1)S(1)} %get-tuple-element.38), channel_id=1, source_target_pairs={{0,1},{1,2},{2,3},{3,0},{4,5},{5,6},{6,7},{7,4},{8,9},{9,10},{10,1... | collective-permute-start | bytes 110600 | tf_op jit(solution)/shard_map/ppermute | solution.py:440
  121.2 7.1 %collective-permute-start.7 = (bf16[144,128]{1,0:T(8,128)(2,1)S(1)}, bf16[144,128]{1,0:T(8,128)(2,1)S(1)}, u32[]{:S(2)}, u32[]{:S(2)}) collective-permute-start(bf16[144,128]{1,0:T(8,128)(2,1)S(1)} %get-tuple-element.39), channel_id=1, source_target_pairs={{0,2},{1,3},{2,0},{3,1},{4,6},{5,7},{6,4},{7,5},{8,10},{9,11},{10,... | collective-permute-start | bytes 110600 | tf_op jit(solution)/shard_map/ppermute | solution.py:440
  123.9 6.3 %collective-permute-start.8 = (bf16[144,128]{1,0:T(8,128)(2,1)S(1)}, bf16[144,128]{1,0:T(8,128)(2,1)S(1)}, u32[]{:S(2)}, u32[]{:S(2)}) collective-permute-start(bf16[144,128]{1,0:T(8,128)(2,1)S(1)} %get-tuple-element.40), channel_id=1, source_target_pairs={{0,3},{1,0},{2,1},{3,2},{4,7},{5,4},{6,5},{7,6},{8,11},{9,8},{10,9... | collective-permute-start | bytes 110600 | tf_op jit(solution)/shard_map/ppermute | solution.py:440
Sparse Core Ops, SparseCore 0:
  60.5 33.2 all-gather.2

commit v5 on v4

--- a/solution.py
+++ b/solution.py
@@ -14,7 +14,7 @@
 NEG = -1e30
 FLOOR = -1e29
 COST_FLOPS = 15_000_000_000
-LOCAL_FLOPS = 30_000_000_000
+LOCAL_FLOPS = 12_000_000_000
 LENGTH_FLOPS = 6_000_000_000
 VMEM_LIMIT = 32 * 1024 * 1024
 
@@ -469,7 +469,7 @@
         return lax.dynamic_index_in_dim(own, source, 0, keepdims=False)[32:160]
 
     mine = jnp.concatenate([queries, chosen(y >> 1), chosen(2 + (y >> 1))], axis=0)
-    gathered = [mine] + [shift(mine, "zl", s + 1) for s in range(3)]
+    gathered = [mine] + [shift(mine, "zl", s + 1) for s in range(2)]
     arrived, lengths, gathered[1], gathered[2] = tie((arrived, key_lengths(leaf_length), gathered[1], gathered[2]))
 
     onward = arrived[:, 0:64].reshape(4, 8, 8, 128).transpose(1, 0, 2, 3).reshape(8, 1, 32, 128)
@@ -478,6 +478,8 @@
     onward, root = tie((onward, root.reshape(512, 128)))
     root_all = lax.all_gather(root, XC, axis=0, tiled=False)
     node_queries = exchange(onward, XCZ)
+    node_queries, last = tie((node_queries, mine))
+    gathered.append(shift(last, "zl", 3))
 
     partials = branch_attend(arrive(info, pieces), node_queries, branch_rows, pieces)
     returned = exchange(partials, XCZ)

time: 141 us -> 145 us (1.028)
  the two profiles are of different devices: /device:TPU:1 before, /device:TPU:6 now
where the time goes in v5:
time: 145 us; the launch traced here: 143 us
  starting transfers between devices  76.5 us (53%)
  waiting for transfers between devices  25.7 us (18%)
  Pallas kernels  19.8 us (14%)
  between operations  14.3 us (10%)
  local copies, waits for them, and re-layouts  5.53 us (4%)
    all_to_all x5, starting transfers between devices, exchange(): return lax.all_to_all(values, axis, split_axis=0, concat_axis=0, tiled=True)  40.5 us
    ppermute x9, starting transfers between devices, shift(): return lax.ppermute(values, axis, [(i, (i + step) % 4) for i in range(4)])  35.9 us
    ppermute x9, waiting for transfers between devices, shift(): return lax.ppermute(values, axis, [(i, (i + step) % 4) for i in range(4)])  15.8 us
    all_to_all x5, waiting for transfers between devices, exchange(): return lax.all_to_all(values, axis, split_axis=0, concat_axis=0, tiled=True)  9.92 us
    pallas_call x1, Pallas kernels, branch_attend(): pl.pallas_call(branch_kernel, out_shape=jax.ShapeDtypeStruct((32, 48, 128...  4.77 us
    pallas_call x1, Pallas kernels, local_attend(): pl.pallas_call(local_kernel, out_shape=tuple((jax.ShapeDtypeStruct((144,...  4.62 us
    pallas_call x1, Pallas kernels, pack_caches(): pl.pallas_call(pack_kernel, out_shape=tuple((jax.ShapeDtypeStruct((4096,...  4.16 us
    unnamed x20, local copies, waits for them, and re-layouts  4.06 us
  transfers between devices with their start and end apart: 15, of which 8 were waited for; matrix products, arithmetic and copies ran while one was open for 2% of the time, Pallas kernels for 11%

profile of v5, /device:TPU:6, one launch (start us, length us, event | category | flops | bytes accessed | tf_op | source)
XLA Modules:
  0.0 142.6 jit_solution(1560317100048394969)
XLA Ops:
  6.5 0.7 copy-done.2
  7.2 2.2 %first_stage.1 = (bf16[4,64,128]{2,1,0:T(8,128)(2,1)S(1)}, s32[1,128]{1,0:T(1,128)S(1)}, bf16[4,160,128]{2,1,0:T(8,128)(2,1)}) custom-call(s32[1,32]{1,0:T(1,128)S(1)} %copy-done.2, s32[1,128]{1,0:T(1,128)} %leaf_ref.1, bf16[128,128]{1,0:T(8,128)(2,1)} %q_hbm.1, bf16[8,2048]{1,0:T(8,128)(2,1)} %root_hbm.1, bf16[128,128]{1,0:T(8,128)(2,1)} %suffix_hbm.1), custom_call_target="tpu_custom_call" | custom-call | tf_op jit(solution)/shard_map/first_stage/pallas_call | solution.py:77
  9.4 4.5 %all-to-all-start = ((bf16[4,160,128]{2,1,0:T(8,128)(2,1)}), bf16[4,160,128]{2,1,0:T(8,128)(2,1)S(1)}, u32[]{:S(2)}, u32[]{:S(2)}) async-start(bf16[4,160,128]{2,1,0:T(8,128)(2,1)} %get-tuple-element.30), calls=%async_computation | async-start | bytes 327680 | tf_op jit(solution)/shard_map/all_to_all | solution.py:444
  14.5 0.1 pad_add_fusion.info
  14.6 4.2 %pack_caches.1 = (bf16[4096,128]{1,0:T(8,128)(2,1)}, bf16[4096,128]{1,0:T(8,128)(2,1)}, bf16[4096,128]{1,0:T(8,128)(2,1)}) custom-call(s32[3]{0:T(128)S(1)} %pad_add_fusion.info, bf16[512,2048]{1,0:T(8,128)(2,1)} %bitcast.22, bf16[512,2048]{1,0:T(8,128)(2,1)} %bitcast.25), custom_call_target="tpu_custom_call" | custom-call | tf_op jit(solution)/shard_map/pack_caches/pallas_call | solution.py:126
  18.8 3.9 %collective-permute-start = (bf16[4096,128]{1,0:T(8,128)(2,1)}, bf16[4096,128]{1,0:T(8,128)(2,1)S(1)}, u32[]{:S(2)}, u32[]{:S(2)}) collective-permute-start(bf16[4096,128]{1,0:T(8,128)(2,1)} %get-tuple-element.26), channel_id=1, source_target_pairs={{0,4},{4,8},{8,12},{12,0},{1,5},{5,9},{9,13},{13,1},{2,6},{6,10},{... | collective-permute-start | bytes 3145736 | tf_op jit(solution)/shard_map/ppermute | solution.py:440
  22.7 4.6 %collective-permute-start.1 = (bf16[4096,128]{1,0:T(8,128)(2,1)}, bf16[4096,128]{1,0:T(8,128)(2,1)}, u32[]{:S(2)}, u32[]{:S(2)}) collective-permute-start(bf16[4096,128]{1,0:T(8,128)(2,1)} %get-tuple-element.27), channel_id=1, source_target_pairs={{0,8},{4,12},{8,0},{12,4},{1,9},{5,13},{9,1},{13,5},{2,10},{6,14},... | collective-permute-start | bytes 3145736 | tf_op jit(solution)/shard_map/ppermute | solution.py:440
  27.3 3.4 %collective-permute-start.2 = (bf16[4096,128]{1,0:T(8,128)(2,1)}, bf16[4096,128]{1,0:T(8,128)(2,1)}, u32[]{:S(2)}, u32[]{:S(2)}) collective-permute-start(bf16[4096,128]{1,0:T(8,128)(2,1)} %get-tuple-element.28), channel_id=1, source_target_pairs={{0,12},{4,0},{8,4},{12,8},{1,13},{5,1},{9,5},{13,9},{2,14},{6,2},{... | collective-permute-start | bytes 3145736 | tf_op jit(solution)/shard_map/ppermute | solution.py:440
  30.7 0.0 all-to-all-done
  30.7 0.7 pad_maximum_fusion
  31.4 15.1 %all-to-all-start.1 = ((bf16[4,192,128]{2,1,0:T(8,128)(2,1)}), bf16[4,192,128]{2,1,0:T(8,128)(2,1)S(1)}, u32[]{:S(2)}, u32[]{:S(2)}) async-start(bf16[4,192,128]{2,1,0:T(8,128)(2,1)} %pad_maximum_fusion), calls=%async_computation.1 | async-start | bytes 393216 | tf_op jit(solution)/shard_map/all_to_all | solution.py:444
  46.5 0.0 copy-done.9
  46.5 2.9 %collective-permute-start.3 = (bf16[384,128]{1,0:T(8,128)(2,1)S(1)}, bf16[384,128]{1,0:T(8,128)(2,1)S(1)}, u32[]{:S(2)}, u32[]{:S(2)}) collective-permute-start(bf16[384,128]{1,0:T(8,128)(2,1)S(1)} %pad_maximum_fusion.1.l0), channel_id=1, source_target_pairs={{0,1},{1,2},{2,3},{3,0},{4,5},{5,6},{6,7},{7,4},{8,9},{9,10},{10,1... | collective-permute-start | bytes 294920 | tf_op jit(solution)/shard_map/ppermute | solution.py:440
  49.5 3.4 %collective-permute-start.4 = (bf16[384,128]{1,0:T(8,128)(2,1)S(1)}, bf16[384,128]{1,0:T(8,128)(2,1)S(1)}, u32[]{:S(2)}, u32[]{:S(2)}) collective-permute-start(bf16[384,128]{1,0:T(8,128)(2,1)S(1)} %pad_maximum_fusion.1.l0), channel_id=1, source_target_pairs={{0,2},{1,3},{2,0},{3,1},{4,6},{5,7},{6,4},{7,5},{8,10},{9,11},{10,... | collective-permute-start | bytes 294920 | tf_op jit(solution)/shard_map/ppermute | solution.py:440
  52.9 0.6 key_lengths.1.lengths_ref
  53.5 6.3 %collective-permute-done.3.l1 = bf16[384,128]{1,0:T(8,128)(2,1)S(1)} collective-permute-done((bf16[384,128]{1,0:T(8,128)(2,1)S(1)}, bf16[384,128]{1,0:T(8,128)(2,1)S(1)}, u32[]{:S(2)}, u32[]{:S(2)}) %collective-permute-start.3) | collective-permute-done | bytes 98336 | tf_op jit(solution)/shard_map/ppermute | solution.py:440
  59.8 3.0 %collective-permute-done.4.l2 = bf16[384,128]{1,0:T(8,128)(2,1)S(1)} collective-permute-done((bf16[384,128]{1,0:T(8,128)(2,1)S(1)}, bf16[384,128]{1,0:T(8,128)(2,1)S(1)}, u32[]{:S(2)}, u32[]{:S(2)}) %collective-permute-start.4) | collective-permute-done | bytes 98336 | tf_op jit(solution)/shard_map/ppermute | solution.py:440
  62.7 1.6 %all-to-all-done.1 = bf16[4,192,128]{2,1,0:T(8,128)(2,1)S(1)} async-done(((bf16[4,192,128]{2,1,0:T(8,128)(2,1)}), bf16[4,192,128]{2,1,0:T(8,128)(2,1)S(1)}, u32[]{:S(2)}, u32[]{:S(2)}) %all-to-all-start.1) | async-done | bytes 196640 | tf_op jit(solution)/shard_map/all_to_all | solution.py:444
  64.4 0.7 copy.11
  65.1 0.8 broadcast_in_dim.17
  65.8 0.0 all-gather.3.cloned.1.call-update
  65.9 6.7 %all-to-all-start.2 = ((bf16[32,32,128]{2,1,0:T(8,128)(2,1)}), bf16[32,32,128]{2,1,0:T(8,128)(2,1)S(1)}, u32[]{:S(2)}, u32[]{:S(2)}) async-start(bf16[32,32,128]{2,1,0:T(8,128)(2,1)} %bitcast.10), calls=%async_computation.2 | async-start | bytes 524288 | tf_op jit(solution)/shard_map/all_to_all | solution.py:444
  72.6 0.0 copy-start
  72.6 0.0 collective-permute-done.p1
  72.6 0.0 collective-permute-done.1.p2
  72.6 0.0 collective-permute-done.2.p3
  72.6 1.1 arrive.1.info
  73.8 0.0 copy-start.3
  73.8 8.1 %all-to-all-done.2.q_ref = bf16[32,32,128]{2,1,0:T(8,128)(2,1)S(1)} async-done(((bf16[32,32,128]{2,1,0:T(8,128)(2,1)}), bf16[32,32,128]{2,1,0:T(8,128)(2,1)S(1)}, u32[]{:S(2)}, u32[]{:S(2)}) %all-to-all-start.2) | async-done | bytes 262176 | tf_op jit(solution)/shard_map/all_to_all | solution.py:444
  81.9 4.8 %branch_attend.1 = bf16[32,48,128]{2,1,0:T(8,128)(2,1)} custom-call(s32[3]{0:T(128)S(1)} %arrive.1.info, bf16[32,32,128]{2,1,0:T(8,128)(2,1)S(1)} %all-to-all-done.2.q_ref, bf16[512,2048]{1,0:T(8,128)(2,1)S(1)} %bitcast.23, bf16[512,2048]{1,0:T(8,128)(2,1)S(1)} %bitcast.24, bf16[4096,128]{1,0:T(8,128)(2,1)S(1)} %collective-permute-done.p1, ...), custom_call_target="tpu_custom_call" | custom-call | tf_op jit(solution)/shard_map/branch_attend/pallas_call | solution.py:254
  86.6 6.2 %all-to-all-start.3 = ((bf16[32,48,128]{2,1,0:T(8,128)(2,1)}), bf16[32,48,128]{2,1,0:T(8,128)(2,1)S(1)}, u32[]{:S(2)}, u32[]{:S(2)}) async-start(bf16[32,48,128]{2,1,0:T(8,128)(2,1)} %branch_attend.1), calls=%async_computation.3 | async-start | bytes 786432 | tf_op jit(solution)/shard_map/all_to_all | solution.py:444
  92.9 5.2 %collective-permute-start.5 = (bf16[384,128]{1,0:T(8,128)(2,1)S(1)}, bf16[384,128]{1,0:T(8,128)(2,1)S(1)}, u32[]{:S(2)}, u32[]{:S(2)}) collective-permute-start(bf16[384,128]{1,0:T(8,128)(2,1)S(1)} %pad_maximum_fusion.1.l0), channel_id=1, source_target_pairs={{0,3},{1,0},{2,1},{3,2},{4,7},{5,4},{6,5},{7,6},{8,11},{9,8},{10,9... | collective-permute-start | bytes 294920 | tf_op jit(solution)/shard_map/ppermute | solution.py:440
  98.1 4.9 %collective-permute-done.5.l3 = bf16[384,128]{1,0:T(8,128)(2,1)S(1)} collective-permute-done((bf16[384,128]{1,0:T(8,128)(2,1)S(1)}, bf16[384,128]{1,0:T(8,128)(2,1)S(1)}, u32[]{:S(2)}, u32[]{:S(2)}) %collective-permute-start.5) | collective-permute-done | bytes 98336 | tf_op jit(solution)/shard_map/ppermute | solution.py:440
  103.0 1.6 %copy-done.1 = bf16[32,16,2048]{2,1,0:T(8,128)(2,1)S(1)} copy-done((bf16[32,16,2048]{2,1,0:T(8,128)(2,1)S(1)}, bf16[32,16,2048]{2,1,0:T(8,128)(2,1)}, u32[]{:S(2)}) %copy-start.1) | copy-done | bytes 2097176
  104.6 0.9 copy-done.5
  105.5 0.9 copy-done.7
  106.4 4.6 %local_attend.1 = (bf16[144,128]{1,0:T(8,128)(2,1)S(1)}, bf16[144,128]{1,0:T(8,128)(2,1)S(1)}, bf16[144,128]{1,0:T(8,128)(2,1)S(1)}, bf16[144,128]{1,0:T(8,128)(2,1)S(1)}) custom-call(s32[3]{0:T(128)S(1)} %pad_add_fusion.info, s32[1,128]{1,0:T(1,128)S(1)} %copy-done.3, s32[1,512]{1,0:T(1,128)S(1)} %key_lengths.1.lengths_ref, bf16[512,2048]{1,0:T(8,128)(2,1)S(1)} %bitcast.26, ...), custom_call_target="tpu_custom_call" | custom-call | flops 12000000000 | bytes 8000000 | tf_op jit(solution)/shard_map/local_attend/pallas_call | solution.py:362
  111.0 0.0 all-to-all-done.3.in_ref
  111.0 1.4 merge_node.1
  112.4 8.0 %all-to-all-start.4 = ((bf16[4,80,128]{2,1,0:T(8,128)(2,1)}), bf16[4,80,128]{2,1,0:T(8,128)(2,1)S(1)}, u32[]{:S(2)}, u32[]{:S(2)}) async-start(bf16[4,80,128]{2,1,0:T(8,128)(2,1)} %merge_node.1), calls=%async_computation.4 | async-start | bytes 163840 | tf_op jit(solution)/shard_map/all_to_all | solution.py:444
  120.4 6.4 %collective-permute-start.6 = (bf16[144,128]{1,0:T(8,128)(2,1)S(1)}, bf16[144,128]{1,0:T(8,128)(2,1)S(1)}, u32[]{:S(2)}, u32[]{:S(2)}) collective-permute-start(bf16[144,128]{1,0:T(8,128)(2,1)S(1)} %get-tuple-element.42), channel_id=1, source_target_pairs={{0,1},{1,2},{2,3},{3,0},{4,5},{5,6},{6,7},{7,4},{8,9},{9,10},{10,1... | collective-permute-start | bytes 110600 | tf_op jit(solution)/shard_map/ppermute | solution.py:440
  126.8 1.9 %collective-permute-start.7 = (bf16[144,128]{1,0:T(8,128)(2,1)S(1)}, bf16[144,128]{1,0:T(8,128)(2,1)S(1)}, u32[]{:S(2)}, u32[]{:S(2)}) collective-permute-start(bf16[144,128]{1,0:T(8,128)(2,1)S(1)} %get-tuple-element.43), channel_id=1, source_target_pairs={{0,2},{1,3},{2,0},{3,1},{4,6},{5,7},{6,4},{7,5},{8,10},{9,11},{10,... | collective-permute-start | bytes 110600 | tf_op jit(solution)/shard_map/ppermute | solution.py:440
  128.7 4.3 %collective-permute-start.8 = (bf16[144,128]{1,0:T(8,128)(2,1)S(1)}, bf16[144,128]{1,0:T(8,128)(2,1)S(1)}, u32[]{:S(2)}, u32[]{:S(2)}) collective-permute-start(bf16[144,128]{1,0:T(8,128)(2,1)S(1)} %get-tuple-element.44), channel_id=1, source_target_pairs={{0,3},{1,0},{2,1},{3,2},{4,7},{5,4},{6,5},{7,6},{8,11},{9,8},{10,9... | collective-permute-start | bytes 110600 | tf_op jit(solution)/shard_map/ppermute | solution.py:440
  133.0 0.0 collective-permute-done.6.l1
  133.0 0.9 collective-permute-done.7.l2
  133.9 0.7 collective-permute-done.8.l3
  134.6 0.2 all-to-all-done.4.branch_ref
  134.8 1.0 finish.1
  (21 shorter events, 0.1 us)
Async XLA Ops:
  6.5 0.7 copy-start.2
  9.4 21.3 %all-to-all-start = ((bf16[4,160,128]{2,1,0:T(8,128)(2,1)}), bf16[4,160,128]{2,1,0:T(8,128)(2,1)S(1)}, u32[]{:S(2)}, u32[]{:S(2)}) async-start(bf16[4,160,128]{2,1,0:T(8,128)(2,1)} %get-tuple-element.30), calls=%async_computation | async-start | bytes 327680 | tf_op jit(solution)/shard_map/all_to_all | solution.py:444
  14.6 31.9 %copy-start.9 = (bf16[128,128]{1,0:T(8,128)(2,1)S(1)}, bf16[128,128]{1,0:T(8,128)(2,1)}, u32[]{:S(2)}) copy-start(bf16[128,128]{1,0:T(8,128)(2,1)} %q_hbm.1) | copy-start | bytes 98308
  14.6 38.3 %copy-start.8 = (s32[32]{0:T(128)S(1)}, s32[32]{0:T(128)}, u32[]{:S(2)}) copy-start(s32[32]{0:T(128)} %lengths.1) | copy-start | bytes 388
  18.8 53.9 %collective-permute-start = (bf16[4096,128]{1,0:T(8,128)(2,1)}, bf16[4096,128]{1,0:T(8,128)(2,1)S(1)}, u32[]{:S(2)}, u32[]{:S(2)}) collective-permute-start(bf16[4096,128]{1,0:T(8,128)(2,1)} %get-tuple-element.26), channel_id=1, source_target_pairs={{0,4},{4,8},{8,12},{12,0},{1,5},{5,9},{9,13},{13,1},{2,6},{6,10},{... | collective-permute-start | bytes 3145736 | tf_op jit(solution)/shard_map/ppermute | solution.py:440
  22.7 49.9 %collective-permute-start.1 = (bf16[4096,128]{1,0:T(8,128)(2,1)}, bf16[4096,128]{1,0:T(8,128)(2,1)}, u32[]{:S(2)}, u32[]{:S(2)}) collective-permute-start(bf16[4096,128]{1,0:T(8,128)(2,1)} %get-tuple-element.27), channel_id=1, source_target_pairs={{0,8},{4,12},{8,0},{12,4},{1,9},{5,13},{9,1},{13,5},{2,10},{6,14},... | collective-permute-start | bytes 3145736 | tf_op jit(solution)/shard_map/ppermute | solution.py:440
  27.3 45.3 %collective-permute-start.2 = (bf16[4096,128]{1,0:T(8,128)(2,1)}, bf16[4096,128]{1,0:T(8,128)(2,1)}, u32[]{:S(2)}, u32[]{:S(2)}) collective-permute-start(bf16[4096,128]{1,0:T(8,128)(2,1)} %get-tuple-element.28), channel_id=1, source_target_pairs={{0,12},{4,0},{8,4},{12,8},{1,13},{5,1},{9,5},{13,9},{2,14},{6,2},{... | collective-permute-start | bytes 3145736 | tf_op jit(solution)/shard_map/ppermute | solution.py:440
  31.4 32.9 %all-to-all-start.1 = ((bf16[4,192,128]{2,1,0:T(8,128)(2,1)}), bf16[4,192,128]{2,1,0:T(8,128)(2,1)S(1)}, u32[]{:S(2)}, u32[]{:S(2)}) async-start(bf16[4,192,128]{2,1,0:T(8,128)(2,1)} %pad_maximum_fusion), calls=%async_computation.1 | async-start | bytes 393216 | tf_op jit(solution)/shard_map/all_to_all | solution.py:444
  46.5 56.5 %all-gather.3.cloned.1.call-start = ((), (), s32[]{:S(2)}) async-start(), calls=%async_computation.5 | async-start | bytes 1179648 | tf_op jit(solution)/shard_map/all_gather | solution.py:479
  46.5 13.2 %collective-permute-start.3 = (bf16[384,128]{1,0:T(8,128)(2,1)S(1)}, bf16[384,128]{1,0:T(8,128)(2,1)S(1)}, u32[]{:S(2)}, u32[]{:S(2)}) collective-permute-start(bf16[384,128]{1,0:T(8,128)(2,1)S(1)} %pad_maximum_fusion.1.l0), channel_id=1, source_target_pairs={{0,1},{1,2},{2,3},{3,0},{4,5},{5,6},{6,7},{7,4},{8,9},{9,10},{10,1... | collective-permute-start | bytes 294920 | tf_op jit(solution)/shard_map/ppermute | solution.py:440
  49.5 13.3 %collective-permute-start.4 = (bf16[384,128]{1,0:T(8,128)(2,1)S(1)}, bf16[384,128]{1,0:T(8,128)(2,1)S(1)}, u32[]{:S(2)}, u32[]{:S(2)}) collective-permute-start(bf16[384,128]{1,0:T(8,128)(2,1)S(1)} %pad_maximum_fusion.1.l0), channel_id=1, source_target_pairs={{0,2},{1,3},{2,0},{3,1},{4,6},{5,7},{6,4},{7,5},{8,10},{9,11},{10,... | collective-permute-start | bytes 294920 | tf_op jit(solution)/shard_map/ppermute | solution.py:440
  59.8 6.1 %copy-start.4 = (bf16[384,128]{1,0:T(8,128)(2,1)}, bf16[384,128]{1,0:T(8,128)(2,1)S(1)}, u32[]{:S(2)}) copy-start(bf16[384,128]{1,0:T(8,128)(2,1)S(1)} %collective-permute-done.3.l1) | copy-start | bytes 294916
  62.7 3.1 %copy-start.6 = (bf16[384,128]{1,0:T(8,128)(2,1)}, bf16[384,128]{1,0:T(8,128)(2,1)S(1)}, u32[]{:S(2)}) copy-start(bf16[384,128]{1,0:T(8,128)(2,1)S(1)} %collective-permute-done.4.l2) | copy-start | bytes 294916
  65.9 16.0 %all-to-all-start.2 = ((bf16[32,32,128]{2,1,0:T(8,128)(2,1)}), bf16[32,32,128]{2,1,0:T(8,128)(2,1)S(1)}, u32[]{:S(2)}, u32[]{:S(2)}) async-start(bf16[32,32,128]{2,1,0:T(8,128)(2,1)} %bitcast.10), calls=%async_computation.2 | async-start | bytes 524288 | tf_op jit(solution)/shard_map/all_to_all | solution.py:444
  72.6 9.3 %copy-start = (bf16[1,512,2048]{2,1,0:T(8,128)(2,1)S(1)}, bf16[1,512,2048]{2,1,0:T(8,128)(2,1)}, u32[]{:S(2)}) copy-start(bf16[1,512,2048]{2,1,0:T(8,128)(2,1)} %param.14) | copy-start | bytes 6291460
  73.8 29.2 %copy-start.3 = (s32[1,128]{1,0:T(1,128)S(1)}, s32[1,128]{1,0:T(1,128)}, u32[]{:S(2)}) copy-start(s32[1,128]{1,0:T(1,128)} %leaf_ref.1) | copy-start | bytes 1540
  86.6 24.3 %all-to-all-start.3 = ((bf16[32,48,128]{2,1,0:T(8,128)(2,1)}), bf16[32,48,128]{2,1,0:T(8,128)(2,1)S(1)}, u32[]{:S(2)}, u32[]{:S(2)}) async-start(bf16[32,48,128]{2,1,0:T(8,128)(2,1)} %branch_attend.1), calls=%async_computation.3 | async-start | bytes 786432 | tf_op jit(solution)/shard_map/all_to_all | solution.py:444
  92.9 10.1 %collective-permute-start.5 = (bf16[384,128]{1,0:T(8,128)(2,1)S(1)}, bf16[384,128]{1,0:T(8,128)(2,1)S(1)}, u32[]{:S(2)}, u32[]{:S(2)}) collective-permute-start(bf16[384,128]{1,0:T(8,128)(2,1)S(1)} %pad_maximum_fusion.1.l0), channel_id=1, source_target_pairs={{0,3},{1,0},{2,1},{3,2},{4,7},{5,4},{6,5},{7,6},{8,11},{9,8},{10,9... | collective-permute-start | bytes 294920 | tf_op jit(solution)/shard_map/ppermute | solution.py:440
  103.0 1.6 %copy-start.1 = (bf16[32,16,2048]{2,1,0:T(8,128)(2,1)S(1)}, bf16[32,16,2048]{2,1,0:T(8,128)(2,1)}, u32[]{:S(2)}) copy-start(bf16[32,16,2048]{2,1,0:T(8,128)(2,1)} %param.16) | copy-start | bytes 6291460
  104.6 0.9 copy-start.5
  105.5 0.9 copy-start.7
  112.4 22.4 %all-to-all-start.4 = ((bf16[4,80,128]{2,1,0:T(8,128)(2,1)}), bf16[4,80,128]{2,1,0:T(8,128)(2,1)S(1)}, u32[]{:S(2)}, u32[]{:S(2)}) async-start(bf16[4,80,128]{2,1,0:T(8,128)(2,1)} %merge_node.1), calls=%async_computation.4 | async-start | bytes 163840 | tf_op jit(solution)/shard_map/all_to_all | solution.py:444
  120.4 12.6 %collective-permute-start.6 = (bf16[144,128]{1,0:T(8,128)(2,1)S(1)}, bf16[144,128]{1,0:T(8,128)(2,1)S(1)}, u32[]{:S(2)}, u32[]{:S(2)}) collective-permute-start(bf16[144,128]{1,0:T(8,128)(2,1)S(1)} %get-tuple-element.42), channel_id=1, source_target_pairs={{0,1},{1,2},{2,3},{3,0},{4,5},{5,6},{6,7},{7,4},{8,9},{9,10},{10,1... | collective-permute-start | bytes 110600 | tf_op jit(solution)/shard_map/ppermute | solution.py:440
  126.8 7.1 %collective-permute-start.7 = (bf16[144,128]{1,0:T(8,128)(2,1)S(1)}, bf16[144,128]{1,0:T(8,128)(2,1)S(1)}, u32[]{:S(2)}, u32[]{:S(2)}) collective-permute-start(bf16[144,128]{1,0:T(8,128)(2,1)S(1)} %get-tuple-element.43), channel_id=1, source_target_pairs={{0,2},{1,3},{2,0},{3,1},{4,6},{5,7},{6,4},{7,5},{8,10},{9,11},{10,... | collective-permute-start | bytes 110600 | tf_op jit(solution)/shard_map/ppermute | solution.py:440
  128.7 5.9 %collective-permute-start.8 = (bf16[144,128]{1,0:T(8,128)(2,1)S(1)}, bf16[144,128]{1,0:T(8,128)(2,1)S(1)}, u32[]{:S(2)}, u32[]{:S(2)}) collective-permute-start(bf16[144,128]{1,0:T(8,128)(2,1)S(1)} %get-tuple-element.44), channel_id=1, source_target_pairs={{0,3},{1,0},{2,1},{3,2},{4,7},{5,4},{6,5},{7,6},{8,11},{9,8},{10,9... | collective-permute-start | bytes 110600 | tf_op jit(solution)/shard_map/ppermute | solution.py:440
Sparse Core Ops, SparseCore 0:
  66.0 24.9 all-gather.2
